TPU v7x, 32 devices: a whole 2x2x4 slice. The times are simulated.
32 devices in a mesh: stream: 16 (over z, y, x), span: 2 (over core).
Axes of the slice: x: 2, y: 2, z: 4, core: 2. Of those that a mesh axis runs over, the one named last changes fastest.
Arguments:
- adjoint_start: float32 [5, 128, 32, 512], P(None, 'stream', 'span'), may hold values from -4 to 4
- source: float32 [5, 128, 32, 512], P(None, 'stream', 'span'), may hold values from -40 to 40
- flow_state: float32 [5, 128, 32, 512], P(None, 'stream', 'span'), may hold values from -4 to 4, as said below
- precond: float32 [5, 5, 128, 32, 512], P(None, None, 'stream', 'span'), may hold values from -0.12 to 0.2
- flux_jac: float32 [3, 5, 5], replicated, may hold values from -4 to 4
- bc_codes: int32 [128, 32], P('stream', 'span'), may hold values from 0 to 2
Outputs:
- adjoint: float32 [5, 128, 32, 512], P(None, 'stream', 'span')
- residual_rms: float32 [2], replicated
Inputs may be any that keep to these rules, and one draw needn't show every extreme that they name: `bc_codes`: 0 is a wall, 1 a far field, 2 an extrapolation face. `flow_state`: density and pressure lie in 0.5 to 2.
All inputs are finite; a program needn't handle non-finite values.
Results may differ from a plain program's by a relative error of at most 0.0003.
Values sent between devices are 32-bit elements; how exact they have to be, the bound alone decides.
No kernel may reach another device: no remote copies, remote signals or barrier semaphores. Data moves between devices by JAX's collectives and lax.ppermute only.
A program may use at most 128 MiB of HBM per device.

v0:
```python
import functools

import jax
import jax.numpy as jnp
from jax import lax
from jax.experimental import pallas as pl
from jax.experimental.pallas import tpu as pltpu
from jax.sharding import PartitionSpec as P

NV = 5
SUB, LANE = 8, 128
F32 = jnp.float32
VMEM = pl.BlockSpec(memory_space=pltpu.VMEM)
SMEM = pl.BlockSpec(memory_space=pltpu.SMEM)


def shape(*dims):
    return jax.ShapeDtypeStruct(dims, F32)


def cost(flops, transcendentals, bytes_accessed):
    return pl.CostEstimate(
        flops=int(flops), transcendentals=int(transcendentals), bytes_accessed=int(bytes_accessed)
    )


def quarter_speed(rho, m1, m2, m3, p):
    momentum = jnp.sqrt(m1 * m1 + m2 * m2 + m3 * m3)
    return 0.25 * (momentum / rho + jnp.sqrt(1.4 * p / rho))


def odd(axis):
    return lax.rem(lax.axis_index(axis), 2) == 1


def stream_faces(v, fa, fb):
    planes = v.shape[1]
    is_odd = odd("stream")
    plane_a = jnp.where(is_odd, 0, planes - 1)
    plane_b = jnp.where(is_odd, planes - 1, 0)
    for c in range(NV):
        fa[c] = v[c, plane_a]
        fb[c] = v[c, plane_b]
    return plane_a, plane_b


def span_rows(v, c, first, last, out_refs):
    is_odd = odd("span")
    planes = v.shape[1]
    for i in range(planes):
        head = v[c, i, first : first + 1, :]
        tail = v[c, i, last : last + 1, :]
        out_refs[0][c, i] = jnp.where(is_odd, head, tail)
        if len(out_refs) > 1:
            out_refs[1][c, i] = jnp.where(is_odd, tail, head)


def pack_kernel(n_span, v, flow, fa, fb, *rest):
    spans, rows = rest[:n_span], rest[n_span:]
    plane_a, plane_b = stream_faces(v, fa, fb)
    for ref, plane in ((fa, plane_a), (fb, plane_b)):
        ref[NV] = quarter_speed(*[flow[c, plane] for c in range(NV)])
    last = v.shape[2] - 1
    for c in range(NV):
        span_rows(v, c, 0, last, spans)
        span_rows(flow, c, 0, last, rows)
    for ref, row in zip(spans, rows):
        ref[NV] = quarter_speed(*[row[c] for c in range(NV)])


def sweep_plane(i, v, prev, nxt, g, gprev, gnxt, tops, bottoms, src, pre, jac, wall, out, ssq):
    rows_n, lanes_n = v.shape[2] // SUB, v.shape[3] // LANE
    lane = lax.broadcasted_iota(jnp.int32, (SUB, LANE), 1)
    row = lax.broadcasted_iota(jnp.int32, (SUB, LANE), 0)
    first_lane, last_lane = lane == 0, lane == LANE - 1
    first_row, last_row = row == 0, row == SUB - 1
    zero = jnp.zeros((SUB, LANE), F32)

    def at(jb, kb):
        return pl.ds(jb * SUB, SUB), pl.ds(kb * LANE, LANE)

    def neighbours(get, get_top, get_bottom, jb, kb):
        own = get(jb, kb)
        up = pltpu.roll(own, 1, 0)
        before_row = get_top(kb) if jb == 0 else pltpu.roll(get(jb - 1, kb), 1, 0)
        up = jnp.where(first_row, before_row, up)
        down = pltpu.roll(own, SUB - 1, 0)
        after_row = get_bottom(kb) if jb == rows_n - 1 else pltpu.roll(get(jb + 1, kb), SUB - 1, 0)
        down = jnp.where(last_row, after_row, down)
        left = pltpu.roll(own, 1, 1)
        left = jnp.where(first_lane, zero if kb == 0 else pltpu.roll(get(jb, kb - 1), 1, 1), left)
        right = pltpu.roll(own, LANE - 1, 1)
        right = jnp.where(
            last_lane, zero if kb == lanes_n - 1 else pltpu.roll(get(jb, kb + 1), LANE - 1, 1), right
        )
        return own, up, down, left, right

    total = ssq
    for jb in range(rows_n):
        for kb in range(lanes_n):
            sl = at(jb, kb)
            gs, gu, gd, gl, gr = neighbours(
                lambda a, b: g[(i, *at(a, b))],
                lambda b: tops(NV, b),
                lambda b: bottoms(NV, b),
                jb,
                kb,
            )
            coefs = [gs + gprev(*sl), gs + gnxt(*sl), gs + gu, gs + gd, gs + gl, gs + gr]
            diag = ((coefs[0] + coefs[1]) + (coefs[2] + coefs[3])) + (coefs[4] + coefs[5])
            diffs, owns, res = [], [], []
            for c in range(NV):
                own, up, down, left, right = neighbours(
                    lambda a, b, c=c: v[(c, i, *at(a, b))],
                    functools.partial(tops, c),
                    functools.partial(bottoms, c),
                    jb,
                    kb,
                )
                before, after = prev(c, *sl), nxt(c, *sl)
                diffs.append((before - after, up - down, left - right))
                owns.append(own)
                pulls = (
                    (coefs[0] * before + coefs[1] * after)
                    + (coefs[2] * up + coefs[3] * down)
                ) + (coefs[4] * left + coefs[5] * right)
                res.append(src[(c, i, *sl)] - (diag * own - pulls))
            for c in range(NV):
                r = res[c]
                for d in range(3):
                    for u in range(NV):
                        r = r - jac[d, u, c] * diffs[u][d]
                res[c] = r
            if kb == 0:
                code = wall(jb)
                on_wall = first_lane & (code != 1)
                for c in range(NV):
                    t = gs * owns[c]
                    for u in range(NV):
                        t = t + jac[2, u, c] * owns[u]
                    if c == 3:
                        t = jnp.where(code == 0, -t, t)
                    res[c] = res[c] + jnp.where(on_wall, t, zero)
            for c in range(NV):
                total = total + res[c] * res[c]
            for c in range(NV):
                a = owns[c]
                for u in range(NV):
                    a = a + pre[(u, c, i, *sl)] * res[u]
                out[(c, i, *sl)] = a
    return total


def spread_codes(bc, codes):
    planes, columns = bc.shape
    eye = lax.broadcasted_iota(jnp.int32, (columns, columns), 0) == lax.broadcasted_iota(
        jnp.int32, (columns, columns), 1
    )
    for i in range(planes):
        own = jnp.broadcast_to(bc[i : i + 1, :].astype(F32), (columns, columns))
        column = jnp.sum(jnp.where(eye, own, 0.0), axis=1, keepdims=True)
        codes[i] = jnp.broadcast_to(column, (columns, LANE))


def sweep_kernel(first, n_span, *refs):
    refs = list(refs)
    v = refs.pop(0)
    src = refs.pop(0)
    pre = refs.pop(0)
    jac_in = refs.pop(0)
    bc = refs.pop(0)
    speed_in = refs.pop(0)
    ha, hb = refs.pop(0), refs.pop(0)
    spans = [refs.pop(0) for _ in range(n_span)]
    if not first:
        gha, ghb = refs.pop(0), refs.pop(0)
        gspans = [refs.pop(0) for _ in range(n_span)]
    else:
        gha, ghb, gspans = ha, hb, spans
    out, ssq_out = refs.pop(0), refs.pop(0)
    if first:
        g = refs.pop(0)
        fa, fb = refs.pop(0), refs.pop(0)
        span_out = [refs.pop(0) for _ in range(n_span)]
    else:
        g = speed_in
    halves, codes = refs
    planes = v.shape[1]
    spread_codes(bc, codes)

    for d in range(3):
        for u in range(NV):
            for c in range(NV):
                halves[d, u, c] = 0.5 * jac_in[d, u, c]
    if first:

        def speed_plane(i, carry):
            g[i] = quarter_speed(*[speed_in[c, i] for c in range(NV)])
            return carry

        lax.fori_loop(0, planes, speed_plane, 0)

    stream_odd, span_odd = odd("stream"), odd("span")

    def pick(is_odd, pair, even_ref, idx):
        other = 1 - even_ref
        if len(pair) == 1:
            keep = is_odd if even_ref == 1 else jnp.logical_not(is_odd)
            return jnp.where(keep, pair[0][idx], 0.0)
        return jnp.where(is_odd, pair[other][idx], pair[even_ref][idx])

    def low_halo(c, *sl):
        pair = (gha, ghb) if c == NV else (ha, hb)
        return pick(stream_odd, pair, 1, (c, *sl))

    def high_halo(c, *sl):
        pair = (gha, ghb) if c == NV else (ha, hb)
        return pick(stream_odd, pair, 0, (c, *sl))

    def rows_of(even_ref, i):
        def get(c, kb):
            pair = gspans if c == NV else spans
            one = pick(span_odd, pair, even_ref, (c, i, slice(None), pl.ds(kb * LANE, LANE)))
            return jnp.broadcast_to(one, (SUB, LANE))

        return get

    def plane(i, prev, nxt, gprev, gnxt, ssq):
        return sweep_plane(
            i, v, prev, nxt, g, gprev, gnxt, rows_of(1, i), rows_of(0, i), src, pre, halves,
            lambda jb: codes[i, pl.ds(jb * SUB, SUB), :],
            out, ssq,
        )

    def inner(i, ssq):
        return plane(
            i,
            lambda c, *sl: v[(c, i - 1, *sl)],
            lambda c, *sl: v[(c, i + 1, *sl)],
            lambda *sl: g[(i - 1, *sl)],
            lambda *sl: g[(i + 1, *sl)],
            ssq,
        )

    ssq = jnp.zeros((SUB, LANE), F32)
    ssq = lax.fori_loop(1, planes - 1, inner, ssq)
    ssq = plane(
        0, low_halo, lambda c, *sl: v[(c, 1, *sl)],
        lambda *sl: low_halo(NV, *sl), lambda *sl: g[(1, *sl)], ssq,
    )
    ssq = plane(
        planes - 1, lambda c, *sl: v[(c, planes - 2, *sl)], high_halo,
        lambda *sl: g[(planes - 2, *sl)], lambda *sl: high_halo(NV, *sl), ssq,
    )
    ssq_out[...] = ssq
    if first:
        stream_faces(out, fa, fb)
        for c in range(NV):
            span_rows(out, c, 0, v.shape[2] - 1, span_out)


def pairs(count, offset):
    both = []
    for i in range(offset, count - 1, 2):
        both += [(i, i + 1), (i + 1, i)]
    return both


def exchange(faces, axis):
    count = lax.axis_size(axis)
    return [lax.ppermute(face, axis, pairs(count, k)) for k, face in enumerate(faces)]


def all_sum(value):
    for axis in ("span", "stream"):
        count = lax.axis_size(axis)
        if count & (count - 1):
            value = lax.psum(value, axis)
            continue
        step = 1
        while step < count:
            value = value + lax.ppermute(value, axis, [(i, i ^ step) for i in range(count)])
            step *= 2
    return value


def finish_kernel(a, b, out):
    lane = lax.broadcasted_iota(jnp.int32, (SUB, LANE), 1)
    out[...] = jnp.where(lane == 0, jnp.sum(a[...]), jnp.where(lane == 1, jnp.sum(b[...]), 0.0))


def per_device(adjoint_start, source, flow_state, precond, flux_jac, bc_codes):
    _, planes, rows, lanes = adjoint_start.shape
    n_stream, n_span_all = lax.axis_size("stream"), lax.axis_size("span")
    n_span = 1 if n_span_all <= 2 else 2
    cells = planes * rows * lanes
    cells_all = float(NV * cells * n_stream * n_span_all)
    scratch = [pltpu.SMEM((3, NV, NV), F32), pltpu.VMEM((planes, rows, LANE), F32)]

    faces = pl.pallas_call(
        functools.partial(pack_kernel, n_span),
        out_shape=[shape(NV + 1, rows, lanes)] * 2 + [shape(NV + 1, planes, 1, lanes)] * n_span,
        in_specs=[VMEM] * 2,
        out_specs=[VMEM] * (2 + n_span),
        scratch_shapes=[pltpu.VMEM((NV, planes, 1, lanes), F32)] * n_span,
        cost_estimate=cost(cells, 0, 8 * cells),
        name="pack",
    )(adjoint_start, flow_state)
    stream0 = exchange(faces[:2], "stream")
    span0 = exchange(faces[2:], "span")

    outs = pl.pallas_call(
        functools.partial(sweep_kernel, True, n_span),
        out_shape=[shape(NV, planes, rows, lanes), shape(SUB, LANE), shape(planes, rows, lanes)]
        + [shape(NV, rows, lanes)] * 2
        + [shape(NV, planes, 1, lanes)] * n_span,
        in_specs=[VMEM] * 3 + [SMEM] + [VMEM] * (4 + n_span),
        out_specs=[VMEM] * (5 + n_span),
        scratch_shapes=scratch,
        cost_estimate=cost(350 * cells, 4 * cells, 42 * 4 * cells),
        name="sweep_first",
    )(adjoint_start, source, precond, flux_jac, bc_codes, flow_state, *stream0, *span0)
    adjoint, ssq0, quarter = outs[:3]
    stream1 = exchange(outs[3:5], "stream")
    span1 = exchange(outs[5:], "span")

    adjoint, ssq1 = pl.pallas_call(
        functools.partial(sweep_kernel, False, n_span),
        out_shape=[shape(NV, planes, rows, lanes), shape(SUB, LANE)],
        in_specs=[VMEM] * 3 + [SMEM] + [VMEM] * (6 + 2 * n_span),
        out_specs=[VMEM] * 2,
        scratch_shapes=scratch,
        cost_estimate=cost(350 * cells, 0, 42 * 4 * cells),
        name="sweep_second",
    )(adjoint, source, precond, flux_jac, bc_codes, quarter, *stream1, *span1, *stream0, *span0)

    sums = pl.pallas_call(
        finish_kernel, out_shape=shape(SUB, LANE), in_specs=[VMEM] * 2, out_specs=VMEM, name="sums"
    )(ssq0, ssq1)
    residual_rms = jnp.sqrt(all_sum(sums)[0, :2] / cells_all)
    return (adjoint, residual_rms)


def solution(mesh):
    in_specs = (
        P(None, "stream", "span", None),
        P(None, "stream", "span", None),
        P(None, "stream", "span", None),
        P(None, None, "stream", "span", None),
        P(),
        P("stream", "span"),
    )
    out_specs = (P(None, "stream", "span", None), P())
    return jax.shard_map(
        per_device, mesh=mesh, in_specs=in_specs, out_specs=out_specs, check_vma=False
    )
```

profile of v0, /device:TPU:0, one launch (start us, length us, event | category | flops | bytes accessed | tf_op | source)
XLA Modules:
  0.0 66.7 jit_solution(9901794565783089399)
XLA Ops:
  0.6 2.5 %pack.1 = (f32[6,16,512]{2,1,0:T(8,128)}, f32[6,16,512]{2,1,0:T(8,128)}, f32[6,8,1,512]{3,2,1,0:T(1,128)}) custom-call(f32[5,8,16,512]{3,2,1,0:T(8,128)} %refs_0_.1, f32[5,8,16,512]{3,2,1,0:T(8,128)} %refs_5_.1), custom_call_target="tpu_custom_call" | custom-call | flops 65536 | bytes 524288 | tf_op jit(solution)/shard_map/pack/pallas_call | solution.py:300
  3.2 3.0 %collective-permute-start = (f32[6,16,512]{2,1,0:T(8,128)}, f32[6,16,512]{2,1,0:T(8,128)S(1)}, u32[]{:S(2)}, u32[]{:S(2)}) collective-permute-start(f32[6,16,512]{2,1,0:T(8,128)} %get-tuple-element.13), channel_id=1, source_target_pairs={{0,2},{2,0},{4,6},{6,4},{8,10},{10,8},{12,14},{14,12},{16,18},{18,... | collective-permute-start | bytes 589832 | tf_op jit(solution)/shard_map/ppermute | solution.py:271
  6.1 0.7 collective-permute-start.1
  7.5 0.9 %collective-permute-done.2.refs_8_.refs_11_ = f32[6,8,1,512]{3,2,1,0:T(1,128)S(1)} collective-permute-done((f32[6,8,1,512]{3,2,1,0:T(1,128)}, f32[6,8,1,512]{3,2,1,0:T(1,128)S(1)}, u32[]{:S(2)}, u32[]{:S(2)}) %collective-permute-start.2) | collective-permute-done | bytes 98336 | tf_op jit(solution)/shard_map/ppermute | solution.py:271
  8.4 2.9 %collective-permute-done.refs_6_.refs_9_ = f32[6,16,512]{2,1,0:T(8,128)S(1)} collective-permute-done((f32[6,16,512]{2,1,0:T(8,128)}, f32[6,16,512]{2,1,0:T(8,128)S(1)}, u32[]{:S(2)}, u32[]{:S(2)}) %collective-permute-start) | collective-permute-done | bytes 196640 | tf_op jit(solution)/shard_map/ppermute | solution.py:271
  11.3 0.7 copy-done
  11.9 0.7 %copy-done.1 = f32[6,16,512]{2,1,0:T(8,128)} copy-done((f32[6,16,512]{2,1,0:T(8,128)}, f32[6,16,512]{2,1,0:T(8,128)S(1)}, u32[]{:S(2)}) %copy-start.1) | copy-done | bytes 196632
  12.6 9.8 %sweep_first.1 = (f32[5,8,16,512]{3,2,1,0:T(8,128)}, f32[8,128]{1,0:T(8,128)}, f32[8,16,512]{2,1,0:T(8,128)}, f32[5,16,512]{2,1,0:T(8,128)}, f32[5,16,512]{2,1,0:T(8,128)}, /*index=5*/f32[5,8,1,512]{3,2,1,0:T(1,128)}) custom-call(f32[5,8,16,512]{3,2,1,0:T(8,128)} %refs_0_.1, f32[5,8,16,512]{3,2,1,0:T(8,128)} %refs_1_.3, f32[5,5,8,16,512]{4,3,2,1,0:T(8,128)} %refs_2_.3, ...), custom_call_target="tpu_custom_call" | custom-call | flops 22937600 | bytes 11010048 | tf_op jit(solution)/shard_map/sweep_first/pallas_call | solution.py:312
  22.4 6.2 %collective-permute-start.3 = (f32[5,16,512]{2,1,0:T(8,128)}, f32[5,16,512]{2,1,0:T(8,128)S(1)}, u32[]{:S(2)}, u32[]{:S(2)}) collective-permute-start(f32[5,16,512]{2,1,0:T(8,128)} %get-tuple-element.18), channel_id=1, source_target_pairs={{0,2},{2,0},{4,6},{6,4},{8,10},{10,8},{12,14},{14,12},{16,18},{18,... | collective-permute-start | bytes 491528 | tf_op jit(solution)/shard_map/ppermute | solution.py:271
  28.7 0.7 collective-permute-start.4
  29.4 1.5 %collective-permute-done.5.refs_8_ = f32[5,8,1,512]{3,2,1,0:T(1,128)S(1)} collective-permute-done((f32[5,8,1,512]{3,2,1,0:T(1,128)}, f32[5,8,1,512]{3,2,1,0:T(1,128)S(1)}, u32[]{:S(2)}, u32[]{:S(2)}) %collective-permute-start.5) | collective-permute-done | bytes 81952 | tf_op jit(solution)/shard_map/ppermute | solution.py:271
  30.9 4.5 %collective-permute-done.3.refs_6_ = f32[5,16,512]{2,1,0:T(8,128)S(1)} collective-permute-done((f32[5,16,512]{2,1,0:T(8,128)}, f32[5,16,512]{2,1,0:T(8,128)S(1)}, u32[]{:S(2)}, u32[]{:S(2)}) %collective-permute-start.3) | collective-permute-done | bytes 163872 | tf_op jit(solution)/shard_map/ppermute | solution.py:271
  36.1 9.2 %sweep_second.1 = (f32[5,8,16,512]{3,2,1,0:T(8,128)}, f32[8,128]{1,0:T(8,128)}) custom-call(f32[5,8,16,512]{3,2,1,0:T(8,128)} %get-tuple-element.16.refs_0_, f32[5,8,16,512]{3,2,1,0:T(8,128)} %refs_1_.3, f32[5,5,8,16,512]{4,3,2,1,0:T(8,128)} %refs_2_.3, f32[3,5,5]{2,1,0:T(8,128)} %copy.8.refs_3_, s32[8,16]{1,0:T(8,128)} %refs_4_.3, ...), custom_call_target="tpu_custom_call" | custom-call | flops 22937600 | bytes 11010048 | tf_op jit(solution)/shard_map/sweep_second/pallas_call | solution.py:327
  45.3 1.4 %sums.1 = f32[8,128]{1,0:T(8,128)} custom-call(f32[8,128]{1,0:T(8,128)} %get-tuple-element.22.a, f32[8,128]{1,0:T(8,128)} %get-tuple-element.23.b), custom_call_target="tpu_custom_call" | custom-call | tf_op jit(solution)/shard_map/sums/pallas_call | solution.py:337
  46.7 1.4 %collective-permute-done.6 = f32[8,128]{1,0:T(8,128)S(1)} collective-permute-done((f32[8,128]{1,0:T(8,128)}, f32[8,128]{1,0:T(8,128)S(1)}, u32[]{:S(2)}, u32[]{:S(2)}) %collective-permute-start.6) | collective-permute-done | bytes 4128 | tf_op jit(solution)/shard_map/ppermute | solution.py:282
  48.1 0.7 %add.15 = f32[8,128]{1,0:T(8,128)S(1)} add(f32[8,128]{1,0:T(8,128)} %sums.1, f32[8,128]{1,0:T(8,128)S(1)} %collective-permute-done.6) | non-fusion elementwise | flops 1024 | bytes 12288 | tf_op jit(solution)/shard_map/add | solution.py:282
  48.8 2.3 %collective-permute-start.7 = (f32[8,128]{1,0:T(8,128)S(1)}, f32[8,128]{1,0:T(8,128)S(1)}, u32[]{:S(2)}, u32[]{:S(2)}) collective-permute-start(f32[8,128]{1,0:T(8,128)S(1)} %add.15), channel_id=1, source_target_pairs={{0,2},{2,0},{4,6},{6,4},{8,10},{10,8},{12,14},{14,12},{16,18},{18,... | collective-permute-start | bytes 12296 | tf_op jit(solution)/shard_map/ppermute | solution.py:282
  51.1 1.6 %collective-permute-done.7 = f32[8,128]{1,0:T(8,128)S(1)} collective-permute-done((f32[8,128]{1,0:T(8,128)S(1)}, f32[8,128]{1,0:T(8,128)S(1)}, u32[]{:S(2)}, u32[]{:S(2)}) %collective-permute-start.7) | collective-permute-done | bytes 4128 | tf_op jit(solution)/shard_map/ppermute | solution.py:282
  52.7 1.6 %collective-permute-start.8 = (f32[8,128]{1,0:T(8,128)S(1)}, f32[8,128]{1,0:T(8,128)S(1)}, u32[]{:S(2)}, u32[]{:S(2)}) collective-permute-start(f32[8,128]{1,0:T(8,128)S(1)} %add.16), channel_id=1, source_target_pairs={{0,4},{2,6},{4,0},{6,2},{8,12},{10,14},{12,8},{14,10},{16,20},{18,... | collective-permute-start | bytes 12296 | tf_op jit(solution)/shard_map/ppermute | solution.py:282
  54.3 2.0 %collective-permute-done.8 = f32[8,128]{1,0:T(8,128)S(1)} collective-permute-done((f32[8,128]{1,0:T(8,128)S(1)}, f32[8,128]{1,0:T(8,128)S(1)}, u32[]{:S(2)}, u32[]{:S(2)}) %collective-permute-start.8) | collective-permute-done | bytes 4128 | tf_op jit(solution)/shard_map/ppermute | solution.py:282
  56.3 3.7 %collective-permute-start.9 = (f32[8,128]{1,0:T(8,128)S(1)}, f32[8,128]{1,0:T(8,128)S(1)}, u32[]{:S(2)}, u32[]{:S(2)}) collective-permute-start(f32[8,128]{1,0:T(8,128)S(1)} %add.17), channel_id=1, source_target_pairs={{0,8},{2,10},{4,12},{6,14},{8,0},{10,2},{12,4},{14,6},{16,24},{18,... | collective-permute-start | bytes 12296 | tf_op jit(solution)/shard_map/ppermute | solution.py:282
  60.0 1.6 %collective-permute-done.9 = f32[8,128]{1,0:T(8,128)S(1)} collective-permute-done((f32[8,128]{1,0:T(8,128)S(1)}, f32[8,128]{1,0:T(8,128)S(1)}, u32[]{:S(2)}, u32[]{:S(2)}) %collective-permute-start.9) | collective-permute-done | bytes 4128 | tf_op jit(solution)/shard_map/ppermute | solution.py:282
  61.6 3.0 %collective-permute-start.10 = (f32[8,128]{1,0:T(8,128)S(1)}, f32[8,128]{1,0:T(8,128)S(1)}, u32[]{:S(2)}, u32[]{:S(2)}) collective-permute-start(f32[8,128]{1,0:T(8,128)S(1)} %add.18), channel_id=1, source_target_pairs={{0,16},{2,18},{4,20},{6,22},{8,24},{10,26},{12,28},{14,30},{16,0},... | collective-permute-start | bytes 12296 | tf_op jit(solution)/shard_map/ppermute | solution.py:282
  64.6 1.6 %collective-permute-done.10 = f32[8,128]{1,0:T(8,128)S(1)} collective-permute-done((f32[8,128]{1,0:T(8,128)S(1)}, f32[8,128]{1,0:T(8,128)S(1)}, u32[]{:S(2)}, u32[]{:S(2)}) %collective-permute-start.10) | collective-permute-done | bytes 4128 | tf_op jit(solution)/shard_map/ppermute | solution.py:282
  (23 shorter events, 2.0 us)
Async XLA Ops:
  0.6 6.3 %copy-start.6 = (f32[3,5,5]{2,0,1:T(4,128)S(1)}, f32[3,5,5]{2,0,1:T(4,128)}, u32[]{:S(2)}) copy-start(f32[3,5,5]{2,0,1:T(4,128)} %param.10) | copy-start | bytes 904
  3.2 8.1 %collective-permute-start = (f32[6,16,512]{2,1,0:T(8,128)}, f32[6,16,512]{2,1,0:T(8,128)S(1)}, u32[]{:S(2)}, u32[]{:S(2)}) collective-permute-start(f32[6,16,512]{2,1,0:T(8,128)} %get-tuple-element.13), channel_id=1, source_target_pairs={{0,2},{2,0},{4,6},{6,4},{8,10},{10,8},{12,14},{14,12},{16,18},{18,... | collective-permute-start | bytes 589832 | tf_op jit(solution)/shard_map/ppermute | solution.py:271
  6.1 5.1 %collective-permute-start.1 = (f32[6,16,512]{2,1,0:T(8,128)}, f32[6,16,512]{2,1,0:T(8,128)S(1)}, u32[]{:S(2)}, u32[]{:S(2)}) collective-permute-start(f32[6,16,512]{2,1,0:T(8,128)} %get-tuple-element.14), channel_id=1, source_target_pairs={{2,4},{4,2},{6,8},{8,6},{10,12},{12,10},{14,16},{16,14},{18,20},{2... | collective-permute-start | bytes 589832 | tf_op jit(solution)/shard_map/ppermute | solution.py:271
  6.8 1.6 %collective-permute-start.2 = (f32[6,8,1,512]{3,2,1,0:T(1,128)}, f32[6,8,1,512]{3,2,1,0:T(1,128)S(1)}, u32[]{:S(2)}, u32[]{:S(2)}) collective-permute-start(f32[6,8,1,512]{3,2,1,0:T(1,128)} %get-tuple-element.15), channel_id=1, source_target_pairs={{0,1},{1,0},{2,3},{3,2},{4,5},{5,4},{6,7},{7,6},{8,9},{9,8},{10,11... | collective-permute-start | bytes 294920 | tf_op jit(solution)/shard_map/ppermute | solution.py:271
  8.4 2.9 %copy-start.2 = (f32[6,8,1,512]{3,2,1,0:T(1,128)}, f32[6,8,1,512]{3,2,1,0:T(1,128)S(1)}, u32[]{:S(2)}) copy-start(f32[6,8,1,512]{3,2,1,0:T(1,128)S(1)} %collective-permute-done.2.refs_8_.refs_11_) | copy-start | bytes 294916
  11.3 0.7 %copy-start = (f32[6,16,512]{2,1,0:T(8,128)}, f32[6,16,512]{2,1,0:T(8,128)S(1)}, u32[]{:S(2)}) copy-start(f32[6,16,512]{2,1,0:T(8,128)S(1)} %collective-permute-done.refs_6_.refs_9_) | copy-start | bytes 589828
  11.9 0.7 %copy-start.1 = (f32[6,16,512]{2,1,0:T(8,128)}, f32[6,16,512]{2,1,0:T(8,128)S(1)}, u32[]{:S(2)}) copy-start(f32[6,16,512]{2,1,0:T(8,128)S(1)} %collective-permute-done.1.refs_7_.refs_10_) | copy-start | bytes 589828
  22.4 12.9 %collective-permute-start.3 = (f32[5,16,512]{2,1,0:T(8,128)}, f32[5,16,512]{2,1,0:T(8,128)S(1)}, u32[]{:S(2)}, u32[]{:S(2)}) collective-permute-start(f32[5,16,512]{2,1,0:T(8,128)} %get-tuple-element.18), channel_id=1, source_target_pairs={{0,2},{2,0},{4,6},{6,4},{8,10},{10,8},{12,14},{14,12},{16,18},{18,... | collective-permute-start | bytes 491528 | tf_op jit(solution)/shard_map/ppermute | solution.py:271
  28.7 6.7 %collective-permute-start.4 = (f32[5,16,512]{2,1,0:T(8,128)}, f32[5,16,512]{2,1,0:T(8,128)S(1)}, u32[]{:S(2)}, u32[]{:S(2)}) collective-permute-start(f32[5,16,512]{2,1,0:T(8,128)} %get-tuple-element.19), channel_id=1, source_target_pairs={{2,4},{4,2},{6,8},{8,6},{10,12},{12,10},{14,16},{16,14},{18,20},{2... | collective-permute-start | bytes 491528 | tf_op jit(solution)/shard_map/ppermute | solution.py:271
  29.4 1.6 %collective-permute-start.5 = (f32[5,8,1,512]{3,2,1,0:T(1,128)}, f32[5,8,1,512]{3,2,1,0:T(1,128)S(1)}, u32[]{:S(2)}, u32[]{:S(2)}) collective-permute-start(f32[5,8,1,512]{3,2,1,0:T(1,128)} %get-tuple-element.20), channel_id=1, source_target_pairs={{0,1},{1,0},{2,3},{3,2},{4,5},{5,4},{6,7},{7,6},{8,9},{9,8},{10,11... | collective-permute-start | bytes 245768 | tf_op jit(solution)/shard_map/ppermute | solution.py:271
  30.9 4.5 %copy-start.5 = (f32[5,8,1,512]{3,2,1,0:T(1,128)}, f32[5,8,1,512]{3,2,1,0:T(1,128)S(1)}, u32[]{:S(2)}) copy-start(f32[5,8,1,512]{3,2,1,0:T(1,128)S(1)} %collective-permute-done.5.refs_8_) | copy-start | bytes 245764
  35.4 0.7 copy-start.3
  35.4 0.7 %copy-start.4 = (f32[5,16,512]{2,1,0:T(8,128)}, f32[5,16,512]{2,1,0:T(8,128)S(1)}, u32[]{:S(2)}) copy-start(f32[5,16,512]{2,1,0:T(8,128)S(1)} %collective-permute-done.4.refs_7_) | copy-start | bytes 491524
  46.7 1.4 %collective-permute-start.6 = (f32[8,128]{1,0:T(8,128)}, f32[8,128]{1,0:T(8,128)S(1)}, u32[]{:S(2)}, u32[]{:S(2)}) collective-permute-start(f32[8,128]{1,0:T(8,128)} %sums.1), channel_id=1, source_target_pairs={{0,1},{1,0},{2,3},{3,2},{4,5},{5,4},{6,7},{7,6},{8,9},{9,8},{10,11... | collective-permute-start | bytes 12296 | tf_op jit(solution)/shard_map/ppermute | solution.py:282
  48.8 3.9 %collective-permute-start.7 = (f32[8,128]{1,0:T(8,128)S(1)}, f32[8,128]{1,0:T(8,128)S(1)}, u32[]{:S(2)}, u32[]{:S(2)}) collective-permute-start(f32[8,128]{1,0:T(8,128)S(1)} %add.15), channel_id=1, source_target_pairs={{0,2},{2,0},{4,6},{6,4},{8,10},{10,8},{12,14},{14,12},{16,18},{18,... | collective-permute-start | bytes 12296 | tf_op jit(solution)/shard_map/ppermute | solution.py:282
  52.7 3.6 %collective-permute-start.8 = (f32[8,128]{1,0:T(8,128)S(1)}, f32[8,128]{1,0:T(8,128)S(1)}, u32[]{:S(2)}, u32[]{:S(2)}) collective-permute-start(f32[8,128]{1,0:T(8,128)S(1)} %add.16), channel_id=1, source_target_pairs={{0,4},{2,6},{4,0},{6,2},{8,12},{10,14},{12,8},{14,10},{16,20},{18,... | collective-permute-start | bytes 12296 | tf_op jit(solution)/shard_map/ppermute | solution.py:282
  56.3 5.3 %collective-permute-start.9 = (f32[8,128]{1,0:T(8,128)S(1)}, f32[8,128]{1,0:T(8,128)S(1)}, u32[]{:S(2)}, u32[]{:S(2)}) collective-permute-start(f32[8,128]{1,0:T(8,128)S(1)} %add.17), channel_id=1, source_target_pairs={{0,8},{2,10},{4,12},{6,14},{8,0},{10,2},{12,4},{14,6},{16,24},{18,... | collective-permute-start | bytes 12296 | tf_op jit(solution)/shard_map/ppermute | solution.py:282
  61.6 4.6 %collective-permute-start.10 = (f32[8,128]{1,0:T(8,128)S(1)}, f32[8,128]{1,0:T(8,128)S(1)}, u32[]{:S(2)}, u32[]{:S(2)}) collective-permute-start(f32[8,128]{1,0:T(8,128)S(1)} %add.18), channel_id=1, source_target_pairs={{0,16},{2,18},{4,20},{6,22},{8,24},{10,26},{12,28},{14,30},{16,0},... | collective-permute-start | bytes 12296 | tf_op jit(solution)/shard_map/ppermute | solution.py:282
where the time goes:
time: 67 us; the launch traced here: 66.7 us
  Pallas kernels  22.9 us (34%)
  starting transfers between devices  21.4 us (32%)
  waiting for transfers between devices  17.8 us (27%)
  local copies, waits for them, and re-layouts  2.71 us (4%)
  other arithmetic  1.22 us (2%)
  between operations  0.7 us (1%)
    ppermute x5, starting transfers between devices, all_sum(): lax.ppermute(value, axis, [(i, i ^ step) for i in range(count)])  10.7 us
    ppermute x6, starting transfers between devices, exchange(): lax.ppermute(face, axis, pairs(count, k))  10.7 us
    pallas_call x1, Pallas kernels, per_device(): pl.pallas_call(functools.partial(sweep_kernel, True, n_span), out_shape=[...  9.81 us
    ppermute x6, waiting for transfers between devices, exchange(): lax.ppermute(face, axis, pairs(count, k))  9.7 us
    pallas_call x1, Pallas kernels, per_device(): pl.pallas_call(functools.partial(sweep_kernel, False, n_span), out_shape=...  9.19 us
    ppermute x5, waiting for transfers between devices, all_sum(): lax.ppermute(value, axis, [(i, i ^ step) for i in range(count)])  8.12 us
    unnamed x15, local copies, waits for them, and re-layouts  2.71 us
    pallas_call x1, Pallas kernels, per_device(): pl.pallas_call(functools.partial(pack_kernel, n_span), out_shape=[shape(N...  2.54 us
  transfers between devices with their start and end apart: 11, of which 9 were waited for; matrix products, arithmetic and copies ran while one was open for 1% of the time, Pallas kernels for 0%

commit v1 on v0

--- a/solution.py
+++ b/solution.py
@@ -11,11 +11,20 @@
 SUB, LANE = 8, 128
 F32 = jnp.float32
 VMEM = pl.BlockSpec(memory_space=pltpu.VMEM)
+HBM = pl.BlockSpec(memory_space=pltpu.HBM)
 SMEM = pl.BlockSpec(memory_space=pltpu.SMEM)
 
 
 def shape(*dims):
-    return jax.ShapeDtypeStruct(dims, F32)
+    return pltpu.VMEM(dims, F32)
+
+
+def hold(*arrays, space=pltpu.VMEM):
+    return [pltpu.with_memory_space_constraint(a, space) for a in arrays]
+
+
+def params():
+    return pltpu.CompilerParams(vmem_limit_bytes=4 << 20)
 
 
 def cost(flops, transcendentals, bytes_accessed):
@@ -55,8 +64,16 @@
             out_refs[1][c, i] = jnp.where(is_odd, tail, head)
 
 
-def pack_kernel(n_span, v, flow, fa, fb, *rest):
-    spans, rows = rest[:n_span], rest[n_span:]
+def pack_kernel(n_span, v_hbm, flow_hbm, v, flow, fa, fb, *rest):
+    spans, rows, sem = rest[:n_span], rest[n_span:-1], rest[-1]
+    copies = [
+        pltpu.make_async_copy(src, dst, sem.at[k])
+        for k, (src, dst) in enumerate(((flow_hbm, flow), (v_hbm, v)))
+    ]
+    for copy in copies:
+        copy.start()
+    for copy in copies:
+        copy.wait()
     plane_a, plane_b = stream_faces(v, fa, fb)
     for ref, plane in ((fa, plane_a), (fb, plane_b)):
         ref[NV] = quarter_speed(*[flow[c, plane] for c in range(NV)])
@@ -162,101 +179,145 @@
         codes[i] = jnp.broadcast_to(column, (columns, LANE))
 
 
-def sweep_kernel(first, n_span, *refs):
-    refs = list(refs)
-    v = refs.pop(0)
-    src = refs.pop(0)
-    pre = refs.pop(0)
-    jac_in = refs.pop(0)
-    bc = refs.pop(0)
-    speed_in = refs.pop(0)
-    ha, hb = refs.pop(0), refs.pop(0)
-    spans = [refs.pop(0) for _ in range(n_span)]
-    if not first:
-        gha, ghb = refs.pop(0), refs.pop(0)
-        gspans = [refs.pop(0) for _ in range(n_span)]
-    else:
-        gha, ghb, gspans = ha, hb, spans
-    out, ssq_out = refs.pop(0), refs.pop(0)
-    if first:
-        g = refs.pop(0)
-        fa, fb = refs.pop(0), refs.pop(0)
-        span_out = [refs.pop(0) for _ in range(n_span)]
-    else:
-        g = speed_in
-    halves, codes = refs
-    planes = v.shape[1]
-    spread_codes(bc, codes)
-
-    for d in range(3):
-        for u in range(NV):
-            for c in range(NV):
-                halves[d, u, c] = 0.5 * jac_in[d, u, c]
-    if first:
-
-        def speed_plane(i, carry):
-            g[i] = quarter_speed(*[speed_in[c, i] for c in range(NV)])
-            return carry
-
-        lax.fori_loop(0, planes, speed_plane, 0)
-
+def pick(is_odd, pair, even_ref, idx):
+    if len(pair) == 1:
+        keep = is_odd if even_ref == 1 else jnp.logical_not(is_odd)
+        return jnp.where(keep, pair[0][idx], 0.0)
+    return jnp.where(is_odd, pair[1 - even_ref][idx], pair[even_ref][idx])
+
+
+def make_plane(v, g, src, pre, jac, codes, out, streams, g_streams, spans, g_spans):
+    planes = v.shape[1]
     stream_odd, span_odd = odd("stream"), odd("span")
 
-    def pick(is_odd, pair, even_ref, idx):
-        other = 1 - even_ref
-        if len(pair) == 1:
-            keep = is_odd if even_ref == 1 else jnp.logical_not(is_odd)
-            return jnp.where(keep, pair[0][idx], 0.0)
-        return jnp.where(is_odd, pair[other][idx], pair[even_ref][idx])
-
-    def low_halo(c, *sl):
-        pair = (gha, ghb) if c == NV else (ha, hb)
-        return pick(stream_odd, pair, 1, (c, *sl))
-
-    def high_halo(c, *sl):
-        pair = (gha, ghb) if c == NV else (ha, hb)
-        return pick(stream_odd, pair, 0, (c, *sl))
+    def halo(even_ref):
+        return lambda c, *sl: pick(
+            stream_odd, g_streams if c == NV else streams, even_ref, (c, *sl)
+        )
 
     def rows_of(even_ref, i):
         def get(c, kb):
-            pair = gspans if c == NV else spans
+            pair = g_spans if c == NV else spans
             one = pick(span_odd, pair, even_ref, (c, i, slice(None), pl.ds(kb * LANE, LANE)))
             return jnp.broadcast_to(one, (SUB, LANE))
 
         return get
 
-    def plane(i, prev, nxt, gprev, gnxt, ssq):
+    def plane(i, ssq):
+        first = isinstance(i, int) and i == 0
+        last = isinstance(i, int) and i == planes - 1
+        low, high = halo(1), halo(0)
         return sweep_plane(
-            i, v, prev, nxt, g, gprev, gnxt, rows_of(1, i), rows_of(0, i), src, pre, halves,
+            i,
+            v,
+            low if first else lambda c, *sl: v[(c, i - 1, *sl)],
+            high if last else lambda c, *sl: v[(c, i + 1, *sl)],
+            g,
+            (lambda *sl: low(NV, *sl)) if first else lambda *sl: g[(i - 1, *sl)],
+            (lambda *sl: high(NV, *sl)) if last else lambda *sl: g[(i + 1, *sl)],
+            rows_of(1, i),
+            rows_of(0, i),
+            src,
+            pre,
+            jac,
             lambda jb: codes[i, pl.ds(jb * SUB, SUB), :],
-            out, ssq,
-        )
-
-    def inner(i, ssq):
-        return plane(
-            i,
-            lambda c, *sl: v[(c, i - 1, *sl)],
-            lambda c, *sl: v[(c, i + 1, *sl)],
-            lambda *sl: g[(i - 1, *sl)],
-            lambda *sl: g[(i + 1, *sl)],
+            out,
             ssq,
         )
 
-    ssq = jnp.zeros((SUB, LANE), F32)
-    ssq = lax.fori_loop(1, planes - 1, inner, ssq)
-    ssq = plane(
-        0, low_halo, lambda c, *sl: v[(c, 1, *sl)],
-        lambda *sl: low_halo(NV, *sl), lambda *sl: g[(1, *sl)], ssq,
-    )
-    ssq = plane(
-        planes - 1, lambda c, *sl: v[(c, planes - 2, *sl)], high_halo,
-        lambda *sl: g[(planes - 2, *sl)], lambda *sl: high_halo(NV, *sl), ssq,
-    )
-    ssq_out[...] = ssq
-    if first:
-        stream_faces(out, fa, fb)
-        for c in range(NV):
-            span_rows(out, c, 0, v.shape[2] - 1, span_out)
+    return plane
+
+
+def no_sum():
+    return jnp.zeros((SUB, LANE), F32)
+
+
+def first_inner(n_span, v, flow, src_hbm, pre_hbm, jac, bc, *refs):
+    spans = refs[:n_span]
+    out, g, src, pre, codes, ssq_out, sem = refs[n_span:]
+    planes = v.shape[1]
+
+    def loads(i):
+        return (
+            pltpu.make_async_copy(src_hbm.at[:, i], src.at[:, i], sem.at[0, i]),
+            pltpu.make_async_copy(pre_hbm.at[:, :, i], pre.at[:, :, i], sem.at[1, i]),
+        )
+
+    for i in [*range(1, planes - 1), 0, planes - 1]:
+        for load in loads(i):
+            load.start()
+    spread_codes(bc, codes)
+
+    def speed_plane(i, carry):
+        g[i] = quarter_speed(*[flow[c, i] for c in range(NV)])
+        return carry
+
+    lax.fori_loop(0, planes, speed_plane, 0)
+    plane = make_plane(v, g, src, pre, jac, codes, out, (), (), spans, spans)
+
+    def inner(i, ssq):
+        for load in loads(i):
+            load.wait()
+        return plane(i, ssq)
+
+    ssq_out[...] = lax.fori_loop(1, planes - 1, inner, no_sum())
+    for i in (0, planes - 1):
+        for load in loads(i):
+            load.wait()
+
+
+def first_edge(n_span, v, g, src, pre, jac, codes, ssq_in, out_in, ha, hb, *refs):
+    spans = refs[:n_span]
+    out, ssq_out, fa, fb = refs[n_span : n_span + 4]
+    span_out = refs[n_span + 4 :]
+    planes = v.shape[1]
+    plane = make_plane(v, g, src, pre, jac, codes, out, (ha, hb), (ha, hb), spans, spans)
+    ssq_out[...] = plane(planes - 1, plane(0, ssq_in[...]))
+    stream_faces(out, fa, fb)
+    for c in range(NV):
+        span_rows(out, c, 0, v.shape[2] - 1, span_out)
+
+
+def second_inner(n_span, v, g, src, pre, jac, codes, *refs):
+    spans, g_spans = refs[:n_span], refs[n_span : 2 * n_span]
+    out_hbm, ssq_out, out, sem = refs[2 * n_span :]
+    planes = v.shape[1]
+    plane = make_plane(v, g, src, pre, jac, codes, out, (), (), spans, g_spans)
+
+    def store(i):
+        return pltpu.make_async_copy(out.at[:, i], out_hbm.at[:, i], sem.at[i])
+
+    def inner(i, ssq):
+        ssq = plane(i, ssq)
+        store(i).start()
+        return ssq
+
+    ssq_out[...] = lax.fori_loop(1, planes - 1, inner, no_sum())
+
+    def finish(i, carry):
+        store(i).wait()
+        return carry
+
+    lax.fori_loop(1, planes - 1, finish, 0)
+
+
+def second_edge(n_span, v, g, src, pre, jac, codes, ssq_before, ssq_in, out_in, *refs):
+    streams, g_streams = refs[:2], refs[2:4]
+    spans, g_spans = refs[4 : 4 + n_span], refs[4 + n_span : 4 + 2 * n_span]
+    out_hbm, sums, out, sem = refs[4 + 2 * n_span :]
+    planes = v.shape[1]
+    plane = make_plane(v, g, src, pre, jac, codes, out, streams, g_streams, spans, g_spans)
+    ssq = ssq_in[...]
+    stores = []
+    for k, i in enumerate((0, planes - 1)):
+        ssq = plane(i, ssq)
+        stores.append(pltpu.make_async_copy(out.at[:, i], out_hbm.at[:, i], sem.at[k]))
+        stores[-1].start()
+    lane = lax.broadcasted_iota(jnp.int32, sums.shape, 1)
+    before, now = jnp.sum(ssq_before[...]), jnp.sum(ssq)
+    sums[...] = jnp.where(lane == 0, before, jnp.where(lane == 1, now, 0.0))
+    for store in stores:
+        store.wait()
 
 
 def pairs(count, offset):
@@ -271,74 +332,91 @@
     return [lax.ppermute(face, axis, pairs(count, k)) for k, face in enumerate(faces)]
 
 
-def all_sum(value):
-    for axis in ("span", "stream"):
-        count = lax.axis_size(axis)
-        if count & (count - 1):
-            value = lax.psum(value, axis)
-            continue
-        step = 1
-        while step < count:
-            value = value + lax.ppermute(value, axis, [(i, i ^ step) for i in range(count)])
-            step *= 2
-    return value
-
-
-def finish_kernel(a, b, out):
-    lane = lax.broadcasted_iota(jnp.int32, (SUB, LANE), 1)
-    out[...] = jnp.where(lane == 0, jnp.sum(a[...]), jnp.where(lane == 1, jnp.sum(b[...]), 0.0))
-
-
 def per_device(adjoint_start, source, flow_state, precond, flux_jac, bc_codes):
     _, planes, rows, lanes = adjoint_start.shape
     n_stream, n_span_all = lax.axis_size("stream"), lax.axis_size("span")
+    n_devices = n_stream * n_span_all
     n_span = 1 if n_span_all <= 2 else 2
     cells = planes * rows * lanes
-    cells_all = float(NV * cells * n_stream * n_span_all)
-    scratch = [pltpu.SMEM((3, NV, NV), F32), pltpu.VMEM((planes, rows, LANE), F32)]
-
-    faces = pl.pallas_call(
+    field = shape(NV, planes, rows, lanes)
+    tile = shape(SUB, LANE)
+    dma = pltpu.SemaphoreType.DMA
+    jac = 0.5 * flux_jac
+    inner_cost = cost(3000 * cells, 4 * cells, 42 * 4 * cells)
+    edge_cost = cost(100 * cells, 0, 42 * cells)
+
+    v, flow, *faces = pl.pallas_call(
         functools.partial(pack_kernel, n_span),
-        out_shape=[shape(NV + 1, rows, lanes)] * 2 + [shape(NV + 1, planes, 1, lanes)] * n_span,
-        in_specs=[VMEM] * 2,
-        out_specs=[VMEM] * (2 + n_span),
-        scratch_shapes=[pltpu.VMEM((NV, planes, 1, lanes), F32)] * n_span,
+        out_shape=[field, field]
+        + [shape(NV + 1, rows, lanes)] * 2
+        + [shape(NV + 1, planes, 1, lanes)] * n_span,
+        in_specs=[HBM] * 2,
+        out_specs=[VMEM] * (4 + n_span),
+        scratch_shapes=[pltpu.VMEM((NV, planes, 1, lanes), F32)] * n_span + [dma((2,))],
         cost_estimate=cost(cells, 0, 8 * cells),
+        compiler_params=params(),
         name="pack",
-    )(adjoint_start, flow_state)
-    stream0 = exchange(faces[:2], "stream")
-    span0 = exchange(faces[2:], "span")
-
-    outs = pl.pallas_call(
-        functools.partial(sweep_kernel, True, n_span),
-        out_shape=[shape(NV, planes, rows, lanes), shape(SUB, LANE), shape(planes, rows, lanes)]
+    )(*hold(adjoint_start, flow_state, space=pltpu.HBM))
+    streams = exchange(faces[:2], "stream")
+    spans = exchange(faces[2:], "span")
+
+    adjoint, g, src, pre, codes, ssq = pl.pallas_call(
+        functools.partial(first_inner, n_span),
+        out_shape=[
+            field, shape(planes, rows, lanes), field, shape(NV, NV, planes, rows, lanes),
+            shape(planes, rows, LANE), tile,
+        ],
+        in_specs=[VMEM] * 2 + [HBM] * 2 + [SMEM] + [VMEM] * (1 + n_span),
+        out_specs=[VMEM] * 6,
+        scratch_shapes=[dma((2, planes))],
+        cost_estimate=inner_cost,
+        compiler_params=params(),
+        name="first_inner",
+    )(*hold(v, flow), *hold(source, precond, space=pltpu.HBM), jac, *hold(bc_codes, *spans))
+
+    adjoint, ssq_first, *faces = pl.pallas_call(
+        functools.partial(first_edge, n_span),
+        out_shape=[field, tile]
         + [shape(NV, rows, lanes)] * 2
         + [shape(NV, planes, 1, lanes)] * n_span,
-        in_specs=[VMEM] * 3 + [SMEM] + [VMEM] * (4 + n_span),
-        out_specs=[VMEM] * (5 + n_span),
-        scratch_shapes=scratch,
-        cost_estimate=cost(350 * cells, 4 * cells, 42 * 4 * cells),
-        name="sweep_first",
-    )(adjoint_start, source, precond, flux_jac, bc_codes, flow_state, *stream0, *span0)
-    adjoint, ssq0, quarter = outs[:3]
-    stream1 = exchange(outs[3:5], "stream")
-    span1 = exchange(outs[5:], "span")
-
-    adjoint, ssq1 = pl.pallas_call(
-        functools.partial(sweep_kernel, False, n_span),
-        out_shape=[shape(NV, planes, rows, lanes), shape(SUB, LANE)],
-        in_specs=[VMEM] * 3 + [SMEM] + [VMEM] * (6 + 2 * n_span),
-        out_specs=[VMEM] * 2,
-        scratch_shapes=scratch,
-        cost_estimate=cost(350 * cells, 0, 42 * 4 * cells),
-        name="sweep_second",
-    )(adjoint, source, precond, flux_jac, bc_codes, quarter, *stream1, *span1, *stream0, *span0)
-
-    sums = pl.pallas_call(
-        finish_kernel, out_shape=shape(SUB, LANE), in_specs=[VMEM] * 2, out_specs=VMEM, name="sums"
-    )(ssq0, ssq1)
-    residual_rms = jnp.sqrt(all_sum(sums)[0, :2] / cells_all)
-    return (adjoint, residual_rms)
+        in_specs=[VMEM] * 4 + [SMEM] + [VMEM] * (5 + n_span),
+        out_specs=[VMEM] * (4 + n_span),
+        input_output_aliases={7: 0},
+        cost_estimate=edge_cost,
+        compiler_params=params(),
+        name="first_edge",
+    )(*hold(v, g, src, pre), jac, *hold(codes, ssq, adjoint, *streams, *spans))
+    streams_next = exchange(faces[:2], "stream")
+    spans_next = exchange(faces[2:], "span")
+
+    result, ssq = pl.pallas_call(
+        functools.partial(second_inner, n_span),
+        out_shape=[pltpu.HBM(adjoint_start.shape, F32), tile],
+        in_specs=[VMEM] * 4 + [SMEM] + [VMEM] * (1 + 2 * n_span),
+        out_specs=[HBM, VMEM],
+        scratch_shapes=[field, dma((planes,))],
+        cost_estimate=inner_cost,
+        compiler_params=params(),
+        name="second_inner",
+    )(*hold(adjoint, g, src, pre), jac, *hold(codes, *spans_next, *spans))
+
+    result, sums = pl.pallas_call(
+        functools.partial(second_edge, n_span),
+        out_shape=[pltpu.HBM(adjoint_start.shape, F32), shape(n_devices, LANE)],
+        in_specs=[VMEM] * 4 + [SMEM] + [VMEM] * 3 + [HBM] + [VMEM] * (4 + 2 * n_span),
+        out_specs=[HBM, VMEM],
+        scratch_shapes=[field, dma((2,))],
+        input_output_aliases={8: 0},
+        cost_estimate=edge_cost,
+        compiler_params=params(),
+        name="second_edge",
+    )(
+        *hold(adjoint, g, src, pre), jac, *hold(codes, ssq_first, ssq), *hold(result, space=pltpu.HBM),
+        *hold(*streams_next, *streams, *spans_next, *spans),
+    )
+    sums = lax.all_to_all(sums, ("stream", "span"), 0, 0, tiled=True)
+    cells_all = float(NV * cells * n_devices)
+    return (result, jnp.sqrt(jnp.sum(sums, axis=0)[:2] / cells_all))
 
 
 def solution(mesh):

time: 67 us -> 44.6 us (0.67)
  waiting for transfers between devices: 17.8 us -> 1.28 us
  blocking collectives: 0 us -> 14.6 us
  starting transfers between devices: 21.4 us -> 10.9 us
  Pallas kernels: 22.9 us -> 16.4 us
  local copies, waits for them, and re-layouts: 2.71 us -> 0.01 us
    all_to_all x0 -> x1, blocking collectives: none -> 14.6 us  [per_device(): sums = lax.all_to_all(sums, ('stream', 'span'), 0, 0, tiled=True)]
    ppermute x5 -> x0, starting transfers between devices: 10.7 us -> none  [all_sum(): lax.ppermute(value, axis, [(i, i ^ step) for i in range(count)])]
    ppermute x6, waiting for transfers between devices: 9.7 us -> 1.28 us  [exchange(): lax.ppermute(face, axis, pairs(count, k))]
    ppermute x5 -> x0, waiting for transfers between devices: 8.12 us -> none  [all_sum(): lax.ppermute(value, axis, [(i, i ^ step) for i in range(count)])]
    pallas_call x4 -> x5, Pallas kernels: 22.9 us -> 16.4 us  [the longest x1 5.35 us: per_device(): pl.pallas_call(functools.partial(first_inner, n_span), out_shape=[field,...]
    unnamed x15 -> x4, local copies, waits for them, and re-layouts: 2.71 us -> 0.01 us
    add x5 -> x0, other arithmetic: 0.69 us -> none  [all_sum(): value + lax.ppermute(value, axis, [(i, i ^ step) for i in range(count)])]
  transfers between devices with their start and end apart: 11 -> 6, of which waited for: 9 -> 1; matrix products, arithmetic and copies ran while one was open for 1% -> 0% of each run, Pallas kernels for 0% -> 23%
where the time goes in v1:
time: 44.6 us; the launch traced here: 44.5 us
  Pallas kernels  16.4 us (37%)
  blocking collectives  14.6 us (33%)
  starting transfers between devices  10.9 us (24%)
  waiting for transfers between devices  1.28 us (3%)
  between operations  0.78 us (2%)
  other arithmetic  0.58 us (1%)
    all_to_all x1, blocking collectives, per_device(): sums = lax.all_to_all(sums, ('stream', 'span'), 0, 0, tiled=True)  14.6 us
    ppermute x6, starting transfers between devices, exchange(): lax.ppermute(face, axis, pairs(count, k))  10.9 us
    pallas_call x1, Pallas kernels, per_device(): pl.pallas_call(functools.partial(first_inner, n_span), out_shape=[field,...  5.35 us
    pallas_call x1, Pallas kernels, per_device(): pl.pallas_call(functools.partial(second_inner, n_span), out_shape=[pltpu....  4.73 us
    pallas_call x1, Pallas kernels, per_device(): pl.pallas_call(functools.partial(second_edge, n_span), out_shape=[pltpu.H...  2.53 us
    pallas_call x1, Pallas kernels, per_device(): pl.pallas_call(functools.partial(first_edge, n_span), out_shape=[field, t...  1.89 us
    pallas_call x1, Pallas kernels, per_device(): pl.pallas_call(functools.partial(pack_kernel, n_span), out_shape=[field,...  1.89 us
    ppermute x6, waiting for transfers between devices, exchange(): lax.ppermute(face, axis, pairs(count, k))  1.28 us
  transfers between devices with their start and end apart: 6, of which 1 were waited for; matrix products, arithmetic and copies ran while one was open for 0% of the time, Pallas kernels for 23%

profile of v1, /device:TPU:0, one launch (start us, length us, event | category | flops | bytes accessed | tf_op | source)
XLA Modules:
  0.0 44.5 jit_solution(6829006446725080220)
XLA Ops:
  0.6 0.0 copy-start.1
  0.6 0.0 copy-start
  0.7 1.9 %pack.1 = (f32[5,8,16,512]{3,2,1,0:T(8,128)S(1)}, f32[5,8,16,512]{3,2,1,0:T(8,128)S(1)}, f32[6,16,512]{2,1,0:T(8,128)S(1)}, f32[6,16,512]{2,1,0:T(8,128)S(1)}, f32[6,8,1,512]{3,2,1,0:T(1,128)S(1)}) custom-call(f32[5,8,16,512]{3,2,1,0:T(8,128)} %v_hbm.1, f32[5,8,16,512]{3,2,1,0:T(8,128)} %flow_hbm.1), custom_call_target="tpu_custom_call" | custom-call | flops 65536 | bytes 524288 | tf_op jit(solution)/shard_map/pack/pallas_call | solution.py:348
  2.5 0.6 %collective-permute-start = (f32[6,8,1,512]{3,2,1,0:T(1,128)S(1)}, f32[6,8,1,512]{3,2,1,0:T(1,128)S(1)}, u32[]{:S(2)}, u32[]{:S(2)}) collective-permute-start(f32[6,8,1,512]{3,2,1,0:T(1,128)S(1)} %get-tuple-element.24), channel_id=1, source_target_pairs={{0,1},{1,0},{2,3},{3,2},{4,5},{5,4},{6,7},{7,6},{8,9},{9,8},{10,11... | collective-permute-start | bytes 294920 | tf_op jit(solution)/shard_map/ppermute | solution.py:332
  3.1 2.6 %collective-permute-start.1 = (f32[6,16,512]{2,1,0:T(8,128)S(1)}, f32[6,16,512]{2,1,0:T(8,128)S(1)}, u32[]{:S(2)}, u32[]{:S(2)}) collective-permute-start(f32[6,16,512]{2,1,0:T(8,128)S(1)} %get-tuple-element.31), channel_id=1, source_target_pairs={{0,2},{2,0},{4,6},{6,4},{8,10},{10,8},{12,14},{14,12},{16,18},{18,... | collective-permute-start | bytes 589832 | tf_op jit(solution)/shard_map/ppermute | solution.py:332
  5.7 0.7 %collective-permute-start.2 = (f32[6,16,512]{2,1,0:T(8,128)S(1)}, f32[6,16,512]{2,1,0:T(8,128)S(1)}, u32[]{:S(2)}, u32[]{:S(2)}) collective-permute-start(f32[6,16,512]{2,1,0:T(8,128)S(1)} %get-tuple-element.32), channel_id=1, source_target_pairs={{2,4},{4,2},{6,8},{8,6},{10,12},{12,10},{14,16},{16,14},{18,20},{2... | collective-permute-start | bytes 589832 | tf_op jit(solution)/shard_map/ppermute | solution.py:332
  6.3 0.0 copy-done.1
  6.4 0.0 collective-permute-done.refs_0_.refs_1_.refs_5_
  6.4 0.0 copy-done
  6.4 5.4 %first_inner.1 = (f32[5,8,16,512]{3,2,1,0:T(8,128)S(1)}, f32[8,16,512]{2,1,0:T(8,128)S(1)}, f32[5,8,16,512]{3,2,1,0:T(8,128)S(1)}, f32[5,5,8,16,512]{4,3,2,1,0:T...) custom-call(f32[5,8,16,512]{3,2,1,0:T(8,128)S(1)} %get-tuple-element.22.v, ...), custom_call_target="tpu_custom_call" | custom-call | flops 196608000 | bytes 11010048 | tf_op jit(solution)/shard_map/first_inner/pallas_call | solution.py:363
  11.7 0.0 collective-permute-done.1.ha.refs_2_
  11.7 0.0 collective-permute-done.2.hb.refs_3_
  11.8 1.9 %first_edge.1 = (f32[5,8,16,512]{3,2,1,0:T(8,128)S(1)}, f32[8,128]{1,0:T(8,128)S(1)}, f32[5,16,512]{2,1,0:T(8,128)S(1)}, f32[5,16,512]{2,1,0:T(8,128)S(1)}, f32[5,8,1,512]{3,2,1,0:T(1,128)S(1)}) custom-call(f32[5,8,16,512]{3,2,1,0:T(8,128)S(1)} %get-tuple-element.22.v, f32[8,16,512]{2,1,0:T(8,128)S(1)} %get-tuple-element.25.g, ...), custom_call_target="tpu_custom_call", output_to_operand_aliasing={{0}: (7, {})} | custom-call | flops 6553600 | bytes 2752512 | tf_op jit(solution)/shard_map/first_edge/pallas_call | solution.py:377
  13.7 6.4 %collective-permute-start.4 = (f32[5,16,512]{2,1,0:T(8,128)S(1)}, f32[5,16,512]{2,1,0:T(8,128)S(1)}, u32[]{:S(2)}, u32[]{:S(2)}) collective-permute-start(f32[5,16,512]{2,1,0:T(8,128)S(1)} %get-tuple-element.38), channel_id=1, source_target_pairs={{0,2},{2,0},{4,6},{6,4},{8,10},{10,8},{12,14},{14,12},{16,18},{18,... | collective-permute-start | bytes 491528 | tf_op jit(solution)/shard_map/ppermute | solution.py:332
  20.0 0.7 %collective-permute-start.5 = (f32[5,16,512]{2,1,0:T(8,128)S(1)}, f32[5,16,512]{2,1,0:T(8,128)S(1)}, u32[]{:S(2)}, u32[]{:S(2)}) collective-permute-start(f32[5,16,512]{2,1,0:T(8,128)S(1)} %get-tuple-element.39), channel_id=1, source_target_pairs={{2,4},{4,2},{6,8},{8,6},{10,12},{12,10},{14,16},{16,14},{18,20},{2... | collective-permute-start | bytes 491528 | tf_op jit(solution)/shard_map/ppermute | solution.py:332
  20.7 0.1 collective-permute-start.3
  20.8 1.3 %collective-permute-done.3.refs_0_.refs_4_ = f32[5,8,1,512]{3,2,1,0:T(1,128)S(1)} collective-permute-done((f32[5,8,1,512]{3,2,1,0:T(1,128)S(1)}, f32[5,8,1,512]{3,2,1,0:T(1,128)S(1)}, u32[]{:S(2)}, u32[]{:S(2)}) %collective-permute-start.3) | collective-permute-done | bytes 81952 | tf_op jit(solution)/shard_map/ppermute | solution.py:332
  22.0 4.7 %second_inner.1 = (f32[5,8,16,512]{3,2,1,0:T(8,128)}, f32[8,128]{1,0:T(8,128)S(1)}) custom-call(f32[5,8,16,512]{3,2,1,0:T(8,128)S(1)} %get-tuple-element.33.v, f32[8,16,512]{2,1,0:T(8,128)S(1)} %get-tuple-element.25.g, f32[5,8,16,512]{3,2,1,0:T(8,128)S(1)} %get-tuple-element.26.src, f32[5,5,8,16,512]{4,3,2,1,0:T(8,128)S(1)} %get-tuple-element.27.pre, ...), custom_call_target="tpu_custom_call" | custom-call | flops 196608000 | bytes 11010048 | tf_op jit(solution)/shard_map/second_inner/pallas_call | solution.py:392
  26.8 0.0 collective-permute-done.4.refs_0_
  26.8 0.0 collective-permute-done.5.refs_1_
  26.8 2.5 %second_edge.1 = (f32[5,8,16,512]{3,2,1,0:T(8,128)}, f32[32,128]{1,0:T(8,128)S(1)}) custom-call(f32[5,8,16,512]{3,2,1,0:T(8,128)S(1)} %get-tuple-element.33.v, f32[8,16,512]{2,1,0:T(8,128)S(1)} %get-tuple-element.25.g, f32[5,8,16,512]{3,2,1,0:T(8,128)S(1)} %get-tuple-element.26.src, ...), custom_call_target="tpu_custom_call", output_to_operand_aliasing={{0}: (8, {})} | custom-call | flops 6553600 | bytes 2752512 | tf_op jit(solution)/shard_map/second_edge/pallas_call | solution.py:403
  29.3 14.6 %all_to_all.9 = f32[32,1,128]{2,1,0:T(1,128)S(1)} all-to-all(f32[32,1,128]{2,1,0:T(1,128)S(1)} %bitcast.3), channel_id=1, replica_groups=mesh['stream'=16,'span'=2] {'stream','span'}, dimensions={0} | all-to-all | bytes 32768 | tf_op jit(solution)/shard_map/all_to_all | solution.py:417
  43.9 0.1 reduce_sum.9
  43.9 0.5 %multiply_sqrt_fusion = f32[2]{0:T(128)} fusion(f32[128]{0:T(128)S(1)} %reduce_sum.9), kind=kLoop, calls=%fused_computation.1 | loop fusion | flops 2 | bytes 16 | tf_op jit(solution)/shard_map/sqrt | solution.py:419
  (1 shorter events, 0.0 us)
Async XLA Ops:
  0.6 5.7 %copy-start.1 = (f32[3,5,5]{2,0,1:T(4,128)S(1)}, f32[3,5,5]{2,0,1:T(4,128)}, u32[]{:S(2)}) copy-start(f32[3,5,5]{2,0,1:T(4,128)} %param.10) | copy-start | bytes 904
  0.6 5.7 %copy-start = (s32[8,16]{1,0:T(8,128)S(1)}, s32[8,16]{1,0:T(8,128)}, u32[]{:S(2)}) copy-start(s32[8,16]{1,0:T(8,128)} %bc.1) | copy-start | bytes 1540
  2.5 3.8 %collective-permute-start = (f32[6,8,1,512]{3,2,1,0:T(1,128)S(1)}, f32[6,8,1,512]{3,2,1,0:T(1,128)S(1)}, u32[]{:S(2)}, u32[]{:S(2)}) collective-permute-start(f32[6,8,1,512]{3,2,1,0:T(1,128)S(1)} %get-tuple-element.24), channel_id=1, source_target_pairs={{0,1},{1,0},{2,3},{3,2},{4,5},{5,4},{6,7},{7,6},{8,9},{9,8},{10,11... | collective-permute-start | bytes 294920 | tf_op jit(solution)/shard_map/ppermute | solution.py:332
  3.1 8.6 %collective-permute-start.1 = (f32[6,16,512]{2,1,0:T(8,128)S(1)}, f32[6,16,512]{2,1,0:T(8,128)S(1)}, u32[]{:S(2)}, u32[]{:S(2)}) collective-permute-start(f32[6,16,512]{2,1,0:T(8,128)S(1)} %get-tuple-element.31), channel_id=1, source_target_pairs={{0,2},{2,0},{4,6},{6,4},{8,10},{10,8},{12,14},{14,12},{16,18},{18,... | collective-permute-start | bytes 589832 | tf_op jit(solution)/shard_map/ppermute | solution.py:332
  5.7 6.1 %collective-permute-start.2 = (f32[6,16,512]{2,1,0:T(8,128)S(1)}, f32[6,16,512]{2,1,0:T(8,128)S(1)}, u32[]{:S(2)}, u32[]{:S(2)}) collective-permute-start(f32[6,16,512]{2,1,0:T(8,128)S(1)} %get-tuple-element.32), channel_id=1, source_target_pairs={{2,4},{4,2},{6,8},{8,6},{10,12},{12,10},{14,16},{16,14},{18,20},{2... | collective-permute-start | bytes 589832 | tf_op jit(solution)/shard_map/ppermute | solution.py:332
  13.7 13.1 %collective-permute-start.4 = (f32[5,16,512]{2,1,0:T(8,128)S(1)}, f32[5,16,512]{2,1,0:T(8,128)S(1)}, u32[]{:S(2)}, u32[]{:S(2)}) collective-permute-start(f32[5,16,512]{2,1,0:T(8,128)S(1)} %get-tuple-element.38), channel_id=1, source_target_pairs={{0,2},{2,0},{4,6},{6,4},{8,10},{10,8},{12,14},{14,12},{16,18},{18,... | collective-permute-start | bytes 491528 | tf_op jit(solution)/shard_map/ppermute | solution.py:332
  20.0 6.8 %collective-permute-start.5 = (f32[5,16,512]{2,1,0:T(8,128)S(1)}, f32[5,16,512]{2,1,0:T(8,128)S(1)}, u32[]{:S(2)}, u32[]{:S(2)}) collective-permute-start(f32[5,16,512]{2,1,0:T(8,128)S(1)} %get-tuple-element.39), channel_id=1, source_target_pairs={{2,4},{4,2},{6,8},{8,6},{10,12},{12,10},{14,16},{16,14},{18,20},{2... | collective-permute-start | bytes 491528 | tf_op jit(solution)/shard_map/ppermute | solution.py:332
  20.7 1.3 %collective-permute-start.3 = (f32[5,8,1,512]{3,2,1,0:T(1,128)S(1)}, f32[5,8,1,512]{3,2,1,0:T(1,128)S(1)}, u32[]{:S(2)}, u32[]{:S(2)}) collective-permute-start(f32[5,8,1,512]{3,2,1,0:T(1,128)S(1)} %get-tuple-element.35), channel_id=1, source_target_pairs={{0,1},{1,0},{2,3},{3,2},{4,5},{5,4},{6,7},{7,6},{8,9},{9,8},{10,11... | collective-permute-start | bytes 245768 | tf_op jit(solution)/shard_map/ppermute | solution.py:332

commit v2 on v1

v2 whole, which is shorter than its diff:
```python
import functools

import jax
import jax.numpy as jnp
from jax import lax
from jax.experimental import pallas as pl
from jax.experimental.pallas import tpu as pltpu
from jax.sharding import PartitionSpec as P


NV = 5
SUB, LANE = 8, 128
F32 = jnp.float32
VMEM = pl.BlockSpec(memory_space=pltpu.VMEM)
HBM = pl.BlockSpec(memory_space=pltpu.HBM)


def shape(*dims):
    return pltpu.VMEM(dims, F32)


def hold(*arrays, space=pltpu.VMEM):
    return [pltpu.with_memory_space_constraint(a, space) for a in arrays]


def params():
    return pltpu.CompilerParams(vmem_limit_bytes=4 << 20)


def cost(flops, transcendentals, bytes_accessed):
    return pl.CostEstimate(
        flops=int(flops), transcendentals=int(transcendentals), bytes_accessed=int(bytes_accessed)
    )


def quarter_speed(rho, m1, m2, m3, p):
    momentum = jnp.sqrt(m1 * m1 + m2 * m2 + m3 * m3)
    return 0.25 * (momentum / rho + jnp.sqrt(1.4 * p / rho))


def odd(axis):
    return lax.rem(lax.axis_index(axis), 2) == 1


def face_planes(planes):
    is_odd = odd("stream")
    return jnp.where(is_odd, 0, planes - 1), jnp.where(is_odd, planes - 1, 0)


def span_rows(field, c, i, out_refs, k):
    is_odd = odd("span")
    last = field.shape[2] - 1
    head = field[c, i, 0:1, :]
    tail = field[c, i, last : last + 1, :]
    out_refs[0][c, k] = jnp.where(is_odd, head, tail)
    if len(out_refs) > 1:
        out_refs[1][c, k] = jnp.where(is_odd, tail, head)


def pack_kernel(n_span, v_hbm, flow_hbm, v, flow, fa, fb, *rest):
    spans, rows, sem = rest[:n_span], rest[n_span:-1], rest[-1]
    planes = v.shape[1]

    def loads(at, k):
        return [
            pltpu.make_async_copy(src.at[:, at], dst.at[:, at], sem.at[n, k])
            for n, (src, dst) in enumerate(((flow_hbm, flow), (v_hbm, v)))
        ]

    ends = face_planes(planes)
    groups = [loads(ends[0], 0), loads(ends[1], 1), loads(pl.ds(1, planes - 2), 2)]
    for group in groups:
        for load in group:
            load.start()
    for group, face, plane in zip(groups, (fa, fb), ends):
        for load in group:
            load.wait()
        face[NV] = quarter_speed(*[flow[c, plane] for c in range(NV)])
        for c in range(NV):
            face[c] = v[c, plane]
    for load in groups[2]:
        load.wait()
    for c in range(NV):
        for i in range(planes):
            span_rows(v, c, i, spans, i)
            span_rows(flow, c, i, rows, i)
    for ref, row in zip(spans, rows):
        ref[NV] = quarter_speed(*[row[c] for c in range(NV)])


def sweep_plane(i, v, prev, nxt, sign, g, gprev, gnxt, tops, bottoms, src, pre, jac, wall, put, ssq):
    rows_n, lanes_n = v.shape[2] // SUB, v.shape[3] // LANE
    lane = lax.broadcasted_iota(jnp.int32, (SUB, LANE), 1)
    row = lax.broadcasted_iota(jnp.int32, (SUB, LANE), 0)
    first_lane, last_lane = lane == 0, lane == LANE - 1
    first_row, last_row = row == 0, row == SUB - 1
    zero = jnp.zeros((SUB, LANE), F32)

    def at(jb, kb):
        return pl.ds(jb * SUB, SUB), pl.ds(kb * LANE, LANE)

    def shifts(get):
        @functools.cache
        def turned(jb, kb, shift, axis):
            return pltpu.roll(tile(jb, kb), shift % (SUB, LANE)[axis], axis)

        @functools.cache
        def tile(jb, kb):
            return get(*at(jb, kb))

        def shifted(top, bottom, jb, kb):
            before = top(kb) if jb == 0 else turned(jb - 1, kb, 1, 0)
            after = bottom(kb) if jb == rows_n - 1 else turned(jb + 1, kb, -1, 0)
            low = zero if kb == 0 else turned(jb, kb - 1, 1, 1)
            high = zero if kb == lanes_n - 1 else turned(jb, kb + 1, -1, 1)
            return (
                tile(jb, kb),
                jnp.where(first_row, before, turned(jb, kb, 1, 0)),
                jnp.where(last_row, after, turned(jb, kb, -1, 0)),
                jnp.where(first_lane, low, turned(jb, kb, 1, 1)),
                jnp.where(last_lane, high, turned(jb, kb, -1, 1)),
            )

        return shifted

    g_shift = shifts(lambda *sl: g[(i, *sl)])
    v_shift = [shifts(lambda *sl, c=c: v[(c, i, *sl)]) for c in range(NV)]
    total = ssq
    for kb in range(lanes_n):
        for jb in range(rows_n):
            sl = at(jb, kb)
            gs, gu, gd, gl, gr = g_shift(
                functools.partial(tops, NV), functools.partial(bottoms, NV), jb, kb
            )
            coefs = [gs + gprev(*sl), gs + gnxt(*sl), gs + gu, gs + gd, gs + gl, gs + gr]
            diag = ((coefs[0] + coefs[1]) + (coefs[2] + coefs[3])) + (coefs[4] + coefs[5])
            diffs, owns, res = [], [], []
            for c in range(NV):
                own, up, down, left, right = v_shift[c](
                    functools.partial(tops, c), functools.partial(bottoms, c), jb, kb
                )
                before, after = prev(c, *sl), nxt(c, *sl)
                across = before - after if sign is None else sign * (before - after)
                diffs.append((across, up - down, left - right))
                owns.append(own)
                pulls = (
                    (coefs[0] * before + coefs[1] * after)
                    + (coefs[2] * up + coefs[3] * down)
                ) + (coefs[4] * left + coefs[5] * right)
                res.append(src[(c, i, *sl)] - (diag * own - pulls))
            for c in range(NV):
                r = res[c]
                for d in range(3):
                    for u in range(NV):
                        r = r - jac[(d * NV + u) * NV + c] * diffs[u][d]
                res[c] = r
            if kb == 0:
                code = wall(jb)
                on_wall = first_lane & (code != 1)
                for c in range(NV):
                    t = gs * owns[c]
                    for u in range(NV):
                        t = t + jac[(2 * NV + u) * NV + c] * owns[u]
                    if c == 3:
                        t = jnp.where(code == 0, -t, t)
                    res[c] = res[c] + jnp.where(on_wall, t, zero)
            for c in range(NV):
                total = total + res[c] * res[c]
            for c in range(NV):
                a = owns[c]
                for u in range(NV):
                    a = a + pre[(u, c, i, *sl)] * res[u]
                put(c, sl, a)
    return total


def spread_codes(bc, codes):
    planes, columns = bc.shape
    eye = lax.broadcasted_iota(jnp.int32, (columns, columns), 0) == lax.broadcasted_iota(
        jnp.int32, (columns, columns), 1
    )
    for i in range(planes):
        own = jnp.broadcast_to(bc[i : i + 1, :].astype(F32), (columns, columns))
        column = jnp.sum(jnp.where(eye, own, 0.0), axis=1, keepdims=True)
        codes[i] = jnp.broadcast_to(column, (columns, LANE))


def pick(is_odd, pair, even_ref, idx):
    if len(pair) == 1:
        keep = is_odd if even_ref == 1 else jnp.logical_not(is_odd)
        return jnp.where(keep, pair[0][idx], 0.0)
    return jnp.where(is_odd, pair[1 - even_ref][idx], pair[even_ref][idx])


def make_plane(v, g, src, pre, jac, codes, put, spans, g_spans, span_at=None):
    span_odd = odd("span")

    def rows_of(even_ref, i):
        def get(c, kb):
            pair = g_spans if c == NV else spans
            k = i if c == NV or span_at is None else span_at
            one = pick(span_odd, pair, even_ref, (c, k, slice(None), pl.ds(kb * LANE, LANE)))
            return jnp.broadcast_to(one, (SUB, LANE))

        return get

    def plane(i, ssq, inside=None, halo=None, g_halo=None, sign=None, real=None):
        if halo is None:
            prev = lambda c, *sl: v[(c, i - 1, *sl)]
            nxt = lambda c, *sl: v[(c, i + 1, *sl)]
            gprev = lambda *sl: g[(i - 1, *sl)]
            gnxt = lambda *sl: g[(i + 1, *sl)]
        else:
            prev = lambda c, *sl: v[(c, inside, *sl)]
            nxt = lambda c, *sl: real * halo[(c, *sl)]
            gprev = lambda *sl: g[(inside, *sl)]
            gnxt = lambda *sl: real * g_halo[(NV, *sl)]
        return sweep_plane(
            i, v, prev, nxt, sign, g, gprev, gnxt, rows_of(1, i), rows_of(0, i), src, pre, jac,
            lambda jb: codes[i, pl.ds(jb * SUB, SUB), :],
            functools.partial(put, i),
            ssq,
        )

    return plane


def edge_of(pair, planes):
    low = odd("stream") if pair == 0 else jnp.logical_not(odd("stream"))
    return (
        jnp.where(low, 0, planes - 1),
        jnp.where(low, 1, planes - 2),
        jnp.where(low, -1.0, 1.0).astype(F32),
    )


def no_sum():
    return jnp.zeros((SUB, LANE), F32)


def first_inner(n_span, v, flow, src_hbm, pre_hbm, jac_in, bc, *refs):
    spans = refs[:n_span]
    out, g, src, pre, codes, jac, ssq_out = refs[n_span : n_span + 7]
    span_out, sem = refs[n_span + 7 : -1], refs[-1]
    planes = v.shape[1]

    def load(n, i):
        source, target = ((src_hbm, src), (pre_hbm, pre))[n]
        at = (slice(None),) * (n + 1) + (i,)
        return pltpu.make_async_copy(source.at[at], target.at[at], sem.at[n, i])

    order = [*range(1, planes - 1), 0, planes - 1]
    for i in order:
        load(0, i).start()
        load(1, i).start()
    spread_codes(bc, codes)
    for d in range(3):
        for u in range(NV):
            for c in range(NV):
                jac[(d * NV + u) * NV + c] = jnp.broadcast_to(
                    0.5 * jac_in[d, u : u + 1, c : c + 1], (SUB, LANE)
                )

    def speed_plane(i, carry):
        g[i] = quarter_speed(*[flow[c, i] for c in range(NV)])
        return carry

    lax.fori_loop(0, planes, speed_plane, 0)

    def put(i, c, sl, a):
        out[(c, i, *sl)] = a

    plane = make_plane(v, g, src, pre, jac, codes, put, spans, spans)

    def inner(i, ssq):
        load(0, i).wait()
        load(1, i).wait()
        ssq = plane(i, ssq)
        for c in range(NV):
            span_rows(out, c, i, span_out, i)
        return ssq

    ssq_out[...] = lax.fori_loop(1, planes - 1, inner, no_sum())
    for i in (0, planes - 1):
        load(0, i).wait()
        load(1, i).wait()


def first_edge(pair, n_span, v, g, src, pre, jac, codes, ssq_in, out_in, halo, *refs):
    spans = refs[:n_span]
    out, ssq_out, face = refs[n_span : n_span + 3]
    span_out = refs[n_span + 3 :]
    planes = v.shape[1]

    def put(i, c, sl, a):
        out[(c, i, *sl)] = a
        face[(c, *sl)] = a

    plane = make_plane(v, g, src, pre, jac, codes, put, spans, spans)
    i, inside, sign = edge_of(pair, planes)
    ssq_out[...] = plane(i, ssq_in[...], inside, halo, halo, sign, partner_at(pair))
    if pair == 1:
        for k in range(2):
            at = edge_of(k, planes)[0]
            for c in range(NV):
                span_rows(out, c, at, span_out, k)


def second_inner(n_span, v, g, src, pre, jac, codes, *refs):
    spans, g_spans = refs[:n_span], refs[n_span : 2 * n_span]
    out_hbm, ssq_out, out, sem = refs[2 * n_span :]
    planes = v.shape[1]

    def put(i, c, sl, a):
        out[(c, i, *sl)] = a

    plane = make_plane(v, g, src, pre, jac, codes, put, spans, g_spans)

    def store(i):
        return pltpu.make_async_copy(out.at[:, i], out_hbm.at[:, i], sem.at[i])

    def inner(i, ssq):
        ssq = plane(i, ssq)
        store(i).start()
        return ssq

    ssq_out[...] = lax.fori_loop(1, planes - 1, inner, no_sum())

    def finish(i, carry):
        store(i).wait()
        return carry

    lax.fori_loop(1, planes - 1, finish, 0)


def second_edge(pair, n_span, v, g, src, pre, jac, codes, ssq_in, halo, g_halo, *refs):
    spans, g_spans = refs[:n_span], refs[n_span : 2 * n_span]
    refs = refs[2 * n_span :]
    planes = v.shape[1]
    i, inside, sign = edge_of(pair, planes)
    ssq_before = refs[0] if pair == 1 else None
    out, ssq_out = refs[-2:]

    def put(i, c, sl, a):
        out[(c, *sl)] = a

    plane = make_plane(v, g, src, pre, jac, codes, put, spans, g_spans, pair)
    ssq = plane(i, ssq_in[...], inside, halo, g_halo, sign, partner_at(pair))
    if pair == 0:
        ssq_out[...] = ssq
        return
    lane = lax.broadcasted_iota(jnp.int32, ssq_out.shape, 1)
    before, now = jnp.sum(ssq_before[...]), jnp.sum(ssq)
    ssq_out[...] = jnp.where(lane == 0, before, jnp.where(lane == 1, now, 0.0))


def tail_kernel(cells_all, sums, edge_a, edge_b, result_in, result, rms, sem):
    ends = face_planes(result.shape[1])
    stores = [
        pltpu.make_async_copy(edge, result.at[:, end], sem.at[k])
        for k, (edge, end) in enumerate(zip((edge_a, edge_b), ends))
    ]
    for store in stores:
        store.start()
    total = jnp.sum(sums[...], axis=0, keepdims=True)
    rms[...] = jnp.sqrt(total / cells_all)[:, : rms.shape[1]]
    for store in stores:
        store.wait()


def pairs(count, offset):
    both = []
    for i in range(offset, count - 1, 2):
        both += [(i, i + 1), (i + 1, i)]
    return both


def exchange_pair(face, axis, pair):
    return lax.ppermute(face, axis, pairs(lax.axis_size(axis), pair))


def exchange_stream(face, pair):
    streams, spans = lax.axis_size("stream"), lax.axis_size("span")
    along = dict(pairs(streams, pair))
    across = dict(pairs(spans, 0))
    moves = []
    for i in range(streams):
        for j in range(spans):
            if i in along:
                moves.append((i * spans + j, along[i] * spans + j))
            elif j in across:
                moves.append((i * spans + j, i * spans + across[j]))
    return lax.ppermute(face, ("stream", "span"), moves)


def partner_at(pair):
    at, count = lax.axis_index("stream"), lax.axis_size("stream")
    is_odd = odd("stream")
    other = jnp.where(is_odd, at - 1, at + 1) if pair == 0 else jnp.where(is_odd, at + 1, at - 1)
    return jnp.where((other >= 0) & (other < count), 1.0, 0.0).astype(F32)


def exchange(faces, axis):
    return [exchange_pair(face, axis, pair) for pair, face in enumerate(faces)]


def per_device(adjoint_start, source, flow_state, precond, flux_jac, bc_codes):
    _, planes, rows, lanes = adjoint_start.shape
    n_stream, n_span_all = lax.axis_size("stream"), lax.axis_size("span")
    n_devices = n_stream * n_span_all
    n_span = 1 if n_span_all <= 2 else 2
    cells = planes * rows * lanes
    field = shape(NV, planes, rows, lanes)
    tile = shape(SUB, LANE)
    dma = pltpu.SemaphoreType.DMA
    inner_cost = cost(3000 * cells, 4 * cells, 42 * 4 * cells)
    edge_cost = cost(100 * cells, 0, 42 * cells)

    v, flow, *faces = pl.pallas_call(
        functools.partial(pack_kernel, n_span),
        out_shape=[field, field]
        + [shape(NV + 1, rows, lanes)] * 2
        + [shape(NV + 1, planes, 1, lanes)] * n_span,
        in_specs=[HBM] * 2,
        out_specs=[VMEM] * (4 + n_span),
        scratch_shapes=[pltpu.VMEM((NV, planes, 1, lanes), F32)] * n_span + [dma((2, 3))],
        cost_estimate=cost(cells, 0, 8 * cells),
        compiler_params=params(),
        name="pack",
    )(*hold(adjoint_start, flow_state, space=pltpu.HBM))
    streams = []
    for pair, face in enumerate(faces[:2]):
        streams.append(exchange_stream(face, pair))
    spans = exchange(faces[2:], "span")

    adjoint, g, src, pre, codes, jac, ssq, *rows_out = pl.pallas_call(
        functools.partial(first_inner, n_span),
        out_shape=[
            field, shape(planes, rows, lanes), field,
            shape(NV, NV, planes, rows, lanes), shape(planes, rows, LANE), shape(3 * NV * NV, SUB, LANE), tile,
        ]
        + [shape(NV, planes, 1, lanes)] * n_span,
        in_specs=[VMEM] * 2 + [HBM] * 2 + [VMEM] * (2 + n_span),
        out_specs=[VMEM] * (7 + n_span),
        scratch_shapes=[dma((2, planes))],
        cost_estimate=inner_cost,
        compiler_params=params(),
        name="first_inner",
    )(
        *hold(v, flow), *hold(source, precond, space=pltpu.HBM), *hold(flux_jac, bc_codes, *spans)
    )
    spans_inner = exchange(rows_out, "span")

    streams_next = []
    for pair in range(2):
        n_out = n_span if pair == 1 else 0
        first_edge_call = pl.pallas_call(
            functools.partial(first_edge, pair, n_span),
            out_shape=[field, tile, shape(NV, rows, lanes)] + [shape(NV, 2, 1, lanes)] * n_out,
            in_specs=[VMEM] * 5 + [VMEM] * (4 + n_span),
            out_specs=[VMEM] * (3 + n_out),
            input_output_aliases={7: 0},
            cost_estimate=edge_cost,
            compiler_params=params(),
        )
        adjoint, ssq, face, *rows_out = first_edge_call(
            *hold(v, g, src, pre, jac, codes, ssq, adjoint, streams[pair], *spans)
        )
        streams_next.append(exchange_stream(face, pair))
    ssq_first = ssq
    spans_edge = exchange(rows_out, "span")

    result, ssq = pl.pallas_call(
        functools.partial(second_inner, n_span),
        out_shape=[pltpu.HBM(adjoint_start.shape, F32), tile],
        in_specs=[VMEM] * 5 + [VMEM] * (1 + 2 * n_span),
        out_specs=[HBM, VMEM],
        scratch_shapes=[field, dma((planes,))],
        cost_estimate=inner_cost,
        compiler_params=params(),
        name="second_inner",
    )(*hold(adjoint, g, src, pre, jac), *hold(codes, *spans_inner, *spans))

    face = shape(NV, rows, lanes)
    edges = []
    for pair in range(2):
        edge, ssq = pl.pallas_call(
            functools.partial(second_edge, pair, n_span),
            out_shape=[face, shape(n_devices, LANE) if pair else tile],
            in_specs=[VMEM] * (9 + 2 * n_span + pair),
            out_specs=[VMEM] * 2,
            cost_estimate=edge_cost,
            compiler_params=params(),
        )(
            *hold(adjoint, g, src, pre, jac, codes, ssq, streams_next[pair], streams[pair]),
            *hold(*spans_edge, *spans, *([ssq_first] * pair)),
        )
        edges.append(edge)
    sums = lax.all_to_all(ssq, ("stream", "span"), 0, 0, tiled=True)
    result, rms = pl.pallas_call(
        functools.partial(tail_kernel, float(NV * cells * n_devices)),
        out_shape=[pltpu.HBM(adjoint_start.shape, F32), jax.ShapeDtypeStruct((1, 2), F32)],
        in_specs=[VMEM] * 3 + [HBM],
        out_specs=[HBM, VMEM],
        scratch_shapes=[dma((2,))],
        input_output_aliases={3: 0},
        compiler_params=params(),
        name="tail",
    )(*hold(sums, *edges), *hold(result, space=pltpu.HBM))
    return (result, rms.reshape(2))


def solution(mesh):
    in_specs = (
        P(None, "stream", "span", None),
        P(None, "stream", "span", None),
        P(None, "stream", "span", None),
        P(None, None, "stream", "span", None),
        P(),
        P("stream", "span"),
    )
    out_specs = (P(None, "stream", "span", None), P())

    return jax.shard_map(
        per_device, mesh=mesh, in_specs=in_specs, out_specs=out_specs, check_vma=False
    )
```

time: 44.6 us -> 38.6 us (0.87)
  starting transfers between devices: 10.9 us -> 6.73 us
  waiting for transfers between devices: 1.28 us -> 5.17 us
  Pallas kernels: 16.4 us -> 12.9 us
  blocking collectives: 14.6 us -> 12.9 us
  other arithmetic: 0.58 us -> 0 us
    ppermute x6 -> x7, starting transfers between devices: 10.9 us -> 6.73 us  [the longest x4 5.65 us: exchange_stream(): return lax.ppermute(face, ('stream', 'span'), moves)]
    ppermute x6 -> x7, waiting for transfers between devices: 1.28 us -> 5.17 us  [the longest x4 3.18 us: exchange_stream(): return lax.ppermute(face, ('stream', 'span'), moves)]
    all_to_all x1, blocking collectives: 14.6 us -> 12.9 us  [per_device(): sums = lax.all_to_all(ssq, ('stream', 'span'), 0, 0, tiled=True)]
    pallas_call x1, Pallas kernels: 4.73 us -> 3.46 us  [per_device(): pl.pallas_call(functools.partial(second_inner, n_span), out_shape=[pltpu....]
    pallas_call x1, Pallas kernels: 5.35 us -> 4.16 us  [per_device(): pl.pallas_call(functools.partial(first_inner, n_span), out_shape=[field,...]
    pallas_call x2 -> x5, Pallas kernels: 4.42 us -> 3.3 us  [the longest x1 1.26 us: per_device(): pl.pallas_call(functools.partial(tail_kernel, float(NV * cells * n_device...]
    sqrt x1 -> x0, other arithmetic: 0.52 us -> none  [per_device(): return (result, jnp.sqrt(jnp.sum(sums, axis=0)[:2] / cells_all))]
  transfers between devices with their start and end apart: 6 -> 7, of which waited for: 1 -> 4; matrix products, arithmetic and copies ran while one was open for 0% -> 0% of each run, Pallas kernels for 23% -> 24%
where the time goes in v2:
time: 38.6 us; the launch traced here: 38.5 us
  Pallas kernels  12.9 us (33%)
  blocking collectives  12.9 us (33%)
  starting transfers between devices  6.73 us (17%)
  waiting for transfers between devices  5.17 us (13%)
  between operations  0.72 us (2%)
    all_to_all x1, blocking collectives, per_device(): sums = lax.all_to_all(ssq, ('stream', 'span'), 0, 0, tiled=True)  12.9 us
    ppermute x4, starting transfers between devices, exchange_stream(): return lax.ppermute(face, ('stream', 'span'), moves)  5.65 us
    pallas_call x1, Pallas kernels, per_device(): pl.pallas_call(functools.partial(first_inner, n_span), out_shape=[field,...  4.16 us
    pallas_call x1, Pallas kernels, per_device(): pl.pallas_call(functools.partial(second_inner, n_span), out_shape=[pltpu....  3.46 us
    ppermute x4, waiting for transfers between devices, exchange_stream(): return lax.ppermute(face, ('stream', 'span'), moves)  3.18 us
    pallas_call x1, Pallas kernels, per_device(): pl.pallas_call(functools.partial(pack_kernel, n_span), out_shape=[field,...  1.99 us
    ppermute x3, waiting for transfers between devices, exchange_pair(): return lax.ppermute(face, axis, pairs(lax.axis_size(axis), pair))  1.99 us
    pallas_call x1, Pallas kernels, per_device(): pl.pallas_call(functools.partial(tail_kernel, float(NV * cells * n_device...  1.26 us
  transfers between devices with their start and end apart: 7, of which 4 were waited for; matrix products, arithmetic and copies ran while one was open for 0% of the time, Pallas kernels for 24%

profile of v2, /device:TPU:0, one launch (start us, length us, event | category | flops | bytes accessed | tf_op | source)
XLA Modules:
  0.0 38.5 jit_solution(10439961839567126590)
XLA Ops:
  0.7 2.0 %pack.1 = (f32[5,8,16,512]{3,2,1,0:T(8,128)S(1)}, f32[5,8,16,512]{3,2,1,0:T(8,128)S(1)}, f32[6,16,512]{2,1,0:T(8,128)S(1)}, f32[6,16,512]{2,1,0:T(8,128)S(1)}, f32[6,8,1,512]{3,2,1,0:T(1,128)S(1)}) custom-call(f32[5,8,16,512]{3,2,1,0:T(8,128)} %v_hbm.1, f32[5,8,16,512]{3,2,1,0:T(8,128)} %flow_hbm.1), custom_call_target="tpu_custom_call" | custom-call | flops 65536 | bytes 524288 | tf_op jit(solution)/shard_map/pack/pallas_call | solution.py:419
  2.7 3.0 %collective-permute-start.1 = (f32[6,16,512]{2,1,0:T(8,128)S(1)}, f32[6,16,512]{2,1,0:T(8,128)S(1)}, u32[]{:S(2)}, u32[]{:S(2)}) collective-permute-start(f32[6,16,512]{2,1,0:T(8,128)S(1)} %get-tuple-element.40), channel_id=1, source_target_pairs={{0,2},{1,3},{2,0},{3,1},{4,6},{5,7},{6,4},{7,5},{8,10},{9,11},{10,... | collective-permute-start | bytes 589832 | tf_op jit(solution)/shard_map/ppermute | solution.py:393
  5.7 0.0 collective-permute-start.2
  5.7 0.5 %collective-permute-start = (f32[6,8,1,512]{3,2,1,0:T(1,128)S(1)}, f32[6,8,1,512]{3,2,1,0:T(1,128)S(1)}, u32[]{:S(2)}, u32[]{:S(2)}) collective-permute-start(f32[6,8,1,512]{3,2,1,0:T(1,128)S(1)} %get-tuple-element.32), channel_id=1, source_target_pairs={{0,1},{1,0},{2,3},{3,2},{4,5},{5,4},{6,7},{7,6},{8,9},{9,8},{10,11... | collective-permute-start | bytes 294920 | tf_op jit(solution)/shard_map/ppermute | solution.py:379
  6.2 0.0 copy-done.1
  6.2 1.1 %collective-permute-done.refs_0_.refs_1_ = f32[6,8,1,512]{3,2,1,0:T(1,128)S(1)} collective-permute-done((f32[6,8,1,512]{3,2,1,0:T(1,128)S(1)}, f32[6,8,1,512]{3,2,1,0:T(1,128)S(1)}, u32[]{:S(2)}, u32[]{:S(2)}) %collective-permute-start) | collective-permute-done | bytes 98336 | tf_op jit(solution)/shard_map/ppermute | solution.py:379
  7.3 4.2 %first_inner.1 = (f32[5,8,16,512]{3,2,1,0:T(8,128)S(1)}, f32[8,16,512]{2,1,0:T(8,128)S(1)}, f32[5,8,16,512]{3,2,1,0:T(8,128)S(1)}, f32[5,5,8,16,512]{4,3,2,1,0:T...) custom-call(f32[5,8,16,512]{3,2,1,0:T(8,128)S(1)} %get-tuple-element, ...), custom_call_target="tpu_custom_call" | custom-call | flops 196608000 | bytes 11010048 | tf_op jit(solution)/shard_map/first_inner/pallas_call | solution.py:436
  11.4 2.6 %collective-permute-done.1.halo.g_halo = f32[6,16,512]{2,1,0:T(8,128)S(1)} collective-permute-done((f32[6,16,512]{2,1,0:T(8,128)S(1)}, f32[6,16,512]{2,1,0:T(8,128)S(1)}, u32[]{:S(2)}, u32[]{:S(2)}) %collective-permute-start.1) | collective-permute-done | bytes 196640 | tf_op jit(solution)/shard_map/ppermute | solution.py:393
  14.1 0.5 %shard_map.77 = (f32[5,8,16,512]{3,2,1,0:T(8,128)S(1)}, f32[8,128]{1,0:T(8,128)S(1)}, f32[5,16,512]{2,1,0:T(8,128)S(1)}) custom-call(f32[5,8,16,512]{3,2,1,0:T(8,128)S(1)} %get-tuple-element.30.v, f32[8,16,512]{2,1,0:T(8,128)S(1)} %get-tuple-element.33.g, f32[5,8,16,512]{3,2,1,0:T(8,128)S(1)} %get-tuple-element.34.src, ...), custom_call_target="tpu_custom_call", output_to_operand_aliasing={{0}: (7, {})} | custom-call | flops 6553600 | bytes 2752512 | tf_op jit(solution)/shard_map/pallas_call | solution.py:466
  14.5 2.5 %collective-permute-start.4 = (f32[5,16,512]{2,1,0:T(8,128)S(1)}, f32[5,16,512]{2,1,0:T(8,128)S(1)}, u32[]{:S(2)}, u32[]{:S(2)}) collective-permute-start(f32[5,16,512]{2,1,0:T(8,128)S(1)} %get-tuple-element.47), channel_id=1, source_target_pairs={{0,2},{1,3},{2,0},{3,1},{4,6},{5,7},{6,4},{7,5},{8,10},{9,11},{10,... | collective-permute-start | bytes 491528 | tf_op jit(solution)/shard_map/ppermute | solution.py:393
  17.1 0.0 collective-permute-done.2.halo.g_halo
  17.1 0.5 %shard_map.78 = (f32[5,8,16,512]{3,2,1,0:T(8,128)S(1)}, f32[8,128]{1,0:T(8,128)S(1)}, f32[5,16,512]{2,1,0:T(8,128)S(1)}, f32[5,2,1,512]{3,2,1,0:T(1,128)S(1)}) custom-call(f32[5,8,16,512]{3,2,1,0:T(8,128)S(1)} %get-tuple-element.30.v, f32[8,16,512]{2,1,0:T(8,128)S(1)} %get-tuple-element.33.g, ...), custom_call_target="tpu_custom_call", output_to_operand_aliasing={{0}: (7, {})} | custom-call | flops 6553600 | bytes 2752512 | tf_op jit(solution)/shard_map/pallas_call | solution.py:466
  17.6 0.1 collective-permute-start.6
  17.7 0.5 %collective-permute-start.3 = (f32[5,8,1,512]{3,2,1,0:T(1,128)S(1)}, f32[5,8,1,512]{3,2,1,0:T(1,128)S(1)}, u32[]{:S(2)}, u32[]{:S(2)}) collective-permute-start(f32[5,8,1,512]{3,2,1,0:T(1,128)S(1)} %get-tuple-element.45), channel_id=1, source_target_pairs={{0,1},{1,0},{2,3},{3,2},{4,5},{5,4},{6,7},{7,6},{8,9},{9,8},{10,11... | collective-permute-start | bytes 245768 | tf_op jit(solution)/shard_map/ppermute | solution.py:379
  18.1 0.1 collective-permute-start.5
  18.2 0.9 %collective-permute-done.3.refs_0_ = f32[5,8,1,512]{3,2,1,0:T(1,128)S(1)} collective-permute-done((f32[5,8,1,512]{3,2,1,0:T(1,128)S(1)}, f32[5,8,1,512]{3,2,1,0:T(1,128)S(1)}, u32[]{:S(2)}, u32[]{:S(2)}) %collective-permute-start.3) | collective-permute-done | bytes 81952 | tf_op jit(solution)/shard_map/ppermute | solution.py:379
  19.1 3.5 %second_inner.1 = (f32[5,8,16,512]{3,2,1,0:T(8,128)}, f32[8,128]{1,0:T(8,128)S(1)}) custom-call(f32[5,8,16,512]{3,2,1,0:T(8,128)S(1)} %get-tuple-element.44.v, f32[8,16,512]{2,1,0:T(8,128)S(1)} %get-tuple-element.33.g, f32[5,8,16,512]{3,2,1,0:T(8,128)S(1)} %get-tuple-element.34.src, f32[5,5,8,16,512]{4,3,2,1,0:T(8,128)S(1)} %get-tuple-element.35.pre, ...), custom_call_target="tpu_custom_call" | custom-call | flops 196608000 | bytes 11010048 | tf_op jit(solution)/shard_map/second_inner/pallas_call | solution.py:473
  22.6 0.0 collective-permute-done.5.refs_0_
  22.6 0.6 %collective-permute-done.4.halo = f32[5,16,512]{2,1,0:T(8,128)S(1)} collective-permute-done((f32[5,16,512]{2,1,0:T(8,128)S(1)}, f32[5,16,512]{2,1,0:T(8,128)S(1)}, u32[]{:S(2)}, u32[]{:S(2)}) %collective-permute-start.4) | collective-permute-done | bytes 163872 | tf_op jit(solution)/shard_map/ppermute | solution.py:393
  23.2 0.5 %shard_map.79 = (f32[5,16,512]{2,1,0:T(8,128)S(1)}, f32[8,128]{1,0:T(8,128)S(1)}) custom-call(f32[5,8,16,512]{3,2,1,0:T(8,128)S(1)} %get-tuple-element.44.v, f32[8,16,512]{2,1,0:T(8,128)S(1)} %get-tuple-element.33.g, f32[5,8,16,512]{3,2,1,0:T(8,128)S(1)} %get-tuple-element.34.src, f32[5,5,8,16,512]{4,3,2,1,0:T(8,128)S(1)} %get-tuple-element.35.pre, ...), custom_call_target="tpu_custom_call" | custom-call | flops 6553600 | bytes 2752512 | tf_op jit(solution)/shard_map/pallas_call | solution.py:487
  23.7 0.0 collective-permute-done.6.halo
  23.7 0.6 %shard_map.80 = (f32[5,16,512]{2,1,0:T(8,128)S(1)}, f32[32,128]{1,0:T(8,128)S(1)}) custom-call(f32[5,8,16,512]{3,2,1,0:T(8,128)S(1)} %get-tuple-element.44.v, f32[8,16,512]{2,1,0:T(8,128)S(1)} %get-tuple-element.33.g, f32[5,8,16,512]{3,2,1,0:T(8,128)S(1)} %get-tuple-element.34.src, f32[5,5,8,16,512]{4,3,2,1,0:T(8,128)S(1)} %get-tuple-element.35.pre, ...), custom_call_target="tpu_custom_call" | custom-call | flops 6553600 | bytes 2752512 | tf_op jit(solution)/shard_map/pallas_call | solution.py:487
  24.3 12.9 %all_to_all.11 = f32[32,1,128]{2,1,0:T(1,128)S(1)} all-to-all(f32[32,1,128]{2,1,0:T(1,128)S(1)} %bitcast.6), channel_id=1, replica_groups=mesh['stream'=16,'span'=2] {'stream','span'}, dimensions={0} | all-to-all | bytes 32768 | tf_op jit(solution)/shard_map/all_to_all | solution.py:499
  37.2 1.3 %tail.1 = (f32[5,8,16,512]{3,2,1,0:T(8,128)}, f32[1,2]{1,0:T(1,128)}) custom-call(f32[32,128]{1,0:T(8,128)S(1)} %bitcast.5, f32[5,16,512]{2,1,0:T(8,128)S(1)} %get-tuple-element.53.edge_a, f32[5,16,512]{2,1,0:T(8,128)S(1)} %get-tuple-element.54.edge_b, f32[5,8,16,512]{3,2,1,0:T(8,128)} %get-tuple-element.55.result_in), custom_call_target="tpu_custom_call", output_to_operand_aliasing={{0}: (3, {})} | custom-call | tf_op jit(solution)/shard_map/tail/pallas_call | solution.py:500
  (4 shorter events, 0.0 us)
Async XLA Ops:
  0.6 5.6 %copy-start.1 = (f32[3,5,5]{2,0,1:T(4,128)S(1)}, f32[3,5,5]{2,0,1:T(4,128)}, u32[]{:S(2)}) copy-start(f32[3,5,5]{2,0,1:T(4,128)} %param.10) | copy-start | bytes 904
  0.6 6.6 %copy-start = (s32[8,16]{1,0:T(8,128)S(1)}, s32[8,16]{1,0:T(8,128)}, u32[]{:S(2)}) copy-start(s32[8,16]{1,0:T(8,128)} %bc.1) | copy-start | bytes 1540
  2.7 11.4 %collective-permute-start.1 = (f32[6,16,512]{2,1,0:T(8,128)S(1)}, f32[6,16,512]{2,1,0:T(8,128)S(1)}, u32[]{:S(2)}, u32[]{:S(2)}) collective-permute-start(f32[6,16,512]{2,1,0:T(8,128)S(1)} %get-tuple-element.40), channel_id=1, source_target_pairs={{0,2},{1,3},{2,0},{3,1},{4,6},{5,7},{6,4},{7,5},{8,10},{9,11},{10,... | collective-permute-start | bytes 589832 | tf_op jit(solution)/shard_map/ppermute | solution.py:393
  5.7 11.4 %collective-permute-start.2 = (f32[6,16,512]{2,1,0:T(8,128)S(1)}, f32[6,16,512]{2,1,0:T(8,128)S(1)}, u32[]{:S(2)}, u32[]{:S(2)}) collective-permute-start(f32[6,16,512]{2,1,0:T(8,128)S(1)} %get-tuple-element.43), channel_id=1, source_target_pairs={{0,1},{1,0},{2,4},{3,5},{4,2},{5,3},{6,8},{7,9},{8,6},{9,7},{10,12... | collective-permute-start | bytes 589832 | tf_op jit(solution)/shard_map/ppermute | solution.py:393
  5.7 1.6 %collective-permute-start = (f32[6,8,1,512]{3,2,1,0:T(1,128)S(1)}, f32[6,8,1,512]{3,2,1,0:T(1,128)S(1)}, u32[]{:S(2)}, u32[]{:S(2)}) collective-permute-start(f32[6,8,1,512]{3,2,1,0:T(1,128)S(1)} %get-tuple-element.32), channel_id=1, source_target_pairs={{0,1},{1,0},{2,3},{3,2},{4,5},{5,4},{6,7},{7,6},{8,9},{9,8},{10,11... | collective-permute-start | bytes 294920 | tf_op jit(solution)/shard_map/ppermute | solution.py:379
  14.5 8.7 %collective-permute-start.4 = (f32[5,16,512]{2,1,0:T(8,128)S(1)}, f32[5,16,512]{2,1,0:T(8,128)S(1)}, u32[]{:S(2)}, u32[]{:S(2)}) collective-permute-start(f32[5,16,512]{2,1,0:T(8,128)S(1)} %get-tuple-element.47), channel_id=1, source_target_pairs={{0,2},{1,3},{2,0},{3,1},{4,6},{5,7},{6,4},{7,5},{8,10},{9,11},{10,... | collective-permute-start | bytes 491528 | tf_op jit(solution)/shard_map/ppermute | solution.py:393
  17.6 6.1 %collective-permute-start.6 = (f32[5,16,512]{2,1,0:T(8,128)S(1)}, f32[5,16,512]{2,1,0:T(8,128)S(1)}, u32[]{:S(2)}, u32[]{:S(2)}) collective-permute-start(f32[5,16,512]{2,1,0:T(8,128)S(1)} %get-tuple-element.50), channel_id=1, source_target_pairs={{0,1},{1,0},{2,4},{3,5},{4,2},{5,3},{6,8},{7,9},{8,6},{9,7},{10,12... | collective-permute-start | bytes 491528 | tf_op jit(solution)/shard_map/ppermute | solution.py:393
  17.7 1.5 %collective-permute-start.3 = (f32[5,8,1,512]{3,2,1,0:T(1,128)S(1)}, f32[5,8,1,512]{3,2,1,0:T(1,128)S(1)}, u32[]{:S(2)}, u32[]{:S(2)}) collective-permute-start(f32[5,8,1,512]{3,2,1,0:T(1,128)S(1)} %get-tuple-element.45), channel_id=1, source_target_pairs={{0,1},{1,0},{2,3},{3,2},{4,5},{5,4},{6,7},{7,6},{8,9},{9,8},{10,11... | collective-permute-start | bytes 245768 | tf_op jit(solution)/shard_map/ppermute | solution.py:379
  18.1 4.5 %collective-permute-start.5 = (f32[5,2,1,512]{3,2,1,0:T(1,128)S(1)}, f32[5,2,1,512]{3,2,1,0:T(1,128)S(1)}, u32[]{:S(2)}, u32[]{:S(2)}) collective-permute-start(f32[5,2,1,512]{3,2,1,0:T(1,128)S(1)} %get-tuple-element.48), channel_id=1, source_target_pairs={{0,1},{1,0},{2,3},{3,2},{4,5},{5,4},{6,7},{7,6},{8,9},{9,8},{10,11... | collective-permute-start | bytes 61448 | tf_op jit(solution)/shard_map/ppermute | solution.py:379

commit v3 on v2

--- a/solution.py
+++ b/solution.py
@@ -9,8 +9,10 @@
 
 
 NV = 5
+SWEEPS = 2
 SUB, LANE = 8, 128
 F32 = jnp.float32
+ORDER = (1, 0)
 VMEM = pl.BlockSpec(memory_space=pltpu.VMEM)
 HBM = pl.BlockSpec(memory_space=pltpu.HBM)
 
@@ -49,43 +51,76 @@
 
 def span_rows(field, c, i, out_refs, k):
     is_odd = odd("span")
-    last = field.shape[2] - 1
-    head = field[c, i, 0:1, :]
-    tail = field[c, i, last : last + 1, :]
-    out_refs[0][c, k] = jnp.where(is_odd, head, tail)
+    last = field.shape[-2] - 1
+    at = (i,) if c is None else (c, i)
+    to = (k,) if c is None else (c, k)
+    head = field[(*at, slice(0, 1))]
+    tail = field[(*at, slice(last, last + 1))]
+    out_refs[0][to] = jnp.where(is_odd, head, tail)
     if len(out_refs) > 1:
-        out_refs[1][c, k] = jnp.where(is_odd, tail, head)
-
-
-def pack_kernel(n_span, v_hbm, flow_hbm, v, flow, fa, fb, *rest):
-    spans, rows, sem = rest[:n_span], rest[n_span:-1], rest[-1]
+        out_refs[1][to] = jnp.where(is_odd, tail, head)
+
+
+def pack_kernel(v_hbm, flow_hbm, fa, fb, face_in, sem):
+    ends = face_planes(v_hbm.shape[1])
+    faces = (fa, fb)
+    fields = (flow_hbm, v_hbm)
+    loads = [
+        [
+            pltpu.make_async_copy(field.at[:, ends[pair]], face_in.at[pair, n], sem.at[pair, n])
+            for n, field in enumerate(fields)
+        ]
+        for pair in range(2)
+    ]
+    for pair in ORDER:
+        for load in loads[pair]:
+            load.start()
+    for pair in ORDER:
+        for load in loads[pair]:
+            load.wait()
+        faces[pair][NV] = quarter_speed(*[face_in[pair, 0, c] for c in range(NV)])
+        for c in range(NV):
+            faces[pair][c] = face_in[pair, 1, c]
+
+
+def plane_loads(src_hbm, pre_hbm, src, pre, sem, i):
+    return (
+        pltpu.make_async_copy(src_hbm.at[:, i], src.at[:, i], sem.at[0, i]),
+        pltpu.make_async_copy(pre_hbm.at[:, :, i], pre.at[:, :, i], sem.at[1, i]),
+    )
+
+
+def load_kernel(n_span, v_hbm, flow_hbm, src_hbm, pre_hbm, jac_in, bc, *refs):
+    v, g, src, pre, codes, jac = refs[:6]
+    spans, (flow, sem) = refs[6 : 6 + n_span], refs[6 + n_span :]
     planes = v.shape[1]
-
-    def loads(at, k):
-        return [
-            pltpu.make_async_copy(src.at[:, at], dst.at[:, at], sem.at[n, k])
-            for n, (src, dst) in enumerate(((flow_hbm, flow), (v_hbm, v)))
+    loads = [
+        [
+            pltpu.make_async_copy(source.at[:, i], target.at[:, i], sem.at[n, i])
+            for n, (source, target) in enumerate(((flow_hbm, flow), (v_hbm, v)))
         ]
-
-    ends = face_planes(planes)
-    groups = [loads(ends[0], 0), loads(ends[1], 1), loads(pl.ds(1, planes - 2), 2)]
-    for group in groups:
-        for load in group:
-            load.start()
-    for group, face, plane in zip(groups, (fa, fb), ends):
-        for load in group:
+        for i in range(planes)
+    ]
+    early = plane_loads(src_hbm, pre_hbm, src, pre, sem.at[pl.ds(2, 2)], 1)
+    for load in [load for pair in loads for load in pair] + [*early]:
+        load.start()
+    spread_codes(bc, codes)
+    for d in range(3):
+        for u in range(NV):
+            for c in range(NV):
+                jac[(d * NV + u) * NV + c] = jnp.broadcast_to(
+                    0.5 * jac_in[d, u : u + 1, c : c + 1], (SUB, LANE)
+                )
+    for i in range(planes):
+        for load in loads[i]:
             load.wait()
-        face[NV] = quarter_speed(*[flow[c, plane] for c in range(NV)])
+        g[i] = quarter_speed(*[flow[c, i] for c in range(NV)])
         for c in range(NV):
-            face[c] = v[c, plane]
-    for load in groups[2]:
+            span_rows(v, c, i, spans, i)
+    for i in range(planes):
+        span_rows(g, None, i, [span.at[NV] for span in spans], i)
+    for load in early:
         load.wait()
-    for c in range(NV):
-        for i in range(planes):
-            span_rows(v, c, i, spans, i)
-            span_rows(flow, c, i, rows, i)
-    for ref, row in zip(spans, rows):
-        ref[NV] = quarter_speed(*[row[c] for c in range(NV)])
 
 
 def sweep_plane(i, v, prev, nxt, sign, g, gprev, gnxt, tops, bottoms, src, pre, jac, wall, put, ssq):
@@ -238,34 +273,18 @@
     return jnp.zeros((SUB, LANE), F32)
 
 
-def first_inner(n_span, v, flow, src_hbm, pre_hbm, jac_in, bc, *refs):
+def first_inner(n_span, part, v, g, jac, codes, src_hbm, pre_hbm, src_in, pre_in, *refs):
     spans = refs[:n_span]
-    out, g, src, pre, codes, jac, ssq_out = refs[n_span : n_span + 7]
-    span_out, sem = refs[n_span + 7 : -1], refs[-1]
+    out, src, pre, ssq_out, sem = refs[n_span:]
     planes = v.shape[1]
 
-    def load(n, i):
-        source, target = ((src_hbm, src), (pre_hbm, pre))[n]
-        at = (slice(None),) * (n + 1) + (i,)
-        return pltpu.make_async_copy(source.at[at], target.at[at], sem.at[n, i])
-
-    order = [*range(1, planes - 1), 0, planes - 1]
-    for i in order:
-        load(0, i).start()
-        load(1, i).start()
-    spread_codes(bc, codes)
-    for d in range(3):
-        for u in range(NV):
-            for c in range(NV):
-                jac[(d * NV + u) * NV + c] = jnp.broadcast_to(
-                    0.5 * jac_in[d, u : u + 1, c : c + 1], (SUB, LANE)
-                )
-
-    def speed_plane(i, carry):
-        g[i] = quarter_speed(*[flow[c, i] for c in range(NV)])
-        return carry
-
-    lax.fori_loop(0, planes, speed_plane, 0)
+    def loads(i):
+        return plane_loads(src_hbm, pre_hbm, src, pre, sem, i)
+
+    late = [*range(2, planes - 1), 0, planes - 1]
+    for i in late:
+        for load in loads(i):
+            load.start()
 
     def put(i, c, sl, a):
         out[(c, i, *sl)] = a
@@ -273,17 +292,33 @@
     plane = make_plane(v, g, src, pre, jac, codes, put, spans, spans)
 
     def inner(i, ssq):
-        load(0, i).wait()
-        load(1, i).wait()
-        ssq = plane(i, ssq)
+        @pl.when(i > 1)
+        def _():
+            for load in loads(i):
+                load.wait()
+
+        return plane(i, ssq)
+
+    ssq_out[...] = lax.fori_loop(1, part, inner, no_sum())
+    for i in late[part - 2 :]:
+        for load in loads(i):
+            load.wait()
+
+
+def first_rest(n_span, part, v, g, src, pre, jac, codes, ssq_in, out_in, *refs):
+    spans = refs[:n_span]
+    out, ssq_out = refs[n_span : n_span + 2]
+    span_out = refs[n_span + 2 :]
+    planes = v.shape[1]
+
+    def put(i, c, sl, a):
+        out[(c, i, *sl)] = a
+
+    plane = make_plane(v, g, src, pre, jac, codes, put, spans, spans)
+    ssq_out[...] = lax.fori_loop(part, planes - 1, plane, ssq_in[...])
+    for i in range(1, planes - 1):
         for c in range(NV):
             span_rows(out, c, i, span_out, i)
-        return ssq
-
-    ssq_out[...] = lax.fori_loop(1, planes - 1, inner, no_sum())
-    for i in (0, planes - 1):
-        load(0, i).wait()
-        load(1, i).wait()
 
 
 def first_edge(pair, n_span, v, g, src, pre, jac, codes, ssq_in, out_in, halo, *refs):
@@ -299,7 +334,7 @@
     plane = make_plane(v, g, src, pre, jac, codes, put, spans, spans)
     i, inside, sign = edge_of(pair, planes)
     ssq_out[...] = plane(i, ssq_in[...], inside, halo, halo, sign, partner_at(pair))
-    if pair == 1:
+    if pair == ORDER[1]:
         for k in range(2):
             at = edge_of(k, planes)[0]
             for c in range(NV):
@@ -338,7 +373,7 @@
     refs = refs[2 * n_span :]
     planes = v.shape[1]
     i, inside, sign = edge_of(pair, planes)
-    ssq_before = refs[0] if pair == 1 else None
+    last = pair == ORDER[1]
     out, ssq_out = refs[-2:]
 
     def put(i, c, sl, a):
@@ -346,24 +381,26 @@
 
     plane = make_plane(v, g, src, pre, jac, codes, put, spans, g_spans, pair)
     ssq = plane(i, ssq_in[...], inside, halo, g_halo, sign, partner_at(pair))
-    if pair == 0:
+    if not last:
         ssq_out[...] = ssq
         return
     lane = lax.broadcasted_iota(jnp.int32, ssq_out.shape, 1)
-    before, now = jnp.sum(ssq_before[...]), jnp.sum(ssq)
+    before, now = jnp.sum(refs[0][...]), jnp.sum(ssq)
     ssq_out[...] = jnp.where(lane == 0, before, jnp.where(lane == 1, now, 0.0))
 
 
-def tail_kernel(cells_all, sums, edge_a, edge_b, result_in, result, rms, sem):
+def tail_kernel(cells_all, sums, edge_a, edge_b, result_in, result, rms_hbm, rms, sem):
     ends = face_planes(result.shape[1])
     stores = [
         pltpu.make_async_copy(edge, result.at[:, end], sem.at[k])
         for k, (edge, end) in enumerate(zip((edge_a, edge_b), ends))
     ]
+    total = jnp.sum(sums[...], axis=0, keepdims=True)
     for store in stores:
         store.start()
-    total = jnp.sum(sums[...], axis=0, keepdims=True)
     rms[...] = jnp.sqrt(total / cells_all)[:, : rms.shape[1]]
+    stores.append(pltpu.make_async_copy(rms, rms_hbm, sem.at[2]))
+    stores[-1].start()
     for store in stores:
         store.wait()
 
@@ -416,98 +453,130 @@
     inner_cost = cost(3000 * cells, 4 * cells, 42 * 4 * cells)
     edge_cost = cost(100 * cells, 0, 42 * cells)
 
-    v, flow, *faces = pl.pallas_call(
-        functools.partial(pack_kernel, n_span),
-        out_shape=[field, field]
-        + [shape(NV + 1, rows, lanes)] * 2
-        + [shape(NV + 1, planes, 1, lanes)] * n_span,
+    faces = pl.pallas_call(
+        pack_kernel,
+        out_shape=[shape(NV + 1, rows, lanes)] * 2,
         in_specs=[HBM] * 2,
-        out_specs=[VMEM] * (4 + n_span),
-        scratch_shapes=[pltpu.VMEM((NV, planes, 1, lanes), F32)] * n_span + [dma((2, 3))],
+        out_specs=[VMEM] * 2,
+        scratch_shapes=[shape(2, 2, NV, rows, lanes), dma((2, 2))],
         cost_estimate=cost(cells, 0, 8 * cells),
         compiler_params=params(),
         name="pack",
     )(*hold(adjoint_start, flow_state, space=pltpu.HBM))
     streams = []
-    for pair, face in enumerate(faces[:2]):
+    for pair, face in enumerate(faces):
         streams.append(exchange_stream(face, pair))
-    spans = exchange(faces[2:], "span")
-
-    adjoint, g, src, pre, codes, jac, ssq, *rows_out = pl.pallas_call(
-        functools.partial(first_inner, n_span),
+
+    load_call = pl.pallas_call(
+        functools.partial(load_kernel, n_span),
         out_shape=[
-            field, shape(planes, rows, lanes), field,
-            shape(NV, NV, planes, rows, lanes), shape(planes, rows, LANE), shape(3 * NV * NV, SUB, LANE), tile,
+            field, shape(planes, rows, lanes), field, shape(NV, NV, planes, rows, lanes),
+            shape(planes, rows, LANE), shape(3 * NV * NV, SUB, LANE),
         ]
-        + [shape(NV, planes, 1, lanes)] * n_span,
-        in_specs=[VMEM] * 2 + [HBM] * 2 + [VMEM] * (2 + n_span),
-        out_specs=[VMEM] * (7 + n_span),
+        + [shape(NV + 1, planes, 1, lanes)] * n_span,
+        in_specs=[HBM] * 4 + [VMEM] * 2,
+        out_specs=[VMEM] * (6 + n_span),
+        scratch_shapes=[field, dma((4, planes))],
+        cost_estimate=inner_cost,
+        compiler_params=params(),
+        name="load",
+    )
+    v, g, src, pre, codes, jac, *rows_out = load_call(
+        *hold(adjoint_start, flow_state, source, precond, space=pltpu.HBM),
+        *hold(flux_jac, bc_codes),
+    )
+    spans = exchange(rows_out, "span")
+
+    part = 1 + max((planes - 2) * 2 // 3, 1)
+    first_call = pl.pallas_call(
+        functools.partial(first_inner, n_span, part),
+        out_shape=[field, field, shape(NV, NV, planes, rows, lanes), tile],
+        in_specs=[VMEM] * 4 + [HBM] * 2 + [VMEM] * (2 + n_span),
+        out_specs=[VMEM] * 4,
         scratch_shapes=[dma((2, planes))],
+        input_output_aliases={6: 1, 7: 2},
         cost_estimate=inner_cost,
         compiler_params=params(),
         name="first_inner",
-    )(
-        *hold(v, flow), *hold(source, precond, space=pltpu.HBM), *hold(flux_jac, bc_codes, *spans)
-    )
-    spans_inner = exchange(rows_out, "span")
-
-    streams_next = []
-    for pair in range(2):
-        n_out = n_span if pair == 1 else 0
-        first_edge_call = pl.pallas_call(
+    )
+    adjoint, src, pre, ssq = first_call(
+        *hold(v, g, jac, codes), *hold(source, precond, space=pltpu.HBM), *hold(src, pre, *spans)
+    )
+
+    def first_edge_call(pair, adjoint, ssq):
+        n_out = n_span if pair == ORDER[1] else 0
+        edge_call = pl.pallas_call(
             functools.partial(first_edge, pair, n_span),
             out_shape=[field, tile, shape(NV, rows, lanes)] + [shape(NV, 2, 1, lanes)] * n_out,
-            in_specs=[VMEM] * 5 + [VMEM] * (4 + n_span),
+            in_specs=[VMEM] * (9 + n_span),
             out_specs=[VMEM] * (3 + n_out),
             input_output_aliases={7: 0},
             cost_estimate=edge_cost,
             compiler_params=params(),
         )
-        adjoint, ssq, face, *rows_out = first_edge_call(
+        adjoint, ssq, face, *rows_out = edge_call(
             *hold(v, g, src, pre, jac, codes, ssq, adjoint, streams[pair], *spans)
         )
-        streams_next.append(exchange_stream(face, pair))
+        return adjoint, ssq, exchange_stream(face, pair), rows_out
+
+    streams_next = [None, None]
+    adjoint, ssq, streams_next[ORDER[0]], _ = first_edge_call(ORDER[0], adjoint, ssq)
+    rest_call = pl.pallas_call(
+        functools.partial(first_rest, n_span, part),
+        out_shape=[field, tile] + [shape(NV, planes, 1, lanes)] * n_span,
+        in_specs=[VMEM] * (8 + n_span),
+        out_specs=[VMEM] * (2 + n_span),
+        input_output_aliases={7: 0},
+        cost_estimate=inner_cost,
+        compiler_params=params(),
+        name="first_rest",
+    )
+    adjoint, ssq, *rows_out = rest_call(*hold(v, g, src, pre, jac, codes, ssq, adjoint, *spans))
+    spans_inner = exchange(rows_out, "span")
+    adjoint, ssq, streams_next[ORDER[1]], rows_out = first_edge_call(ORDER[1], adjoint, ssq)
     ssq_first = ssq
     spans_edge = exchange(rows_out, "span")
 
-    result, ssq = pl.pallas_call(
+    second_call = pl.pallas_call(
         functools.partial(second_inner, n_span),
         out_shape=[pltpu.HBM(adjoint_start.shape, F32), tile],
-        in_specs=[VMEM] * 5 + [VMEM] * (1 + 2 * n_span),
+        in_specs=[VMEM] * (6 + 2 * n_span),
         out_specs=[HBM, VMEM],
         scratch_shapes=[field, dma((planes,))],
         cost_estimate=inner_cost,
         compiler_params=params(),
         name="second_inner",
-    )(*hold(adjoint, g, src, pre, jac), *hold(codes, *spans_inner, *spans))
+    )
+    result, ssq = second_call(*hold(adjoint, g, src, pre, jac, codes, *spans_inner, *spans))
 
     face = shape(NV, rows, lanes)
-    edges = []
-    for pair in range(2):
-        edge, ssq = pl.pallas_call(
+    edges = [None, None]
+    for pair in ORDER:
+        last = pair == ORDER[1]
+        edge_call = pl.pallas_call(
             functools.partial(second_edge, pair, n_span),
-            out_shape=[face, shape(n_devices, LANE) if pair else tile],
-            in_specs=[VMEM] * (9 + 2 * n_span + pair),
+            out_shape=[face, shape(n_devices, LANE) if last else tile],
+            in_specs=[VMEM] * (9 + 2 * n_span + last),
             out_specs=[VMEM] * 2,
             cost_estimate=edge_cost,
             compiler_params=params(),
-        )(
+        )
+        edges[pair], ssq = edge_call(
             *hold(adjoint, g, src, pre, jac, codes, ssq, streams_next[pair], streams[pair]),
-            *hold(*spans_edge, *spans, *([ssq_first] * pair)),
+            *hold(*spans_edge, *spans, *([ssq_first] * last)),
         )
-        edges.append(edge)
     sums = lax.all_to_all(ssq, ("stream", "span"), 0, 0, tiled=True)
     result, rms = pl.pallas_call(
         functools.partial(tail_kernel, float(NV * cells * n_devices)),
-        out_shape=[pltpu.HBM(adjoint_start.shape, F32), jax.ShapeDtypeStruct((1, 2), F32)],
+        out_shape=[pltpu.HBM(adjoint_start.shape, F32), pltpu.HBM((1, SWEEPS), F32)],
         in_specs=[VMEM] * 3 + [HBM],
-        out_specs=[HBM, VMEM],
-        scratch_shapes=[dma((2,))],
+        out_specs=[HBM] * 2,
+        scratch_shapes=[shape(1, SWEEPS), dma((3,))],
         input_output_aliases={3: 0},
         compiler_params=params(),
         name="tail",
     )(*hold(sums, *edges), *hold(result, space=pltpu.HBM))
-    return (result, rms.reshape(2))
+    return (result, rms.reshape(SWEEPS))
 
 
 def solution(mesh):

time: 38.6 us -> 38.2 us (0.990)
  waiting for transfers between devices: 5.17 us -> 2.42 us
  Pallas kernels: 12.9 us -> 14.9 us
  starting transfers between devices: 6.73 us -> 8.22 us
  blocking collectives: 12.9 us -> 11.8 us
    ppermute x4, waiting for transfers between devices: 3.18 us -> 0.36 us  [exchange_stream(): return lax.ppermute(face, ('stream', 'span'), moves)]
    pallas_call x7 -> x9, Pallas kernels: 11.7 us -> 14.1 us  [the longest x1 3.82 us: per_device(): second_call(*hold(adjoint, g, src, pre, jac, codes, *spans_inner, *spans))]
    ppermute x4, starting transfers between devices: 5.65 us -> 7.64 us  [exchange_stream(): return lax.ppermute(face, ('stream', 'span'), moves)]
    all_to_all x1, blocking collectives: 12.9 us -> 11.8 us  [per_device(): sums = lax.all_to_all(ssq, ('stream', 'span'), 0, 0, tiled=True)]
    ppermute x3, starting transfers between devices: 1.08 us -> 0.58 us  [exchange_pair(): return lax.ppermute(face, axis, pairs(lax.axis_size(axis), pair))]
    pallas_call x1, Pallas kernels: 1.26 us -> 0.76 us  [per_device(): pl.pallas_call(functools.partial(tail_kernel, float(NV * cells * n_device...]
  transfers between devices with their start and end apart: 7 -> 7, of which waited for: 4 -> 3; matrix products, arithmetic and copies ran while one was open for 0% -> 0% of each run, Pallas kernels for 24% -> 32%
where the time goes in v3:
time: 38.2 us; the launch traced here: 38 us
  Pallas kernels  14.9 us (39%)
  blocking collectives  11.8 us (31%)
  starting transfers between devices  8.22 us (22%)
  waiting for transfers between devices  2.42 us (6%)
  between operations  0.75 us (2%)
    all_to_all x1, blocking collectives, per_device(): sums = lax.all_to_all(ssq, ('stream', 'span'), 0, 0, tiled=True)  11.8 us
    ppermute x4, starting transfers between devices, exchange_stream(): return lax.ppermute(face, ('stream', 'span'), moves)  7.64 us
    pallas_call x1, Pallas kernels, per_device(): second_call(*hold(adjoint, g, src, pre, jac, codes, *spans_inner, *spans))  3.82 us
    pallas_call x1, Pallas kernels, per_device(): first_call(*hold(v, g, jac, codes), *hold(source, precond, space=pltpu.HB...  3.16 us
    pallas_call x1, Pallas kernels, per_device(): load_call(*hold(adjoint_start, flow_state, source, precond, space=pltpu.H...  2.52 us
    ppermute x3, waiting for transfers between devices, exchange_pair(): return lax.ppermute(face, axis, pairs(lax.axis_size(axis), pair))  2.06 us
    pallas_call x1, Pallas kernels, per_device(): pl.pallas_call(pack_kernel, out_shape=[shape(NV + 1, rows, lanes)] * 2, i...  1.24 us
    pallas_call x2, Pallas kernels, per_device(): edge_call(*hold(adjoint, g, src, pre, jac, codes, ssq, streams_next[pair]...  1.19 us
  transfers between devices with their start and end apart: 7, of which 3 were waited for; matrix products, arithmetic and copies ran while one was open for 0% of the time, Pallas kernels for 32%

profile of v3, /device:TPU:0, one launch (start us, length us, event | category | flops | bytes accessed | tf_op | source)
XLA Modules:
  0.0 38.0 jit_solution(4998870243259088843)
XLA Ops:
  0.6 1.2 %pack.1 = (f32[6,16,512]{2,1,0:T(8,128)S(1)}, f32[6,16,512]{2,1,0:T(8,128)S(1)}) custom-call(f32[5,8,16,512]{3,2,1,0:T(8,128)} %v_hbm.3, f32[5,8,16,512]{3,2,1,0:T(8,128)} %flow_hbm.3), custom_call_target="tpu_custom_call" | custom-call | flops 65536 | bytes 524288 | tf_op jit(solution)/shard_map/pack/pallas_call | solution.py:456
  1.9 0.6 %collective-permute-start.1 = (f32[6,16,512]{2,1,0:T(8,128)S(1)}, f32[6,16,512]{2,1,0:T(8,128)S(1)}, u32[]{:S(2)}, u32[]{:S(2)}) collective-permute-start(f32[6,16,512]{2,1,0:T(8,128)S(1)} %get-tuple-element.44), channel_id=1, source_target_pairs={{0,1},{1,0},{2,4},{3,5},{4,2},{5,3},{6,8},{7,9},{8,6},{9,7},{10,12... | collective-permute-start | bytes 589832 | tf_op jit(solution)/shard_map/ppermute | solution.py:430
  2.5 4.0 %collective-permute-start.2 = (f32[6,16,512]{2,1,0:T(8,128)S(1)}, f32[6,16,512]{2,1,0:T(8,128)S(1)}, u32[]{:S(2)}, u32[]{:S(2)}) collective-permute-start(f32[6,16,512]{2,1,0:T(8,128)S(1)} %get-tuple-element.49), channel_id=1, source_target_pairs={{0,2},{1,3},{2,0},{3,1},{4,6},{5,7},{6,4},{7,5},{8,10},{9,11},{10,... | collective-permute-start | bytes 589832 | tf_op jit(solution)/shard_map/ppermute | solution.py:430
  6.4 2.5 %load.1 = (f32[5,8,16,512]{3,2,1,0:T(8,128)S(1)}, f32[8,16,512]{2,1,0:T(8,128)S(1)}, f32[5,8,16,512]{3,2,1,0:T(8,128)S(1)}, f32[5,5,8,16,512]{4,3,2,1,0:T(8,128)...) custom-call(f32[5,8,16,512]{3,2,1,0:T(8,128)} %v_hbm.3, ...), custom_call_target="tpu_custom_call" | custom-call | flops 196608000 | bytes 11010048 | tf_op jit(solution)/shard_map/load/pallas_call | solution.py:484
  9.0 0.1 collective-permute-start
  9.0 1.3 %collective-permute-done.refs_0_.refs_1_ = f32[6,8,1,512]{3,2,1,0:T(1,128)S(1)} collective-permute-done((f32[6,8,1,512]{3,2,1,0:T(1,128)S(1)}, f32[6,8,1,512]{3,2,1,0:T(1,128)S(1)}, u32[]{:S(2)}, u32[]{:S(2)}) %collective-permute-start) | collective-permute-done | bytes 98336 | tf_op jit(solution)/shard_map/ppermute | solution.py:416
  10.3 3.2 %first_inner.1 = (f32[5,8,16,512]{3,2,1,0:T(8,128)S(1)}, f32[5,8,16,512]{3,2,1,0:T(8,128)S(1)}, f32[5,5,8,16,512]{4,3,2,1,0:T(8,128)S(1)}, f32[8,128]{1,0:T(8,128)S(1)}) custom-call(f32[5,8,16,512]{3,2,1,0:T(8,128)S(1)} %get-tuple-element.33.v, f32[8,16,512]{2,1,0:T(8,128)S(1)} %get-tuple-element.34.g, ...), custom_call_target="tpu_custom_call", output_to_operand_aliasing={{1}: (6, {}), {2}: (7, {})} | custom-call | flops 196608000 | bytes 11010048 | tf_op jit(solution)/shard_map/first_inner/pallas_call | solution.py:502
  13.5 0.5 %shard_map.77 = (f32[5,8,16,512]{3,2,1,0:T(8,128)S(1)}, f32[8,128]{1,0:T(8,128)S(1)}, f32[5,16,512]{2,1,0:T(8,128)S(1)}) custom-call(f32[5,8,16,512]{3,2,1,0:T(8,128)S(1)} %get-tuple-element.33.v, f32[8,16,512]{2,1,0:T(8,128)S(1)} %get-tuple-element.34.g, f32[5,8,16,512]{3,2,1,0:T(8,128)S(1)} %get-tuple-element.40.src, ...), custom_call_target="tpu_custom_call", output_to_operand_aliasing={{0}: (7, {})} | custom-call | flops 6553600 | bytes 2752512 | tf_op jit(solution)/shard_map/pallas_call | solution.py:517
  14.0 0.2 collective-permute-start.4
  14.3 1.1 %first_rest.1 = (f32[5,8,16,512]{3,2,1,0:T(8,128)S(1)}, f32[8,128]{1,0:T(8,128)S(1)}, f32[5,8,1,512]{3,2,1,0:T(1,128)S(1)}) custom-call(f32[5,8,16,512]{3,2,1,0:T(8,128)S(1)} %get-tuple-element.33.v, f32[8,16,512]{2,1,0:T(8,128)S(1)} %get-tuple-element.34.g, f32[5,8,16,512]{3,2,1,0:T(8,128)S(1)} %get-tuple-element.40.src, ...), custom_call_target="tpu_custom_call", output_to_operand_aliasing={{0}: (7, {})} | custom-call | flops 196608000 | bytes 11010048 | tf_op jit(solution)/shard_map/first_rest/pallas_call | solution.py:534
  15.3 0.0 collective-permute-done.2.halo.g_halo
  15.3 0.6 %shard_map.78 = (f32[5,8,16,512]{3,2,1,0:T(8,128)S(1)}, f32[8,128]{1,0:T(8,128)S(1)}, f32[5,16,512]{2,1,0:T(8,128)S(1)}, f32[5,2,1,512]{3,2,1,0:T(1,128)S(1)}) custom-call(f32[5,8,16,512]{3,2,1,0:T(8,128)S(1)} %get-tuple-element.33.v, f32[8,16,512]{2,1,0:T(8,128)S(1)} %get-tuple-element.34.g, ...), custom_call_target="tpu_custom_call", output_to_operand_aliasing={{0}: (7, {})} | custom-call | flops 6553600 | bytes 2752512 | tf_op jit(solution)/shard_map/pallas_call | solution.py:517
  15.9 2.9 %collective-permute-start.6 = (f32[5,16,512]{2,1,0:T(8,128)S(1)}, f32[5,16,512]{2,1,0:T(8,128)S(1)}, u32[]{:S(2)}, u32[]{:S(2)}) collective-permute-start(f32[5,16,512]{2,1,0:T(8,128)S(1)} %get-tuple-element.56), channel_id=1, source_target_pairs={{0,2},{1,3},{2,0},{3,1},{4,6},{5,7},{6,4},{7,5},{8,10},{9,11},{10,... | collective-permute-start | bytes 491528 | tf_op jit(solution)/shard_map/ppermute | solution.py:430
  18.8 0.0 collective-permute-start.3
  18.8 0.5 %collective-permute-start.5 = (f32[5,2,1,512]{3,2,1,0:T(1,128)S(1)}, f32[5,2,1,512]{3,2,1,0:T(1,128)S(1)}, u32[]{:S(2)}, u32[]{:S(2)}) collective-permute-start(f32[5,2,1,512]{3,2,1,0:T(1,128)S(1)} %get-tuple-element.54), channel_id=1, source_target_pairs={{0,1},{1,0},{2,3},{3,2},{4,5},{5,4},{6,7},{7,6},{8,9},{9,8},{10,11... | collective-permute-start | bytes 61448 | tf_op jit(solution)/shard_map/ppermute | solution.py:416
  19.3 0.8 %collective-permute-done.3.refs_0_ = f32[5,8,1,512]{3,2,1,0:T(1,128)S(1)} collective-permute-done((f32[5,8,1,512]{3,2,1,0:T(1,128)S(1)}, f32[5,8,1,512]{3,2,1,0:T(1,128)S(1)}, u32[]{:S(2)}, u32[]{:S(2)}) %collective-permute-start.3) | collective-permute-done | bytes 81952 | tf_op jit(solution)/shard_map/ppermute | solution.py:416
  20.1 3.8 %second_inner.1 = (f32[5,8,16,512]{3,2,1,0:T(8,128)}, f32[8,128]{1,0:T(8,128)S(1)}) custom-call(f32[5,8,16,512]{3,2,1,0:T(8,128)S(1)} %get-tuple-element.50.v, f32[8,16,512]{2,1,0:T(8,128)S(1)} %get-tuple-element.34.g, f32[5,8,16,512]{3,2,1,0:T(8,128)S(1)} %get-tuple-element.40.src, f32[5,5,8,16,512]{4,3,2,1,0:T(8,128)S(1)} %get-tuple-element.41.pre, ...), custom_call_target="tpu_custom_call" | custom-call | flops 196608000 | bytes 11010048 | tf_op jit(solution)/shard_map/second_inner/pallas_call | solution.py:550
  23.9 0.0 collective-permute-done.5.refs_0_
  23.9 0.0 collective-permute-done.4.halo
  23.9 0.5 %shard_map.79 = (f32[5,16,512]{2,1,0:T(8,128)S(1)}, f32[8,128]{1,0:T(8,128)S(1)}) custom-call(f32[5,8,16,512]{3,2,1,0:T(8,128)S(1)} %get-tuple-element.50.v, f32[8,16,512]{2,1,0:T(8,128)S(1)} %get-tuple-element.34.g, f32[5,8,16,512]{3,2,1,0:T(8,128)S(1)} %get-tuple-element.40.src, f32[5,5,8,16,512]{4,3,2,1,0:T(8,128)S(1)} %get-tuple-element.41.pre, ...), custom_call_target="tpu_custom_call" | custom-call | flops 6553600 | bytes 2752512 | tf_op jit(solution)/shard_map/pallas_call | solution.py:564
  24.5 0.4 collective-permute-done.6.halo
  24.8 0.6 %shard_map.80 = (f32[5,16,512]{2,1,0:T(8,128)S(1)}, f32[32,128]{1,0:T(8,128)S(1)}) custom-call(f32[5,8,16,512]{3,2,1,0:T(8,128)S(1)} %get-tuple-element.50.v, f32[8,16,512]{2,1,0:T(8,128)S(1)} %get-tuple-element.34.g, f32[5,8,16,512]{3,2,1,0:T(8,128)S(1)} %get-tuple-element.40.src, f32[5,5,8,16,512]{4,3,2,1,0:T(8,128)S(1)} %get-tuple-element.41.pre, ...), custom_call_target="tpu_custom_call" | custom-call | flops 6553600 | bytes 2752512 | tf_op jit(solution)/shard_map/pallas_call | solution.py:564
  25.5 11.8 %all_to_all.11 = f32[32,1,128]{2,1,0:T(1,128)S(1)} all-to-all(f32[32,1,128]{2,1,0:T(1,128)S(1)} %bitcast.6), channel_id=1, replica_groups=mesh['stream'=16,'span'=2] {'stream','span'}, dimensions={0} | all-to-all | bytes 32768 | tf_op jit(solution)/shard_map/all_to_all | solution.py:568
  37.3 0.8 %tail.1 = (f32[5,8,16,512]{3,2,1,0:T(8,128)}, f32[1,2]{1,0:T(1,128)}) custom-call(f32[32,128]{1,0:T(8,128)S(1)} %bitcast.5, f32[5,16,512]{2,1,0:T(8,128)S(1)} %get-tuple-element.59.edge_a, f32[5,16,512]{2,1,0:T(8,128)S(1)} %get-tuple-element.60.edge_b, f32[5,8,16,512]{3,2,1,0:T(8,128)} %get-tuple-element.61.result_in), custom_call_target="tpu_custom_call", output_to_operand_aliasing={{0}: (3, {})} | custom-call | tf_op jit(solution)/shard_map/tail/pallas_call | solution.py:569
  (6 shorter events, 0.0 us)
Async XLA Ops:
  0.6 5.8 %copy-start.1 = (f32[3,5,5]{2,0,1:T(4,128)S(1)}, f32[3,5,5]{2,0,1:T(4,128)}, u32[]{:S(2)}) copy-start(f32[3,5,5]{2,0,1:T(4,128)} %param.10) | copy-start | bytes 904
  0.6 5.8 %copy-start = (s32[8,16]{1,0:T(8,128)S(1)}, s32[8,16]{1,0:T(8,128)}, u32[]{:S(2)}) copy-start(s32[8,16]{1,0:T(8,128)} %bc.1) | copy-start | bytes 1540
  1.9 11.6 %collective-permute-start.1 = (f32[6,16,512]{2,1,0:T(8,128)S(1)}, f32[6,16,512]{2,1,0:T(8,128)S(1)}, u32[]{:S(2)}, u32[]{:S(2)}) collective-permute-start(f32[6,16,512]{2,1,0:T(8,128)S(1)} %get-tuple-element.44), channel_id=1, source_target_pairs={{0,1},{1,0},{2,4},{3,5},{4,2},{5,3},{6,8},{7,9},{8,6},{9,7},{10,12... | collective-permute-start | bytes 589832 | tf_op jit(solution)/shard_map/ppermute | solution.py:430
  2.5 12.9 %collective-permute-start.2 = (f32[6,16,512]{2,1,0:T(8,128)S(1)}, f32[6,16,512]{2,1,0:T(8,128)S(1)}, u32[]{:S(2)}, u32[]{:S(2)}) collective-permute-start(f32[6,16,512]{2,1,0:T(8,128)S(1)} %get-tuple-element.49), channel_id=1, source_target_pairs={{0,2},{1,3},{2,0},{3,1},{4,6},{5,7},{6,4},{7,5},{8,10},{9,11},{10,... | collective-permute-start | bytes 589832 | tf_op jit(solution)/shard_map/ppermute | solution.py:430
  9.0 1.4 %collective-permute-start = (f32[6,8,1,512]{3,2,1,0:T(1,128)S(1)}, f32[6,8,1,512]{3,2,1,0:T(1,128)S(1)}, u32[]{:S(2)}, u32[]{:S(2)}) collective-permute-start(f32[6,8,1,512]{3,2,1,0:T(1,128)S(1)} %get-tuple-element.39), channel_id=1, source_target_pairs={{0,1},{1,0},{2,3},{3,2},{4,5},{5,4},{6,7},{7,6},{8,9},{9,8},{10,11... | collective-permute-start | bytes 294920 | tf_op jit(solution)/shard_map/ppermute | solution.py:416
  14.0 9.9 %collective-permute-start.4 = (f32[5,16,512]{2,1,0:T(8,128)S(1)}, f32[5,16,512]{2,1,0:T(8,128)S(1)}, u32[]{:S(2)}, u32[]{:S(2)}) collective-permute-start(f32[5,16,512]{2,1,0:T(8,128)S(1)} %get-tuple-element.53), channel_id=1, source_target_pairs={{0,1},{1,0},{2,4},{3,5},{4,2},{5,3},{6,8},{7,9},{8,6},{9,7},{10,12... | collective-permute-start | bytes 491528 | tf_op jit(solution)/shard_map/ppermute | solution.py:430
  15.9 8.9 %collective-permute-start.6 = (f32[5,16,512]{2,1,0:T(8,128)S(1)}, f32[5,16,512]{2,1,0:T(8,128)S(1)}, u32[]{:S(2)}, u32[]{:S(2)}) collective-permute-start(f32[5,16,512]{2,1,0:T(8,128)S(1)} %get-tuple-element.56), channel_id=1, source_target_pairs={{0,2},{1,3},{2,0},{3,1},{4,6},{5,7},{6,4},{7,5},{8,10},{9,11},{10,... | collective-permute-start | bytes 491528 | tf_op jit(solution)/shard_map/ppermute | solution.py:430
  18.8 1.3 %collective-permute-start.3 = (f32[5,8,1,512]{3,2,1,0:T(1,128)S(1)}, f32[5,8,1,512]{3,2,1,0:T(1,128)S(1)}, u32[]{:S(2)}, u32[]{:S(2)}) collective-permute-start(f32[5,8,1,512]{3,2,1,0:T(1,128)S(1)} %get-tuple-element.51), channel_id=1, source_target_pairs={{0,1},{1,0},{2,3},{3,2},{4,5},{5,4},{6,7},{7,6},{8,9},{9,8},{10,11... | collective-permute-start | bytes 245768 | tf_op jit(solution)/shard_map/ppermute | solution.py:416
  18.8 5.1 %collective-permute-start.5 = (f32[5,2,1,512]{3,2,1,0:T(1,128)S(1)}, f32[5,2,1,512]{3,2,1,0:T(1,128)S(1)}, u32[]{:S(2)}, u32[]{:S(2)}) collective-permute-start(f32[5,2,1,512]{3,2,1,0:T(1,128)S(1)} %get-tuple-element.54), channel_id=1, source_target_pairs={{0,1},{1,0},{2,3},{3,2},{4,5},{5,4},{6,7},{7,6},{8,9},{9,8},{10,11... | collective-permute-start | bytes 61448 | tf_op jit(solution)/shard_map/ppermute | solution.py:416

commit v4 on v3

--- a/solution.py
+++ b/solution.py
@@ -61,26 +61,23 @@
         out_refs[1][to] = jnp.where(is_odd, tail, head)
 
 
-def pack_kernel(v_hbm, flow_hbm, fa, fb, face_in, sem):
-    ends = face_planes(v_hbm.shape[1])
-    faces = (fa, fb)
-    fields = (flow_hbm, v_hbm)
+def fill_face(face, v, flow):
+    face[NV] = quarter_speed(*[flow(c) for c in range(NV)])
+    for c in range(NV):
+        face[c] = v(c)
+
+
+def pack_kernel(v_hbm, flow_hbm, face, flow_in, v_in, sem):
+    end = face_planes(v_hbm.shape[1])[ORDER[0]]
     loads = [
-        [
-            pltpu.make_async_copy(field.at[:, ends[pair]], face_in.at[pair, n], sem.at[pair, n])
-            for n, field in enumerate(fields)
-        ]
-        for pair in range(2)
+        pltpu.make_async_copy(field.at[:, end], target, sem.at[n])
+        for n, (field, target) in enumerate(((flow_hbm, flow_in), (v_hbm, v_in)))
     ]
-    for pair in ORDER:
-        for load in loads[pair]:
-            load.start()
-    for pair in ORDER:
-        for load in loads[pair]:
-            load.wait()
-        faces[pair][NV] = quarter_speed(*[face_in[pair, 0, c] for c in range(NV)])
-        for c in range(NV):
-            faces[pair][c] = face_in[pair, 1, c]
+    for load in loads:
+        load.start()
+    for load in loads:
+        load.wait()
+    fill_face(face, lambda c: v_in[c], lambda c: flow_in[c])
 
 
 def plane_loads(src_hbm, pre_hbm, src, pre, sem, i):
@@ -90,35 +87,34 @@
     )
 
 
-def load_kernel(n_span, v_hbm, flow_hbm, src_hbm, pre_hbm, jac_in, bc, *refs):
-    v, g, src, pre, codes, jac = refs[:6]
-    spans, (flow, sem) = refs[6 : 6 + n_span], refs[6 + n_span :]
+def load_kernel(n_span, v, flow, src_hbm, pre_hbm, jac_hbm, bc_hbm, *refs):
+    g, src, pre, codes, jac, face = refs[:6]
+    spans, (jac_in, bc, small, sem) = refs[6 : 6 + n_span], refs[6 + n_span :]
     planes = v.shape[1]
-    loads = [
-        [
-            pltpu.make_async_copy(source.at[:, i], target.at[:, i], sem.at[n, i])
-            for n, (source, target) in enumerate(((flow_hbm, flow), (v_hbm, v)))
-        ]
-        for i in range(planes)
+    tables = [
+        pltpu.make_async_copy(jac_hbm, jac_in, small.at[0]),
+        pltpu.make_async_copy(bc_hbm, bc, small.at[1]),
     ]
-    early = plane_loads(src_hbm, pre_hbm, src, pre, sem.at[pl.ds(2, 2)], 1)
-    for load in [load for pair in loads for load in pair] + [*early]:
+    early = plane_loads(src_hbm, pre_hbm, src, pre, sem, 1)
+    for load in [*tables, *early]:
         load.start()
+    end = face_planes(planes)[ORDER[1]]
+    fill_face(face, lambda c: v[c, end], lambda c: flow[c, end])
+    for i in range(planes):
+        g[i] = quarter_speed(*[flow[c, i] for c in range(NV)])
+        for c in range(NV):
+            span_rows(v, c, i, spans, i)
+    for i in range(planes):
+        span_rows(g, None, i, [span.at[NV] for span in spans], i)
+    for load in tables:
+        load.wait()
     spread_codes(bc, codes)
     for d in range(3):
         for u in range(NV):
             for c in range(NV):
                 jac[(d * NV + u) * NV + c] = jnp.broadcast_to(
-                    0.5 * jac_in[d, u : u + 1, c : c + 1], (SUB, LANE)
+                    0.5 * jac_in[u, d : d + 1, c : c + 1], (SUB, LANE)
                 )
-    for i in range(planes):
-        for load in loads[i]:
-            load.wait()
-        g[i] = quarter_speed(*[flow[c, i] for c in range(NV)])
-        for c in range(NV):
-            span_rows(v, c, i, spans, i)
-    for i in range(planes):
-        span_rows(g, None, i, [span.at[NV] for span in spans], i)
     for load in early:
         load.wait()
 
@@ -453,41 +449,48 @@
     inner_cost = cost(3000 * cells, 4 * cells, 42 * 4 * cells)
     edge_cost = cost(100 * cells, 0, 42 * cells)
 
-    faces = pl.pallas_call(
+    face = shape(NV + 1, rows, lanes)
+    first_face = pl.pallas_call(
         pack_kernel,
-        out_shape=[shape(NV + 1, rows, lanes)] * 2,
+        out_shape=face,
         in_specs=[HBM] * 2,
-        out_specs=[VMEM] * 2,
-        scratch_shapes=[shape(2, 2, NV, rows, lanes), dma((2, 2))],
+        out_specs=VMEM,
+        scratch_shapes=[shape(NV, rows, lanes)] * 2 + [dma((2,))],
         cost_estimate=cost(cells, 0, 8 * cells),
         compiler_params=params(),
         name="pack",
     )(*hold(adjoint_start, flow_state, space=pltpu.HBM))
-    streams = []
-    for pair, face in enumerate(faces):
-        streams.append(exchange_stream(face, pair))
-
+    streams = [None, None]
+
+    def send(pair, face):
+        streams[pair] = exchange_stream(face, pair)
+
+    send(ORDER[0], first_face)
+    v = adjoint_start
     load_call = pl.pallas_call(
         functools.partial(load_kernel, n_span),
         out_shape=[
-            field, shape(planes, rows, lanes), field, shape(NV, NV, planes, rows, lanes),
-            shape(planes, rows, LANE), shape(3 * NV * NV, SUB, LANE),
+            shape(planes, rows, lanes), field, shape(NV, NV, planes, rows, lanes),
+            shape(planes, rows, LANE), shape(3 * NV * NV, SUB, LANE), face,
         ]
         + [shape(NV + 1, planes, 1, lanes)] * n_span,
-        in_specs=[HBM] * 4 + [VMEM] * 2,
+        in_specs=[VMEM] * 2 + [HBM] * 4,
         out_specs=[VMEM] * (6 + n_span),
-        scratch_shapes=[field, dma((4, planes))],
+        scratch_shapes=[
+            shape(NV, 3, NV), pltpu.VMEM((planes, rows), jnp.int32), dma((2,)), dma((2, planes)),
+        ],
         cost_estimate=inner_cost,
         compiler_params=params(),
         name="load",
     )
-    v, g, src, pre, codes, jac, *rows_out = load_call(
-        *hold(adjoint_start, flow_state, source, precond, space=pltpu.HBM),
-        *hold(flux_jac, bc_codes),
-    )
+    g, src, pre, codes, jac, second_face, *rows_out = load_call(
+        *hold(v, flow_state),
+        *hold(source, precond, jnp.transpose(flux_jac, (1, 0, 2)), bc_codes, space=pltpu.HBM),
+    )
+    send(ORDER[1], second_face)
     spans = exchange(rows_out, "span")
 
-    part = 1 + max((planes - 2) * 2 // 3, 1)
+    part = 1 + max((planes - 2) * 5 // 6, 1)
     first_call = pl.pallas_call(
         functools.partial(first_inner, n_span, part),
         out_shape=[field, field, shape(NV, NV, planes, rows, lanes), tile],

time: 38.2 us -> 37.3 us (0.976)
  Pallas kernels: 14.9 us -> 13 us
  waiting for transfers between devices: 2.42 us -> 3.7 us
  starting transfers between devices: 8.22 us -> 7.71 us
    ppermute x4, waiting for transfers between devices: 0.36 us -> 1.63 us  [exchange_stream(): return lax.ppermute(face, ('stream', 'span'), moves)]
    pallas_call x2, Pallas kernels: 3.77 us -> 2.64 us  [the longest x1 1.43 us: per_device(): load_call(*hold(v, flow_state), *hold(source, precond, jnp.transpose(flux...]
    pallas_call x1, Pallas kernels: 1.06 us -> 0.5 us  [per_device(): rest_call(*hold(v, g, src, pre, jac, codes, ssq, adjoint, *spans))]
    ppermute x4, starting transfers between devices: 7.64 us -> 7.2 us  [exchange_stream(): return lax.ppermute(face, ('stream', 'span'), moves)]
  transfers between devices with their start and end apart: 7 -> 7, of which waited for: 3 -> 4; matrix products, arithmetic and copies ran while one was open for 0% -> 0% of each run, Pallas kernels for 32% -> 28%
where the time goes in v4:
time: 37.3 us; the launch traced here: 37.1 us
  Pallas kernels  13 us (35%)
  blocking collectives  11.8 us (32%)
  starting transfers between devices  7.71 us (21%)
  waiting for transfers between devices  3.7 us (10%)
  between operations  0.74 us (2%)
    all_to_all x1, blocking collectives, per_device(): sums = lax.all_to_all(ssq, ('stream', 'span'), 0, 0, tiled=True)  11.8 us
    ppermute x4, starting transfers between devices, exchange_stream(): return lax.ppermute(face, ('stream', 'span'), moves)  7.2 us
    pallas_call x1, Pallas kernels, per_device(): second_call(*hold(adjoint, g, src, pre, jac, codes, *spans_inner, *spans))  3.64 us
    pallas_call x1, Pallas kernels, per_device(): first_call(*hold(v, g, jac, codes), *hold(source, precond, space=pltpu.HB...  3.34 us
    ppermute x3, waiting for transfers between devices, exchange_pair(): return lax.ppermute(face, axis, pairs(lax.axis_size(axis), pair))  2.07 us
    ppermute x4, waiting for transfers between devices, exchange_stream(): return lax.ppermute(face, ('stream', 'span'), moves)  1.63 us
    pallas_call x1, Pallas kernels, per_device(): load_call(*hold(v, flow_state), *hold(source, precond, jnp.transpose(flux...  1.43 us
    pallas_call x1, Pallas kernels, per_device(): pl.pallas_call(pack_kernel, out_shape=face, in_specs=[HBM] * 2, out_specs...  1.21 us
  transfers between devices with their start and end apart: 7, of which 4 were waited for; matrix products, arithmetic and copies ran while one was open for 0% of the time, Pallas kernels for 28%

profile of v4, /device:TPU:0, one launch (start us, length us, event | category | flops | bytes accessed | tf_op | source)
XLA Modules:
  0.0 37.1 jit_solution(7510588041602941792)
XLA Ops:
  0.6 1.2 %pack.1 = f32[6,16,512]{2,1,0:T(8,128)S(1)} custom-call(f32[5,8,16,512]{3,2,1,0:T(8,128)} %v.9, f32[5,8,16,512]{3,2,1,0:T(8,128)} %flow_hbm.1), custom_call_target="tpu_custom_call" | custom-call | flops 65536 | bytes 524288 | tf_op jit(solution)/shard_map/pack/pallas_call | solution.py:453
  1.9 0.6 %collective-permute-start.1 = (f32[6,16,512]{2,1,0:T(8,128)S(1)}, f32[6,16,512]{2,1,0:T(8,128)S(1)}, u32[]{:S(2)}, u32[]{:S(2)}) collective-permute-start(f32[6,16,512]{2,1,0:T(8,128)S(1)} %pack.1), channel_id=1, source_target_pairs={{0,1},{1,0},{2,4},{3,5},{4,2},{5,3},{6,8},{7,9},{8,6},{9,7},{10,12... | collective-permute-start | bytes 589832 | tf_op jit(solution)/shard_map/ppermute | solution.py:426
  2.4 0.1 copy-done.1
  2.5 1.4 %load.1 = (f32[8,16,512]{2,1,0:T(8,128)S(1)}, f32[5,8,16,512]{3,2,1,0:T(8,128)S(1)}, f32[5,5,8,16,512]{4,3,2,1,0:T(8,128)S(1)}, f32[8,16,128]{2,1,0:T(8,128)S(1)...) custom-call(f32[5,8,16,512]{3,2,1,0:T(8,128)S(1)} %copy-done, ...), custom_call_target="tpu_custom_call" | custom-call | flops 196608000 | bytes 11010048 | tf_op jit(solution)/shard_map/load/pallas_call | solution.py:486
  3.9 4.0 %collective-permute-start.2 = (f32[6,16,512]{2,1,0:T(8,128)S(1)}, f32[6,16,512]{2,1,0:T(8,128)S(1)}, u32[]{:S(2)}, u32[]{:S(2)}) collective-permute-start(f32[6,16,512]{2,1,0:T(8,128)S(1)} %get-tuple-element.45), channel_id=1, source_target_pairs={{0,2},{1,3},{2,0},{3,1},{4,6},{5,7},{6,4},{7,5},{8,10},{9,11},{10,... | collective-permute-start | bytes 589832 | tf_op jit(solution)/shard_map/ppermute | solution.py:426
  7.9 0.0 collective-permute-start
  7.9 1.3 %collective-permute-done.refs_0_.refs_1_ = f32[6,8,1,512]{3,2,1,0:T(1,128)S(1)} collective-permute-done((f32[6,8,1,512]{3,2,1,0:T(1,128)S(1)}, f32[6,8,1,512]{3,2,1,0:T(1,128)S(1)}, u32[]{:S(2)}, u32[]{:S(2)}) %collective-permute-start) | collective-permute-done | bytes 98336 | tf_op jit(solution)/shard_map/ppermute | solution.py:412
  9.2 3.3 %first_inner.1 = (f32[5,8,16,512]{3,2,1,0:T(8,128)S(1)}, f32[5,8,16,512]{3,2,1,0:T(8,128)S(1)}, f32[5,5,8,16,512]{4,3,2,1,0:T(8,128)S(1)}, f32[8,128]{1,0:T(8,128)S(1)}) custom-call(f32[5,8,16,512]{3,2,1,0:T(8,128)S(1)} %copy-done, f32[8,16,512]{2,1,0:T(8,128)S(1)} %get-tuple-element.31.g, ...), custom_call_target="tpu_custom_call", output_to_operand_aliasing={{1}: (6, {}), {2}: (7, {})} | custom-call | flops 196608000 | bytes 11010048 | tf_op jit(solution)/shard_map/first_inner/pallas_call | solution.py:505
  12.6 0.5 %shard_map.77 = (f32[5,8,16,512]{3,2,1,0:T(8,128)S(1)}, f32[8,128]{1,0:T(8,128)S(1)}, f32[5,16,512]{2,1,0:T(8,128)S(1)}) custom-call(f32[5,8,16,512]{3,2,1,0:T(8,128)S(1)} %copy-done, f32[8,16,512]{2,1,0:T(8,128)S(1)} %get-tuple-element.31.g, f32[5,8,16,512]{3,2,1,0:T(8,128)S(1)} %get-tuple-element.37.src, ...), custom_call_target="tpu_custom_call", output_to_operand_aliasing={{0}: (7, {})} | custom-call | flops 6553600 | bytes 2752512 | tf_op jit(solution)/shard_map/pallas_call | solution.py:520
  13.1 0.2 collective-permute-start.4
  13.3 0.5 %first_rest.1 = (f32[5,8,16,512]{3,2,1,0:T(8,128)S(1)}, f32[8,128]{1,0:T(8,128)S(1)}, f32[5,8,1,512]{3,2,1,0:T(1,128)S(1)}) custom-call(f32[5,8,16,512]{3,2,1,0:T(8,128)S(1)} %copy-done, f32[8,16,512]{2,1,0:T(8,128)S(1)} %get-tuple-element.31.g, f32[5,8,16,512]{3,2,1,0:T(8,128)S(1)} %get-tuple-element.37.src, ...), custom_call_target="tpu_custom_call", output_to_operand_aliasing={{0}: (7, {})} | custom-call | flops 196608000 | bytes 11010048 | tf_op jit(solution)/shard_map/first_rest/pallas_call | solution.py:537
  13.8 1.4 %collective-permute-done.2.halo.g_halo = f32[6,16,512]{2,1,0:T(8,128)S(1)} collective-permute-done((f32[6,16,512]{2,1,0:T(8,128)S(1)}, f32[6,16,512]{2,1,0:T(8,128)S(1)}, u32[]{:S(2)}, u32[]{:S(2)}) %collective-permute-start.2) | collective-permute-done | bytes 196640 | tf_op jit(solution)/shard_map/ppermute | solution.py:426
  15.2 0.5 %shard_map.78 = (f32[5,8,16,512]{3,2,1,0:T(8,128)S(1)}, f32[8,128]{1,0:T(8,128)S(1)}, f32[5,16,512]{2,1,0:T(8,128)S(1)}, f32[5,2,1,512]{3,2,1,0:T(1,128)S(1)}) custom-call(f32[5,8,16,512]{3,2,1,0:T(8,128)S(1)} %copy-done, f32[8,16,512]{2,1,0:T(8,128)S(1)} %get-tuple-element.31.g, ...), custom_call_target="tpu_custom_call", output_to_operand_aliasing={{0}: (7, {})} | custom-call | flops 6553600 | bytes 2752512 | tf_op jit(solution)/shard_map/pallas_call | solution.py:520
  15.7 2.5 %collective-permute-start.6 = (f32[5,16,512]{2,1,0:T(8,128)S(1)}, f32[5,16,512]{2,1,0:T(8,128)S(1)}, u32[]{:S(2)}, u32[]{:S(2)}) collective-permute-start(f32[5,16,512]{2,1,0:T(8,128)S(1)} %get-tuple-element.52), channel_id=1, source_target_pairs={{0,2},{1,3},{2,0},{3,1},{4,6},{5,7},{6,4},{7,5},{8,10},{9,11},{10,... | collective-permute-start | bytes 491528 | tf_op jit(solution)/shard_map/ppermute | solution.py:426
  18.2 0.0 collective-permute-start.3
  18.2 0.5 %collective-permute-start.5 = (f32[5,2,1,512]{3,2,1,0:T(1,128)S(1)}, f32[5,2,1,512]{3,2,1,0:T(1,128)S(1)}, u32[]{:S(2)}, u32[]{:S(2)}) collective-permute-start(f32[5,2,1,512]{3,2,1,0:T(1,128)S(1)} %get-tuple-element.50), channel_id=1, source_target_pairs={{0,1},{1,0},{2,3},{3,2},{4,5},{5,4},{6,7},{7,6},{8,9},{9,8},{10,11... | collective-permute-start | bytes 61448 | tf_op jit(solution)/shard_map/ppermute | solution.py:412
  18.7 0.8 %collective-permute-done.3.refs_0_ = f32[5,8,1,512]{3,2,1,0:T(1,128)S(1)} collective-permute-done((f32[5,8,1,512]{3,2,1,0:T(1,128)S(1)}, f32[5,8,1,512]{3,2,1,0:T(1,128)S(1)}, u32[]{:S(2)}, u32[]{:S(2)}) %collective-permute-start.3) | collective-permute-done | bytes 81952 | tf_op jit(solution)/shard_map/ppermute | solution.py:412
  19.5 3.6 %second_inner.1 = (f32[5,8,16,512]{3,2,1,0:T(8,128)}, f32[8,128]{1,0:T(8,128)S(1)}) custom-call(f32[5,8,16,512]{3,2,1,0:T(8,128)S(1)} %get-tuple-element.46.v, f32[8,16,512]{2,1,0:T(8,128)S(1)} %get-tuple-element.31.g, f32[5,8,16,512]{3,2,1,0:T(8,128)S(1)} %get-tuple-element.37.src, f32[5,5,8,16,512]{4,3,2,1,0:T(8,128)S(1)} %get-tuple-element.38.pre, ...), custom_call_target="tpu_custom_call" | custom-call | flops 196608000 | bytes 11010048 | tf_op jit(solution)/shard_map/second_inner/pallas_call | solution.py:553
  23.1 0.0 collective-permute-done.5.refs_0_
  23.1 0.5 %shard_map.79 = (f32[5,16,512]{2,1,0:T(8,128)S(1)}, f32[8,128]{1,0:T(8,128)S(1)}) custom-call(f32[5,8,16,512]{3,2,1,0:T(8,128)S(1)} %get-tuple-element.46.v, f32[8,16,512]{2,1,0:T(8,128)S(1)} %get-tuple-element.31.g, f32[5,8,16,512]{3,2,1,0:T(8,128)S(1)} %get-tuple-element.37.src, f32[5,5,8,16,512]{4,3,2,1,0:T(8,128)S(1)} %get-tuple-element.38.pre, ...), custom_call_target="tpu_custom_call" | custom-call | flops 6553600 | bytes 2752512 | tf_op jit(solution)/shard_map/pallas_call | solution.py:567
  23.7 0.2 collective-permute-done.6.halo
  23.9 0.6 %shard_map.80 = (f32[5,16,512]{2,1,0:T(8,128)S(1)}, f32[32,128]{1,0:T(8,128)S(1)}) custom-call(f32[5,8,16,512]{3,2,1,0:T(8,128)S(1)} %get-tuple-element.46.v, f32[8,16,512]{2,1,0:T(8,128)S(1)} %get-tuple-element.31.g, f32[5,8,16,512]{3,2,1,0:T(8,128)S(1)} %get-tuple-element.37.src, f32[5,5,8,16,512]{4,3,2,1,0:T(8,128)S(1)} %get-tuple-element.38.pre, ...), custom_call_target="tpu_custom_call" | custom-call | flops 6553600 | bytes 2752512 | tf_op jit(solution)/shard_map/pallas_call | solution.py:567
  24.5 11.8 %all_to_all.11 = f32[32,1,128]{2,1,0:T(1,128)S(1)} all-to-all(f32[32,1,128]{2,1,0:T(1,128)S(1)} %bitcast.7), channel_id=1, replica_groups=mesh['stream'=16,'span'=2] {'stream','span'}, dimensions={0} | all-to-all | bytes 32768 | tf_op jit(solution)/shard_map/all_to_all | solution.py:571
  36.3 0.8 %tail.1 = (f32[5,8,16,512]{3,2,1,0:T(8,128)}, f32[1,2]{1,0:T(1,128)}) custom-call(f32[32,128]{1,0:T(8,128)S(1)} %bitcast.6, f32[5,16,512]{2,1,0:T(8,128)S(1)} %get-tuple-element.55.edge_a, f32[5,16,512]{2,1,0:T(8,128)S(1)} %get-tuple-element.56.edge_b, f32[5,8,16,512]{3,2,1,0:T(8,128)} %get-tuple-element.57.result_in), custom_call_target="tpu_custom_call", output_to_operand_aliasing={{0}: (3, {})} | custom-call | tf_op jit(solution)/shard_map/tail/pallas_call | solution.py:572
  (5 shorter events, 0.0 us)
Async XLA Ops:
  0.6 1.8 %copy-start = (f32[5,8,16,512]{3,2,1,0:T(8,128)S(1)}, f32[5,8,16,512]{3,2,1,0:T(8,128)}, u32[]{:S(2)}) copy-start(f32[5,8,16,512]{3,2,1,0:T(8,128)} %v.9) | copy-start | bytes 3932164
  0.6 1.9 %copy-start.1 = (f32[5,8,16,512]{3,2,1,0:T(8,128)S(1)}, f32[5,8,16,512]{3,2,1,0:T(8,128)}, u32[]{:S(2)}) copy-start(f32[5,8,16,512]{3,2,1,0:T(8,128)} %flow_hbm.1) | copy-start | bytes 3932164
  1.9 10.7 %collective-permute-start.1 = (f32[6,16,512]{2,1,0:T(8,128)S(1)}, f32[6,16,512]{2,1,0:T(8,128)S(1)}, u32[]{:S(2)}, u32[]{:S(2)}) collective-permute-start(f32[6,16,512]{2,1,0:T(8,128)S(1)} %pack.1), channel_id=1, source_target_pairs={{0,1},{1,0},{2,4},{3,5},{4,2},{5,3},{6,8},{7,9},{8,6},{9,7},{10,12... | collective-permute-start | bytes 589832 | tf_op jit(solution)/shard_map/ppermute | solution.py:426
  3.9 11.3 %collective-permute-start.2 = (f32[6,16,512]{2,1,0:T(8,128)S(1)}, f32[6,16,512]{2,1,0:T(8,128)S(1)}, u32[]{:S(2)}, u32[]{:S(2)}) collective-permute-start(f32[6,16,512]{2,1,0:T(8,128)S(1)} %get-tuple-element.45), channel_id=1, source_target_pairs={{0,2},{1,3},{2,0},{3,1},{4,6},{5,7},{6,4},{7,5},{8,10},{9,11},{10,... | collective-permute-start | bytes 589832 | tf_op jit(solution)/shard_map/ppermute | solution.py:426
  7.9 1.3 %collective-permute-start = (f32[6,8,1,512]{3,2,1,0:T(1,128)S(1)}, f32[6,8,1,512]{3,2,1,0:T(1,128)S(1)}, u32[]{:S(2)}, u32[]{:S(2)}) collective-permute-start(f32[6,8,1,512]{3,2,1,0:T(1,128)S(1)} %get-tuple-element.36), channel_id=1, source_target_pairs={{0,1},{1,0},{2,3},{3,2},{4,5},{5,4},{6,7},{7,6},{8,9},{9,8},{10,11... | collective-permute-start | bytes 294920 | tf_op jit(solution)/shard_map/ppermute | solution.py:412
  13.1 10.1 %collective-permute-start.4 = (f32[5,16,512]{2,1,0:T(8,128)S(1)}, f32[5,16,512]{2,1,0:T(8,128)S(1)}, u32[]{:S(2)}, u32[]{:S(2)}) collective-permute-start(f32[5,16,512]{2,1,0:T(8,128)S(1)} %get-tuple-element.49), channel_id=1, source_target_pairs={{0,1},{1,0},{2,4},{3,5},{4,2},{5,3},{6,8},{7,9},{8,6},{9,7},{10,12... | collective-permute-start | bytes 491528 | tf_op jit(solution)/shard_map/ppermute | solution.py:426
  15.7 8.1 %collective-permute-start.6 = (f32[5,16,512]{2,1,0:T(8,128)S(1)}, f32[5,16,512]{2,1,0:T(8,128)S(1)}, u32[]{:S(2)}, u32[]{:S(2)}) collective-permute-start(f32[5,16,512]{2,1,0:T(8,128)S(1)} %get-tuple-element.52), channel_id=1, source_target_pairs={{0,2},{1,3},{2,0},{3,1},{4,6},{5,7},{6,4},{7,5},{8,10},{9,11},{10,... | collective-permute-start | bytes 491528 | tf_op jit(solution)/shard_map/ppermute | solution.py:426
  18.2 1.3 %collective-permute-start.3 = (f32[5,8,1,512]{3,2,1,0:T(1,128)S(1)}, f32[5,8,1,512]{3,2,1,0:T(1,128)S(1)}, u32[]{:S(2)}, u32[]{:S(2)}) collective-permute-start(f32[5,8,1,512]{3,2,1,0:T(1,128)S(1)} %get-tuple-element.47), channel_id=1, source_target_pairs={{0,1},{1,0},{2,3},{3,2},{4,5},{5,4},{6,7},{7,6},{8,9},{9,8},{10,11... | collective-permute-start | bytes 245768 | tf_op jit(solution)/shard_map/ppermute | solution.py:412
  18.2 4.9 %collective-permute-start.5 = (f32[5,2,1,512]{3,2,1,0:T(1,128)S(1)}, f32[5,2,1,512]{3,2,1,0:T(1,128)S(1)}, u32[]{:S(2)}, u32[]{:S(2)}) collective-permute-start(f32[5,2,1,512]{3,2,1,0:T(1,128)S(1)} %get-tuple-element.50), channel_id=1, source_target_pairs={{0,1},{1,0},{2,3},{3,2},{4,5},{5,4},{6,7},{7,6},{8,9},{9,8},{10,11... | collective-permute-start | bytes 61448 | tf_op jit(solution)/shard_map/ppermute | solution.py:412

commit v5 on v4

--- a/solution.py
+++ b/solution.py
@@ -163,19 +163,26 @@
             gs, gu, gd, gl, gr = g_shift(
                 functools.partial(tops, NV), functools.partial(bottoms, NV), jb, kb
             )
-            coefs = [gs + gprev(*sl), gs + gnxt(*sl), gs + gu, gs + gd, gs + gl, gs + gr]
+            coefs = [gs + gprev(*sl), gs if gnxt is None else gs + gnxt(*sl), gs + gu, gs + gd, gs + gl, gs + gr]
             diag = ((coefs[0] + coefs[1]) + (coefs[2] + coefs[3])) + (coefs[4] + coefs[5])
             diffs, owns, res = [], [], []
             for c in range(NV):
                 own, up, down, left, right = v_shift[c](
                     functools.partial(tops, c), functools.partial(bottoms, c), jb, kb
                 )
-                before, after = prev(c, *sl), nxt(c, *sl)
-                across = before - after if sign is None else sign * (before - after)
+                before = prev(c, *sl)
+                ends = coefs[0] * before
+                across = before
+                if nxt is not None:
+                    after = nxt(c, *sl)
+                    ends = ends + coefs[1] * after
+                    across = before - after
+                if sign is not None:
+                    across = sign * across
                 diffs.append((across, up - down, left - right))
                 owns.append(own)
                 pulls = (
-                    (coefs[0] * before + coefs[1] * after)
+                    ends
                     + (coefs[2] * up + coefs[3] * down)
                 ) + (coefs[4] * left + coefs[5] * right)
                 res.append(src[(c, i, *sl)] - (diag * own - pulls))
@@ -195,6 +202,10 @@
                     if c == 3:
                         t = jnp.where(code == 0, -t, t)
                     res[c] = res[c] + jnp.where(on_wall, t, zero)
+            if nxt is None:
+                for c in range(NV):
+                    put(c, sl, res[c])
+                continue
             for c in range(NV):
                 total = total + res[c] * res[c]
             for c in range(NV):
@@ -203,6 +214,30 @@
                     a = a + pre[(u, c, i, *sl)] * res[u]
                 put(c, sl, a)
     return total
+
+
+def finish_plane(i, v, g, pre, jac, partial, halo, g_halo, sign, real, put, ssq):
+    for kb in range(v.shape[3] // LANE):
+        for jb in range(v.shape[2] // SUB):
+            sl = (pl.ds(jb * SUB, SUB), pl.ds(kb * LANE, LANE))
+            gh = real * g_halo[(NV, *sl)]
+            coef = g[(i, *sl)] + gh
+            owns = [v[(c, i, *sl)] for c in range(NV)]
+            halos = [real * halo[(c, *sl)] for c in range(NV)]
+            turned = [sign * h for h in halos]
+            res = []
+            for c in range(NV):
+                r = partial[(c, *sl)] - (gh * owns[c] - coef * halos[c])
+                for u in range(NV):
+                    r = r + jac[u * NV + c] * turned[u]
+                res.append(r)
+                ssq = ssq + r * r
+            for c in range(NV):
+                a = owns[c]
+                for u in range(NV):
+                    a = a + pre[(u, c, i, *sl)] * res[u]
+                put(c, sl, a)
+    return ssq
 
 
 def spread_codes(bc, codes):
@@ -236,16 +271,16 @@
         return get
 
     def plane(i, ssq, inside=None, halo=None, g_halo=None, sign=None, real=None):
-        if halo is None:
+        if inside is None:
             prev = lambda c, *sl: v[(c, i - 1, *sl)]
             nxt = lambda c, *sl: v[(c, i + 1, *sl)]
             gprev = lambda *sl: g[(i - 1, *sl)]
             gnxt = lambda *sl: g[(i + 1, *sl)]
         else:
             prev = lambda c, *sl: v[(c, inside, *sl)]
-            nxt = lambda c, *sl: real * halo[(c, *sl)]
+            nxt = None if halo is None else lambda c, *sl: real * halo[(c, *sl)]
             gprev = lambda *sl: g[(inside, *sl)]
-            gnxt = lambda *sl: real * g_halo[(NV, *sl)]
+            gnxt = None if halo is None else lambda *sl: real * g_halo[(NV, *sl)]
         return sweep_plane(
             i, v, prev, nxt, sign, g, gprev, gnxt, rows_of(1, i), rows_of(0, i), src, pre, jac,
             lambda jb: codes[i, pl.ds(jb * SUB, SUB), :],
@@ -303,15 +338,21 @@
 
 def first_rest(n_span, part, v, g, src, pre, jac, codes, ssq_in, out_in, *refs):
     spans = refs[:n_span]
-    out, ssq_out = refs[n_span : n_span + 2]
-    span_out = refs[n_span + 2 :]
+    out, ssq_out, partial = refs[n_span : n_span + 3]
+    span_out = refs[n_span + 3 :]
     planes = v.shape[1]
 
     def put(i, c, sl, a):
         out[(c, i, *sl)] = a
 
+    def put_partial(i, c, sl, a):
+        partial[(c, *sl)] = a
+
     plane = make_plane(v, g, src, pre, jac, codes, put, spans, spans)
     ssq_out[...] = lax.fori_loop(part, planes - 1, plane, ssq_in[...])
+    ahead = make_plane(v, g, src, pre, jac, codes, put_partial, spans, spans)
+    i, inside, sign = edge_of(ORDER[1], planes)
+    ahead(i, no_sum(), inside, sign=sign)
     for i in range(1, planes - 1):
         for c in range(NV):
             span_rows(out, c, i, span_out, i)
@@ -327,10 +368,15 @@
         out[(c, i, *sl)] = a
         face[(c, *sl)] = a
 
-    plane = make_plane(v, g, src, pre, jac, codes, put, spans, spans)
     i, inside, sign = edge_of(pair, planes)
-    ssq_out[...] = plane(i, ssq_in[...], inside, halo, halo, sign, partner_at(pair))
-    if pair == ORDER[1]:
+    if pair == ORDER[0]:
+        plane = make_plane(v, g, src, pre, jac, codes, put, spans, spans)
+        ssq_out[...] = plane(i, ssq_in[...], inside, halo, halo, sign, partner_at(pair))
+    else:
+        ssq_out[...] = finish_plane(
+            i, v, g, pre, jac, src, halo, halo, sign, partner_at(pair),
+            functools.partial(put, i), ssq_in[...],
+        )
         for k in range(2):
             at = edge_of(k, planes)[0]
             for c in range(NV):
@@ -369,19 +415,34 @@
     refs = refs[2 * n_span :]
     planes = v.shape[1]
     i, inside, sign = edge_of(pair, planes)
-    last = pair == ORDER[1]
-    out, ssq_out = refs[-2:]
-
-    def put(i, c, sl, a):
+
+    if pair == ORDER[0]:
+        out, ssq_out, partial = refs
+
+        def put(i, c, sl, a):
+            out[(c, *sl)] = a
+
+        def put_partial(i, c, sl, a):
+            partial[(c, *sl)] = a
+
+        plane = make_plane(v, g, src, pre, jac, codes, put, spans, g_spans, pair)
+        ssq_out[...] = plane(i, ssq_in[...], inside, halo, g_halo, sign, partner_at(pair))
+        other = ORDER[1]
+        ahead = make_plane(v, g, src, pre, jac, codes, put_partial, spans, g_spans, other)
+        i, inside, sign = edge_of(other, planes)
+        ahead(i, no_sum(), inside, sign=sign)
+        return
+
+    ssq_before, out, ssq_out = refs
+
+    def put_last(c, sl, a):
         out[(c, *sl)] = a
 
-    plane = make_plane(v, g, src, pre, jac, codes, put, spans, g_spans, pair)
-    ssq = plane(i, ssq_in[...], inside, halo, g_halo, sign, partner_at(pair))
-    if not last:
-        ssq_out[...] = ssq
-        return
+    ssq = finish_plane(
+        i, v, g, pre, jac, src, halo, g_halo, sign, partner_at(pair), put_last, ssq_in[...]
+    )
     lane = lax.broadcasted_iota(jnp.int32, ssq_out.shape, 1)
-    before, now = jnp.sum(refs[0][...]), jnp.sum(ssq)
+    before, now = jnp.sum(ssq_before[...]), jnp.sum(ssq)
     ssq_out[...] = jnp.where(lane == 0, before, jnp.where(lane == 1, now, 0.0))
 
 
@@ -506,7 +567,7 @@
         *hold(v, g, jac, codes), *hold(source, precond, space=pltpu.HBM), *hold(src, pre, *spans)
     )
 
-    def first_edge_call(pair, adjoint, ssq):
+    def first_edge_call(pair, src, adjoint, ssq):
         n_out = n_span if pair == ORDER[1] else 0
         edge_call = pl.pallas_call(
             functools.partial(first_edge, pair, n_span),
@@ -523,20 +584,22 @@
         return adjoint, ssq, exchange_stream(face, pair), rows_out
 
     streams_next = [None, None]
-    adjoint, ssq, streams_next[ORDER[0]], _ = first_edge_call(ORDER[0], adjoint, ssq)
+    adjoint, ssq, streams_next[ORDER[0]], _ = first_edge_call(ORDER[0], src, adjoint, ssq)
     rest_call = pl.pallas_call(
         functools.partial(first_rest, n_span, part),
-        out_shape=[field, tile] + [shape(NV, planes, 1, lanes)] * n_span,
+        out_shape=[field, tile, shape(NV, rows, lanes)] + [shape(NV, planes, 1, lanes)] * n_span,
         in_specs=[VMEM] * (8 + n_span),
-        out_specs=[VMEM] * (2 + n_span),
+        out_specs=[VMEM] * (3 + n_span),
         input_output_aliases={7: 0},
         cost_estimate=inner_cost,
         compiler_params=params(),
         name="first_rest",
     )
-    adjoint, ssq, *rows_out = rest_call(*hold(v, g, src, pre, jac, codes, ssq, adjoint, *spans))
+    adjoint, ssq, partial, *rows_out = rest_call(*hold(v, g, src, pre, jac, codes, ssq, adjoint, *spans))
     spans_inner = exchange(rows_out, "span")
-    adjoint, ssq, streams_next[ORDER[1]], rows_out = first_edge_call(ORDER[1], adjoint, ssq)
+    adjoint, ssq, streams_next[ORDER[1]], rows_out = first_edge_call(
+        ORDER[1], partial, adjoint, ssq
+    )
     ssq_first = ssq
     spans_edge = exchange(rows_out, "span")
 
@@ -558,14 +621,15 @@
         last = pair == ORDER[1]
         edge_call = pl.pallas_call(
             functools.partial(second_edge, pair, n_span),
-            out_shape=[face, shape(n_devices, LANE) if last else tile],
+            out_shape=[face, shape(n_devices, LANE)] if last else [face, tile, face],
             in_specs=[VMEM] * (9 + 2 * n_span + last),
-            out_specs=[VMEM] * 2,
+            out_specs=[VMEM] * (2 if last else 3),
             cost_estimate=edge_cost,
             compiler_params=params(),
         )
-        edges[pair], ssq = edge_call(
-            *hold(adjoint, g, src, pre, jac, codes, ssq, streams_next[pair], streams[pair]),
+        edges[pair], ssq, *partial = edge_call(
+            *hold(adjoint, g, *(partial if last else [src]), pre, jac, codes, ssq),
+            *hold(streams_next[pair], streams[pair]),
             *hold(*spans_edge, *spans, *([ssq_first] * last)),
         )
     sums = lax.all_to_all(ssq, ("stream", "span"), 0, 0, tiled=True)

time: 37.3 us -> 36.9 us (0.989)
  waiting for transfers between devices: 3.7 us -> 3.29 us
    ppermute x4, waiting for transfers between devices: 1.63 us -> 1.22 us  [exchange_stream(): return lax.ppermute(face, ('stream', 'span'), moves)]
  transfers between devices with their start and end apart: 7 -> 7, of which waited for: 4 -> 4; matrix products, arithmetic and copies ran while one was open for 0% -> 0% of each run, Pallas kernels for 28% -> 30%
where the time goes in v5:
time: 36.9 us; the launch traced here: 36.7 us
  Pallas kernels  13.1 us (36%)
  blocking collectives  11.8 us (32%)
  starting transfers between devices  7.71 us (21%)
  waiting for transfers between devices  3.29 us (9%)
  between operations  0.72 us (2%)
    all_to_all x1, blocking collectives, per_device(): sums = lax.all_to_all(ssq, ('stream', 'span'), 0, 0, tiled=True)  11.8 us
    ppermute x4, starting transfers between devices, exchange_stream(): return lax.ppermute(face, ('stream', 'span'), moves)  7.19 us
    pallas_call x1, Pallas kernels, per_device(): second_call(*hold(adjoint, g, src, pre, jac, codes, *spans_inner, *spans))  3.66 us
    pallas_call x1, Pallas kernels, per_device(): first_call(*hold(v, g, jac, codes), *hold(source, precond, space=pltpu.HB...  3.34 us
    ppermute x3, waiting for transfers between devices, exchange_pair(): return lax.ppermute(face, axis, pairs(lax.axis_size(axis), pair))  2.07 us
    pallas_call x1, Pallas kernels, per_device(): load_call(*hold(v, flow_state), *hold(source, precond, jnp.transpose(flux...  1.43 us
    ppermute x4, waiting for transfers between devices, exchange_stream(): return lax.ppermute(face, ('stream', 'span'), moves)  1.22 us
    pallas_call x1, Pallas kernels, per_device(): pl.pallas_call(pack_kernel, out_shape=face, in_specs=[HBM] * 2, out_specs...  1.21 us
  transfers between devices with their start and end apart: 7, of which 4 were waited for; matrix products, arithmetic and copies ran while one was open for 0% of the time, Pallas kernels for 30%

profile of v5, /device:TPU:0, one launch (start us, length us, event | category | flops | bytes accessed | tf_op | source)
XLA Modules:
  0.0 36.7 jit_solution(6550831014381712881)
XLA Ops:
  0.6 1.2 %pack.1 = f32[6,16,512]{2,1,0:T(8,128)S(1)} custom-call(f32[5,8,16,512]{3,2,1,0:T(8,128)} %v.9, f32[5,8,16,512]{3,2,1,0:T(8,128)} %flow_hbm.1), custom_call_target="tpu_custom_call" | custom-call | flops 65536 | bytes 524288 | tf_op jit(solution)/shard_map/pack/pallas_call | solution.py:514
  1.9 0.6 %collective-permute-start.1 = (f32[6,16,512]{2,1,0:T(8,128)S(1)}, f32[6,16,512]{2,1,0:T(8,128)S(1)}, u32[]{:S(2)}, u32[]{:S(2)}) collective-permute-start(f32[6,16,512]{2,1,0:T(8,128)S(1)} %pack.1), channel_id=1, source_target_pairs={{0,1},{1,0},{2,4},{3,5},{4,2},{5,3},{6,8},{7,9},{8,6},{9,7},{10,12... | collective-permute-start | bytes 589832 | tf_op jit(solution)/shard_map/ppermute | solution.py:487
  2.4 0.1 copy-done.1
  2.5 1.4 %load.1 = (f32[8,16,512]{2,1,0:T(8,128)S(1)}, f32[5,8,16,512]{3,2,1,0:T(8,128)S(1)}, f32[5,5,8,16,512]{4,3,2,1,0:T(8,128)S(1)}, f32[8,16,128]{2,1,0:T(8,128)S(1)...) custom-call(f32[5,8,16,512]{3,2,1,0:T(8,128)S(1)} %copy-done, ...), custom_call_target="tpu_custom_call" | custom-call | flops 196608000 | bytes 11010048 | tf_op jit(solution)/shard_map/load/pallas_call | solution.py:547
  3.9 4.0 %collective-permute-start.2 = (f32[6,16,512]{2,1,0:T(8,128)S(1)}, f32[6,16,512]{2,1,0:T(8,128)S(1)}, u32[]{:S(2)}, u32[]{:S(2)}) collective-permute-start(f32[6,16,512]{2,1,0:T(8,128)S(1)} %get-tuple-element.48), channel_id=1, source_target_pairs={{0,2},{1,3},{2,0},{3,1},{4,6},{5,7},{6,4},{7,5},{8,10},{9,11},{10,... | collective-permute-start | bytes 589832 | tf_op jit(solution)/shard_map/ppermute | solution.py:487
  7.9 0.0 collective-permute-start
  7.9 1.3 %collective-permute-done.refs_0_.refs_1_ = f32[6,8,1,512]{3,2,1,0:T(1,128)S(1)} collective-permute-done((f32[6,8,1,512]{3,2,1,0:T(1,128)S(1)}, f32[6,8,1,512]{3,2,1,0:T(1,128)S(1)}, u32[]{:S(2)}, u32[]{:S(2)}) %collective-permute-start) | collective-permute-done | bytes 98336 | tf_op jit(solution)/shard_map/ppermute | solution.py:473
  9.2 3.3 %first_inner.1 = (f32[5,8,16,512]{3,2,1,0:T(8,128)S(1)}, f32[5,8,16,512]{3,2,1,0:T(8,128)S(1)}, f32[5,5,8,16,512]{4,3,2,1,0:T(8,128)S(1)}, f32[8,128]{1,0:T(8,128)S(1)}) custom-call(f32[5,8,16,512]{3,2,1,0:T(8,128)S(1)} %copy-done, f32[8,16,512]{2,1,0:T(8,128)S(1)} %get-tuple-element.33.g, ...), custom_call_target="tpu_custom_call", output_to_operand_aliasing={{1}: (6, {}), {2}: (7, {})} | custom-call | flops 196608000 | bytes 11010048 | tf_op jit(solution)/shard_map/first_inner/pallas_call | solution.py:566
  12.6 0.0 collective-permute-done.1.halo.g_halo
  12.6 0.5 %shard_map.77 = (f32[5,8,16,512]{3,2,1,0:T(8,128)S(1)}, f32[8,128]{1,0:T(8,128)S(1)}, f32[5,16,512]{2,1,0:T(8,128)S(1)}) custom-call(f32[5,8,16,512]{3,2,1,0:T(8,128)S(1)} %copy-done, f32[8,16,512]{2,1,0:T(8,128)S(1)} %get-tuple-element.33.g, f32[5,8,16,512]{3,2,1,0:T(8,128)S(1)} %get-tuple-element.39.src, ...), custom_call_target="tpu_custom_call", output_to_operand_aliasing={{0}: (7, {})} | custom-call | flops 6553600 | bytes 2752512 | tf_op jit(solution)/shard_map/pallas_call | solution.py:581
  13.1 0.2 collective-permute-start.4
  13.3 0.9 %first_rest.1 = (f32[5,8,16,512]{3,2,1,0:T(8,128)S(1)}, f32[8,128]{1,0:T(8,128)S(1)}, f32[5,16,512]{2,1,0:T(8,128)S(1)}, f32[5,8,1,512]{3,2,1,0:T(1,128)S(1)}) custom-call(f32[5,8,16,512]{3,2,1,0:T(8,128)S(1)} %copy-done, f32[8,16,512]{2,1,0:T(8,128)S(1)} %get-tuple-element.33.g, ...), custom_call_target="tpu_custom_call", output_to_operand_aliasing={{0}: (7, {})} | custom-call | flops 196608000 | bytes 11010048 | tf_op jit(solution)/shard_map/first_rest/pallas_call | solution.py:598
  14.2 1.1 %collective-permute-done.2.halo.g_halo = f32[6,16,512]{2,1,0:T(8,128)S(1)} collective-permute-done((f32[6,16,512]{2,1,0:T(8,128)S(1)}, f32[6,16,512]{2,1,0:T(8,128)S(1)}, u32[]{:S(2)}, u32[]{:S(2)}) %collective-permute-start.2) | collective-permute-done | bytes 196640 | tf_op jit(solution)/shard_map/ppermute | solution.py:487
  15.2 0.2 shard_map.78
  15.4 2.5 %collective-permute-start.6 = (f32[5,16,512]{2,1,0:T(8,128)S(1)}, f32[5,16,512]{2,1,0:T(8,128)S(1)}, u32[]{:S(2)}, u32[]{:S(2)}) collective-permute-start(f32[5,16,512]{2,1,0:T(8,128)S(1)} %get-tuple-element.56), channel_id=1, source_target_pairs={{0,2},{1,3},{2,0},{3,1},{4,6},{5,7},{6,4},{7,5},{8,10},{9,11},{10,... | collective-permute-start | bytes 491528 | tf_op jit(solution)/shard_map/ppermute | solution.py:487
  17.9 0.5 %collective-permute-start.5 = (f32[5,2,1,512]{3,2,1,0:T(1,128)S(1)}, f32[5,2,1,512]{3,2,1,0:T(1,128)S(1)}, u32[]{:S(2)}, u32[]{:S(2)}) collective-permute-start(f32[5,2,1,512]{3,2,1,0:T(1,128)S(1)} %get-tuple-element.53), channel_id=1, source_target_pairs={{0,1},{1,0},{2,3},{3,2},{4,5},{5,4},{6,7},{7,6},{8,9},{9,8},{10,11... | collective-permute-start | bytes 61448 | tf_op jit(solution)/shard_map/ppermute | solution.py:473
  18.4 0.8 %collective-permute-done.3.refs_0_ = f32[5,8,1,512]{3,2,1,0:T(1,128)S(1)} collective-permute-done((f32[5,8,1,512]{3,2,1,0:T(1,128)S(1)}, f32[5,8,1,512]{3,2,1,0:T(1,128)S(1)}, u32[]{:S(2)}, u32[]{:S(2)}) %collective-permute-start.3) | collective-permute-done | bytes 81952 | tf_op jit(solution)/shard_map/ppermute | solution.py:473
  19.2 3.7 %second_inner.1 = (f32[5,8,16,512]{3,2,1,0:T(8,128)}, f32[8,128]{1,0:T(8,128)S(1)}) custom-call(f32[5,8,16,512]{3,2,1,0:T(8,128)S(1)} %get-tuple-element.49.v, f32[8,16,512]{2,1,0:T(8,128)S(1)} %get-tuple-element.33.g, f32[5,8,16,512]{3,2,1,0:T(8,128)S(1)} %get-tuple-element.39.src, f32[5,5,8,16,512]{4,3,2,1,0:T(8,128)S(1)} %get-tuple-element.40.pre, ...), custom_call_target="tpu_custom_call" | custom-call | flops 196608000 | bytes 11010048 | tf_op jit(solution)/shard_map/second_inner/pallas_call | solution.py:616
  22.8 0.0 collective-permute-done.4.halo
  22.9 0.9 %shard_map.79 = (f32[5,16,512]{2,1,0:T(8,128)S(1)}, f32[8,128]{1,0:T(8,128)S(1)}, f32[5,16,512]{2,1,0:T(8,128)S(1)}) custom-call(f32[5,8,16,512]{3,2,1,0:T(8,128)S(1)} %get-tuple-element.49.v, f32[8,16,512]{2,1,0:T(8,128)S(1)} %get-tuple-element.33.g, f32[5,8,16,512]{3,2,1,0:T(8,128)S(1)} %get-tuple-element.39.src, ...), custom_call_target="tpu_custom_call" | custom-call | flops 6553600 | bytes 2752512 | tf_op jit(solution)/shard_map/pallas_call | solution.py:630
  23.7 0.2 collective-permute-done.6.halo
  23.9 0.3 shard_map.80
  24.2 11.8 %all_to_all.11 = f32[32,1,128]{2,1,0:T(1,128)S(1)} all-to-all(f32[32,1,128]{2,1,0:T(1,128)S(1)} %bitcast.7), channel_id=1, replica_groups=mesh['stream'=16,'span'=2] {'stream','span'}, dimensions={0} | all-to-all | bytes 32768 | tf_op jit(solution)/shard_map/all_to_all | solution.py:635
  35.9 0.8 %tail.1 = (f32[5,8,16,512]{3,2,1,0:T(8,128)}, f32[1,2]{1,0:T(1,128)}) custom-call(f32[32,128]{1,0:T(8,128)S(1)} %bitcast.6, f32[5,16,512]{2,1,0:T(8,128)S(1)} %get-tuple-element.59.edge_a, f32[5,16,512]{2,1,0:T(8,128)S(1)} %get-tuple-element.60.edge_b, f32[5,8,16,512]{3,2,1,0:T(8,128)} %get-tuple-element.61.result_in), custom_call_target="tpu_custom_call", output_to_operand_aliasing={{0}: (3, {})} | custom-call | tf_op jit(solution)/shard_map/tail/pallas_call | solution.py:636
  (5 shorter events, 0.0 us)
Async XLA Ops:
  0.6 1.8 %copy-start = (f32[5,8,16,512]{3,2,1,0:T(8,128)S(1)}, f32[5,8,16,512]{3,2,1,0:T(8,128)}, u32[]{:S(2)}) copy-start(f32[5,8,16,512]{3,2,1,0:T(8,128)} %v.9) | copy-start | bytes 3932164
  0.6 1.9 %copy-start.1 = (f32[5,8,16,512]{3,2,1,0:T(8,128)S(1)}, f32[5,8,16,512]{3,2,1,0:T(8,128)}, u32[]{:S(2)}) copy-start(f32[5,8,16,512]{3,2,1,0:T(8,128)} %flow_hbm.1) | copy-start | bytes 3932164
  1.9 10.7 %collective-permute-start.1 = (f32[6,16,512]{2,1,0:T(8,128)S(1)}, f32[6,16,512]{2,1,0:T(8,128)S(1)}, u32[]{:S(2)}, u32[]{:S(2)}) collective-permute-start(f32[6,16,512]{2,1,0:T(8,128)S(1)} %pack.1), channel_id=1, source_target_pairs={{0,1},{1,0},{2,4},{3,5},{4,2},{5,3},{6,8},{7,9},{8,6},{9,7},{10,12... | collective-permute-start | bytes 589832 | tf_op jit(solution)/shard_map/ppermute | solution.py:487
  3.9 11.3 %collective-permute-start.2 = (f32[6,16,512]{2,1,0:T(8,128)S(1)}, f32[6,16,512]{2,1,0:T(8,128)S(1)}, u32[]{:S(2)}, u32[]{:S(2)}) collective-permute-start(f32[6,16,512]{2,1,0:T(8,128)S(1)} %get-tuple-element.48), channel_id=1, source_target_pairs={{0,2},{1,3},{2,0},{3,1},{4,6},{5,7},{6,4},{7,5},{8,10},{9,11},{10,... | collective-permute-start | bytes 589832 | tf_op jit(solution)/shard_map/ppermute | solution.py:487
  7.9 1.3 %collective-permute-start = (f32[6,8,1,512]{3,2,1,0:T(1,128)S(1)}, f32[6,8,1,512]{3,2,1,0:T(1,128)S(1)}, u32[]{:S(2)}, u32[]{:S(2)}) collective-permute-start(f32[6,8,1,512]{3,2,1,0:T(1,128)S(1)} %get-tuple-element.38), channel_id=1, source_target_pairs={{0,1},{1,0},{2,3},{3,2},{4,5},{5,4},{6,7},{7,6},{8,9},{9,8},{10,11... | collective-permute-start | bytes 294920 | tf_op jit(solution)/shard_map/ppermute | solution.py:473
  13.1 9.8 %collective-permute-start.4 = (f32[5,16,512]{2,1,0:T(8,128)S(1)}, f32[5,16,512]{2,1,0:T(8,128)S(1)}, u32[]{:S(2)}, u32[]{:S(2)}) collective-permute-start(f32[5,16,512]{2,1,0:T(8,128)S(1)} %get-tuple-element.52), channel_id=1, source_target_pairs={{0,1},{1,0},{2,4},{3,5},{4,2},{5,3},{6,8},{7,9},{8,6},{9,7},{10,12... | collective-permute-start | bytes 491528 | tf_op jit(solution)/shard_map/ppermute | solution.py:487
  15.4 8.4 %collective-permute-start.6 = (f32[5,16,512]{2,1,0:T(8,128)S(1)}, f32[5,16,512]{2,1,0:T(8,128)S(1)}, u32[]{:S(2)}, u32[]{:S(2)}) collective-permute-start(f32[5,16,512]{2,1,0:T(8,128)S(1)} %get-tuple-element.56), channel_id=1, source_target_pairs={{0,2},{1,3},{2,0},{3,1},{4,6},{5,7},{6,4},{7,5},{8,10},{9,11},{10,... | collective-permute-start | bytes 491528 | tf_op jit(solution)/shard_map/ppermute | solution.py:487
  17.9 1.3 %collective-permute-start.3 = (f32[5,8,1,512]{3,2,1,0:T(1,128)S(1)}, f32[5,8,1,512]{3,2,1,0:T(1,128)S(1)}, u32[]{:S(2)}, u32[]{:S(2)}) collective-permute-start(f32[5,8,1,512]{3,2,1,0:T(1,128)S(1)} %get-tuple-element.50), channel_id=1, source_target_pairs={{0,1},{1,0},{2,3},{3,2},{4,5},{5,4},{6,7},{7,6},{8,9},{9,8},{10,11... | collective-permute-start | bytes 245768 | tf_op jit(solution)/shard_map/ppermute | solution.py:473
  17.9 4.9 %collective-permute-start.5 = (f32[5,2,1,512]{3,2,1,0:T(1,128)S(1)}, f32[5,2,1,512]{3,2,1,0:T(1,128)S(1)}, u32[]{:S(2)}, u32[]{:S(2)}) collective-permute-start(f32[5,2,1,512]{3,2,1,0:T(1,128)S(1)} %get-tuple-element.53), channel_id=1, source_target_pairs={{0,1},{1,0},{2,3},{3,2},{4,5},{5,4},{6,7},{7,6},{8,9},{9,8},{10,11... | collective-permute-start | bytes 61448 | tf_op jit(solution)/shard_map/ppermute | solution.py:473

commit v6 on v5

--- a/solution.py
+++ b/solution.py
@@ -300,13 +300,22 @@
     )
 
 
+def ahead_of(pair, v, g, src, pre, jac, codes, partial, spans, g_spans, span_at=None):
+    def put(i, c, sl, a):
+        partial[(c, *sl)] = a
+
+    plane = make_plane(v, g, src, pre, jac, codes, put, spans, g_spans, span_at)
+    i, inside, sign = edge_of(pair, v.shape[1])
+    plane(i, no_sum(), inside, sign=sign)
+
+
 def no_sum():
     return jnp.zeros((SUB, LANE), F32)
 
 
 def first_inner(n_span, part, v, g, jac, codes, src_hbm, pre_hbm, src_in, pre_in, *refs):
     spans = refs[:n_span]
-    out, src, pre, ssq_out, sem = refs[n_span:]
+    out, src, pre, ssq_out, partial, sem = refs[n_span:]
     planes = v.shape[1]
 
     def loads(i):
@@ -334,6 +343,7 @@
     for i in late[part - 2 :]:
         for load in loads(i):
             load.wait()
+    ahead_of(ORDER[0], v, g, src, pre, jac, codes, partial, spans, spans)
 
 
 def first_rest(n_span, part, v, g, src, pre, jac, codes, ssq_in, out_in, *refs):
@@ -345,38 +355,27 @@
     def put(i, c, sl, a):
         out[(c, i, *sl)] = a
 
-    def put_partial(i, c, sl, a):
-        partial[(c, *sl)] = a
-
     plane = make_plane(v, g, src, pre, jac, codes, put, spans, spans)
     ssq_out[...] = lax.fori_loop(part, planes - 1, plane, ssq_in[...])
-    ahead = make_plane(v, g, src, pre, jac, codes, put_partial, spans, spans)
-    i, inside, sign = edge_of(ORDER[1], planes)
-    ahead(i, no_sum(), inside, sign=sign)
+    ahead_of(ORDER[1], v, g, src, pre, jac, codes, partial, spans, spans)
     for i in range(1, planes - 1):
         for c in range(NV):
             span_rows(out, c, i, span_out, i)
 
 
-def first_edge(pair, n_span, v, g, src, pre, jac, codes, ssq_in, out_in, halo, *refs):
-    spans = refs[:n_span]
-    out, ssq_out, face = refs[n_span : n_span + 3]
-    span_out = refs[n_span + 3 :]
+def first_edge(pair, v, g, partial, pre, jac, ssq_in, out_in, halo, out, ssq_out, face, *span_out):
     planes = v.shape[1]
 
     def put(i, c, sl, a):
         out[(c, i, *sl)] = a
         face[(c, *sl)] = a
 
-    i, inside, sign = edge_of(pair, planes)
-    if pair == ORDER[0]:
-        plane = make_plane(v, g, src, pre, jac, codes, put, spans, spans)
-        ssq_out[...] = plane(i, ssq_in[...], inside, halo, halo, sign, partner_at(pair))
-    else:
-        ssq_out[...] = finish_plane(
-            i, v, g, pre, jac, src, halo, halo, sign, partner_at(pair),
-            functools.partial(put, i), ssq_in[...],
-        )
+    i, _, sign = edge_of(pair, planes)
+    ssq_out[...] = finish_plane(
+        i, v, g, pre, jac, partial, halo, halo, sign, partner_at(pair),
+        functools.partial(put, i), ssq_in[...],
+    )
+    if pair == ORDER[1]:
         for k in range(2):
             at = edge_of(k, planes)[0]
             for c in range(NV):
@@ -422,15 +421,10 @@
         def put(i, c, sl, a):
             out[(c, *sl)] = a
 
-        def put_partial(i, c, sl, a):
-            partial[(c, *sl)] = a
-
         plane = make_plane(v, g, src, pre, jac, codes, put, spans, g_spans, pair)
         ssq_out[...] = plane(i, ssq_in[...], inside, halo, g_halo, sign, partner_at(pair))
         other = ORDER[1]
-        ahead = make_plane(v, g, src, pre, jac, codes, put_partial, spans, g_spans, other)
-        i, inside, sign = edge_of(other, planes)
-        ahead(i, no_sum(), inside, sign=sign)
+        ahead_of(other, v, g, src, pre, jac, codes, partial, spans, g_spans, other)
         return
 
     ssq_before, out, ssq_out = refs
@@ -452,9 +446,9 @@
         pltpu.make_async_copy(edge, result.at[:, end], sem.at[k])
         for k, (edge, end) in enumerate(zip((edge_a, edge_b), ends))
     ]
-    total = jnp.sum(sums[...], axis=0, keepdims=True)
     for store in stores:
         store.start()
+    total = jnp.sum(sums[...], axis=0, keepdims=True)
     rms[...] = jnp.sqrt(total / cells_all)[:, : rms.shape[1]]
     stores.append(pltpu.make_async_copy(rms, rms_hbm, sem.at[2]))
     stores[-1].start()
@@ -551,40 +545,44 @@
     send(ORDER[1], second_face)
     spans = exchange(rows_out, "span")
 
-    part = 1 + max((planes - 2) * 5 // 6, 1)
+    part = 1 + max((planes - 2) // 2, 1)
     first_call = pl.pallas_call(
         functools.partial(first_inner, n_span, part),
-        out_shape=[field, field, shape(NV, NV, planes, rows, lanes), tile],
+        out_shape=[
+            field, field, shape(NV, NV, planes, rows, lanes), tile, shape(NV, rows, lanes),
+        ],
         in_specs=[VMEM] * 4 + [HBM] * 2 + [VMEM] * (2 + n_span),
-        out_specs=[VMEM] * 4,
+        out_specs=[VMEM] * 5,
         scratch_shapes=[dma((2, planes))],
         input_output_aliases={6: 1, 7: 2},
         cost_estimate=inner_cost,
         compiler_params=params(),
         name="first_inner",
     )
-    adjoint, src, pre, ssq = first_call(
+    adjoint, src, pre, ssq, partial = first_call(
         *hold(v, g, jac, codes), *hold(source, precond, space=pltpu.HBM), *hold(src, pre, *spans)
     )
 
-    def first_edge_call(pair, src, adjoint, ssq):
+    def first_edge_call(pair, partial, adjoint, ssq):
         n_out = n_span if pair == ORDER[1] else 0
         edge_call = pl.pallas_call(
-            functools.partial(first_edge, pair, n_span),
+            functools.partial(first_edge, pair),
             out_shape=[field, tile, shape(NV, rows, lanes)] + [shape(NV, 2, 1, lanes)] * n_out,
-            in_specs=[VMEM] * (9 + n_span),
+            in_specs=[VMEM] * 8,
             out_specs=[VMEM] * (3 + n_out),
-            input_output_aliases={7: 0},
+            input_output_aliases={6: 0},
             cost_estimate=edge_cost,
             compiler_params=params(),
         )
         adjoint, ssq, face, *rows_out = edge_call(
-            *hold(v, g, src, pre, jac, codes, ssq, adjoint, streams[pair], *spans)
+            *hold(v, g, partial, pre, jac, ssq, adjoint, streams[pair])
         )
         return adjoint, ssq, exchange_stream(face, pair), rows_out
 
     streams_next = [None, None]
-    adjoint, ssq, streams_next[ORDER[0]], _ = first_edge_call(ORDER[0], src, adjoint, ssq)
+    adjoint, ssq, streams_next[ORDER[0]], _ = first_edge_call(
+        ORDER[0], partial, adjoint, ssq
+    )
     rest_call = pl.pallas_call(
         functools.partial(first_rest, n_span, part),
         out_shape=[field, tile, shape(NV, rows, lanes)] + [shape(NV, planes, 1, lanes)] * n_span,

time: 36.9 us -> 37 us (level)
  waiting for transfers between devices: 3.29 us -> 2.24 us
  Pallas kernels: 13.1 us -> 14 us
    ppermute x4, waiting for transfers between devices: 1.22 us -> 0.17 us  [exchange_stream(): return lax.ppermute(face, ('stream', 'span'), moves)]
    pallas_call x1, Pallas kernels: 0.86 us -> 1.86 us  [per_device(): rest_call(*hold(v, g, src, pre, jac, codes, ssq, adjoint, *spans))]
  transfers between devices with their start and end apart: 7 -> 7, of which waited for: 4 -> 3; matrix products, arithmetic and copies ran while one was open for 0% -> 0% of each run, Pallas kernels for 30% -> 32%
where the time goes in v6:
time: 37 us; the launch traced here: 36.8 us
  Pallas kernels  14 us (38%)
  blocking collectives  11.7 us (32%)
  starting transfers between devices  7.99 us (22%)
  waiting for transfers between devices  2.24 us (6%)
  between operations  0.73 us (2%)
    all_to_all x1, blocking collectives, per_device(): sums = lax.all_to_all(ssq, ('stream', 'span'), 0, 0, tiled=True)  11.7 us
    ppermute x4, starting transfers between devices, exchange_stream(): return lax.ppermute(face, ('stream', 'span'), moves)  7.48 us
    pallas_call x1, Pallas kernels, per_device(): second_call(*hold(adjoint, g, src, pre, jac, codes, *spans_inner, *spans))  3.66 us
    pallas_call x1, Pallas kernels, per_device(): first_call(*hold(v, g, jac, codes), *hold(source, precond, space=pltpu.HB...  3.53 us
    ppermute x3, waiting for transfers between devices, exchange_pair(): return lax.ppermute(face, axis, pairs(lax.axis_size(axis), pair))  2.07 us
    pallas_call x1, Pallas kernels, per_device(): rest_call(*hold(v, g, src, pre, jac, codes, ssq, adjoint, *spans))  1.86 us
    pallas_call x1, Pallas kernels, per_device(): load_call(*hold(v, flow_state), *hold(source, precond, jnp.transpose(flux...  1.43 us
    pallas_call x1, Pallas kernels, per_device(): pl.pallas_call(pack_kernel, out_shape=face, in_specs=[HBM] * 2, out_specs...  1.21 us
  transfers between devices with their start and end apart: 7, of which 3 were waited for; matrix products, arithmetic and copies ran while one was open for 0% of the time, Pallas kernels for 32%

profile of v6, /device:TPU:0, one launch (start us, length us, event | category | flops | bytes accessed | tf_op | source)
XLA Modules:
  0.0 36.8 jit_solution(12398232377501497051)
XLA Ops:
  0.6 1.2 %pack.1 = f32[6,16,512]{2,1,0:T(8,128)S(1)} custom-call(f32[5,8,16,512]{3,2,1,0:T(8,128)} %v.9, f32[5,8,16,512]{3,2,1,0:T(8,128)} %flow_hbm.1), custom_call_target="tpu_custom_call" | custom-call | flops 65536 | bytes 524288 | tf_op jit(solution)/shard_map/pack/pallas_call | solution.py:508
  1.9 0.6 %collective-permute-start.1 = (f32[6,16,512]{2,1,0:T(8,128)S(1)}, f32[6,16,512]{2,1,0:T(8,128)S(1)}, u32[]{:S(2)}, u32[]{:S(2)}) collective-permute-start(f32[6,16,512]{2,1,0:T(8,128)S(1)} %pack.1), channel_id=1, source_target_pairs={{0,1},{1,0},{2,4},{3,5},{4,2},{5,3},{6,8},{7,9},{8,6},{9,7},{10,12... | collective-permute-start | bytes 589832 | tf_op jit(solution)/shard_map/ppermute | solution.py:481
  2.4 0.1 copy-done.1
  2.5 1.4 %load.1 = (f32[8,16,512]{2,1,0:T(8,128)S(1)}, f32[5,8,16,512]{3,2,1,0:T(8,128)S(1)}, f32[5,5,8,16,512]{4,3,2,1,0:T(8,128)S(1)}, f32[8,16,128]{2,1,0:T(8,128)S(1)...) custom-call(f32[5,8,16,512]{3,2,1,0:T(8,128)S(1)} %copy-done, ...), custom_call_target="tpu_custom_call" | custom-call | flops 196608000 | bytes 11010048 | tf_op jit(solution)/shard_map/load/pallas_call | solution.py:541
  3.9 4.0 %collective-permute-start.2 = (f32[6,16,512]{2,1,0:T(8,128)S(1)}, f32[6,16,512]{2,1,0:T(8,128)S(1)}, u32[]{:S(2)}, u32[]{:S(2)}) collective-permute-start(f32[6,16,512]{2,1,0:T(8,128)S(1)} %get-tuple-element.50), channel_id=1, source_target_pairs={{0,2},{1,3},{2,0},{3,1},{4,6},{5,7},{6,4},{7,5},{8,10},{9,11},{10,... | collective-permute-start | bytes 589832 | tf_op jit(solution)/shard_map/ppermute | solution.py:481
  7.9 0.0 collective-permute-start
  7.9 1.3 %collective-permute-done.refs_0_.refs_1_ = f32[6,8,1,512]{3,2,1,0:T(1,128)S(1)} collective-permute-done((f32[6,8,1,512]{3,2,1,0:T(1,128)S(1)}, f32[6,8,1,512]{3,2,1,0:T(1,128)S(1)}, u32[]{:S(2)}, u32[]{:S(2)}) %collective-permute-start) | collective-permute-done | bytes 98336 | tf_op jit(solution)/shard_map/ppermute | solution.py:467
  9.2 3.5 %first_inner.1 = (f32[5,8,16,512]{3,2,1,0:T(8,128)S(1)}, f32[5,8,16,512]{3,2,1,0:T(8,128)S(1)}, f32[5,5,8,16,512]{4,3,2,1,0:T(8,128)S(1)}, f32[8,128]{1,0:T(8,128)S(1)}, f32[5,16,512]{2,1,0:T(8,128)S(1)}) custom-call(f32[5,8,16,512]{3,2,1,0:T(8,128)S(1)} %copy-done, ...), custom_call_target="tpu_custom_call", output_to_operand_aliasing={{1}: (6, {}), {2}: (7, {})} | custom-call | flops 196608000 | bytes 11010048 | tf_op jit(solution)/shard_map/first_inner/pallas_call | solution.py:562
  12.7 0.0 collective-permute-done.1.halo.g_halo
  12.8 0.2 shard_map.77
  13.0 0.2 collective-permute-start.4
  13.2 1.9 %first_rest.1 = (f32[5,8,16,512]{3,2,1,0:T(8,128)S(1)}, f32[8,128]{1,0:T(8,128)S(1)}, f32[5,16,512]{2,1,0:T(8,128)S(1)}, f32[5,8,1,512]{3,2,1,0:T(1,128)S(1)}) custom-call(f32[5,8,16,512]{3,2,1,0:T(8,128)S(1)} %copy-done, f32[8,16,512]{2,1,0:T(8,128)S(1)} %get-tuple-element.34.g, ...), custom_call_target="tpu_custom_call", output_to_operand_aliasing={{0}: (7, {})} | custom-call | flops 196608000 | bytes 11010048 | tf_op jit(solution)/shard_map/first_rest/pallas_call | solution.py:596
  15.1 0.2 collective-permute-done.2.halo.g_halo
  15.2 0.2 shard_map.78
  15.4 2.7 %collective-permute-start.6 = (f32[5,16,512]{2,1,0:T(8,128)S(1)}, f32[5,16,512]{2,1,0:T(8,128)S(1)}, u32[]{:S(2)}, u32[]{:S(2)}) collective-permute-start(f32[5,16,512]{2,1,0:T(8,128)S(1)} %get-tuple-element.58), channel_id=1, source_target_pairs={{0,2},{1,3},{2,0},{3,1},{4,6},{5,7},{6,4},{7,5},{8,10},{9,11},{10,... | collective-permute-start | bytes 491528 | tf_op jit(solution)/shard_map/ppermute | solution.py:481
  18.2 0.0 collective-permute-start.3
  18.2 0.5 %collective-permute-start.5 = (f32[5,2,1,512]{3,2,1,0:T(1,128)S(1)}, f32[5,2,1,512]{3,2,1,0:T(1,128)S(1)}, u32[]{:S(2)}, u32[]{:S(2)}) collective-permute-start(f32[5,2,1,512]{3,2,1,0:T(1,128)S(1)} %get-tuple-element.55), channel_id=1, source_target_pairs={{0,1},{1,0},{2,3},{3,2},{4,5},{5,4},{6,7},{7,6},{8,9},{9,8},{10,11... | collective-permute-start | bytes 61448 | tf_op jit(solution)/shard_map/ppermute | solution.py:467
  18.7 0.8 %collective-permute-done.3.refs_0_ = f32[5,8,1,512]{3,2,1,0:T(1,128)S(1)} collective-permute-done((f32[5,8,1,512]{3,2,1,0:T(1,128)S(1)}, f32[5,8,1,512]{3,2,1,0:T(1,128)S(1)}, u32[]{:S(2)}, u32[]{:S(2)}) %collective-permute-start.3) | collective-permute-done | bytes 81952 | tf_op jit(solution)/shard_map/ppermute | solution.py:467
  19.5 3.7 %second_inner.1 = (f32[5,8,16,512]{3,2,1,0:T(8,128)}, f32[8,128]{1,0:T(8,128)S(1)}) custom-call(f32[5,8,16,512]{3,2,1,0:T(8,128)S(1)} %get-tuple-element.51.v, f32[8,16,512]{2,1,0:T(8,128)S(1)} %get-tuple-element.34.g, f32[5,8,16,512]{3,2,1,0:T(8,128)S(1)} %get-tuple-element.40.src, f32[5,5,8,16,512]{4,3,2,1,0:T(8,128)S(1)} %get-tuple-element.41.pre, ...), custom_call_target="tpu_custom_call" | custom-call | flops 196608000 | bytes 11010048 | tf_op jit(solution)/shard_map/second_inner/pallas_call | solution.py:614
  23.2 0.9 %shard_map.79 = (f32[5,16,512]{2,1,0:T(8,128)S(1)}, f32[8,128]{1,0:T(8,128)S(1)}, f32[5,16,512]{2,1,0:T(8,128)S(1)}) custom-call(f32[5,8,16,512]{3,2,1,0:T(8,128)S(1)} %get-tuple-element.51.v, f32[8,16,512]{2,1,0:T(8,128)S(1)} %get-tuple-element.34.g, f32[5,8,16,512]{3,2,1,0:T(8,128)S(1)} %get-tuple-element.40.src, ...), custom_call_target="tpu_custom_call" | custom-call | flops 6553600 | bytes 2752512 | tf_op jit(solution)/shard_map/pallas_call | solution.py:628
  24.0 0.0 collective-permute-done.6.halo
  24.0 0.3 shard_map.80
  24.3 11.7 %all_to_all.11 = f32[32,1,128]{2,1,0:T(1,128)S(1)} all-to-all(f32[32,1,128]{2,1,0:T(1,128)S(1)} %bitcast.7), channel_id=1, replica_groups=mesh['stream'=16,'span'=2] {'stream','span'}, dimensions={0} | all-to-all | bytes 32768 | tf_op jit(solution)/shard_map/all_to_all | solution.py:633
  36.0 0.8 %tail.1 = (f32[5,8,16,512]{3,2,1,0:T(8,128)}, f32[1,2]{1,0:T(1,128)}) custom-call(f32[32,128]{1,0:T(8,128)S(1)} %bitcast.6, f32[5,16,512]{2,1,0:T(8,128)S(1)} %get-tuple-element.61.edge_a, f32[5,16,512]{2,1,0:T(8,128)S(1)} %get-tuple-element.62.edge_b, f32[5,8,16,512]{3,2,1,0:T(8,128)} %get-tuple-element.63.result_in), custom_call_target="tpu_custom_call", output_to_operand_aliasing={{0}: (3, {})} | custom-call | tf_op jit(solution)/shard_map/tail/pallas_call | solution.py:634
  (5 shorter events, 0.0 us)
Async XLA Ops:
  0.6 1.8 %copy-start = (f32[5,8,16,512]{3,2,1,0:T(8,128)S(1)}, f32[5,8,16,512]{3,2,1,0:T(8,128)}, u32[]{:S(2)}) copy-start(f32[5,8,16,512]{3,2,1,0:T(8,128)} %v.9) | copy-start | bytes 3932164
  0.6 1.9 %copy-start.1 = (f32[5,8,16,512]{3,2,1,0:T(8,128)S(1)}, f32[5,8,16,512]{3,2,1,0:T(8,128)}, u32[]{:S(2)}) copy-start(f32[5,8,16,512]{3,2,1,0:T(8,128)} %flow_hbm.1) | copy-start | bytes 3932164
  1.9 10.9 %collective-permute-start.1 = (f32[6,16,512]{2,1,0:T(8,128)S(1)}, f32[6,16,512]{2,1,0:T(8,128)S(1)}, u32[]{:S(2)}, u32[]{:S(2)}) collective-permute-start(f32[6,16,512]{2,1,0:T(8,128)S(1)} %pack.1), channel_id=1, source_target_pairs={{0,1},{1,0},{2,4},{3,5},{4,2},{5,3},{6,8},{7,9},{8,6},{9,7},{10,12... | collective-permute-start | bytes 589832 | tf_op jit(solution)/shard_map/ppermute | solution.py:481
  3.9 11.3 %collective-permute-start.2 = (f32[6,16,512]{2,1,0:T(8,128)S(1)}, f32[6,16,512]{2,1,0:T(8,128)S(1)}, u32[]{:S(2)}, u32[]{:S(2)}) collective-permute-start(f32[6,16,512]{2,1,0:T(8,128)S(1)} %get-tuple-element.50), channel_id=1, source_target_pairs={{0,2},{1,3},{2,0},{3,1},{4,6},{5,7},{6,4},{7,5},{8,10},{9,11},{10,... | collective-permute-start | bytes 589832 | tf_op jit(solution)/shard_map/ppermute | solution.py:481
  7.9 1.3 %collective-permute-start = (f32[6,8,1,512]{3,2,1,0:T(1,128)S(1)}, f32[6,8,1,512]{3,2,1,0:T(1,128)S(1)}, u32[]{:S(2)}, u32[]{:S(2)}) collective-permute-start(f32[6,8,1,512]{3,2,1,0:T(1,128)S(1)} %get-tuple-element.39), channel_id=1, source_target_pairs={{0,1},{1,0},{2,3},{3,2},{4,5},{5,4},{6,7},{7,6},{8,9},{9,8},{10,11... | collective-permute-start | bytes 294920 | tf_op jit(solution)/shard_map/ppermute | solution.py:467
  13.0 10.2 %collective-permute-start.4 = (f32[5,16,512]{2,1,0:T(8,128)S(1)}, f32[5,16,512]{2,1,0:T(8,128)S(1)}, u32[]{:S(2)}, u32[]{:S(2)}) collective-permute-start(f32[5,16,512]{2,1,0:T(8,128)S(1)} %get-tuple-element.54), channel_id=1, source_target_pairs={{0,1},{1,0},{2,4},{3,5},{4,2},{5,3},{6,8},{7,9},{8,6},{9,7},{10,12... | collective-permute-start | bytes 491528 | tf_op jit(solution)/shard_map/ppermute | solution.py:481
  15.4 8.6 %collective-permute-start.6 = (f32[5,16,512]{2,1,0:T(8,128)S(1)}, f32[5,16,512]{2,1,0:T(8,128)S(1)}, u32[]{:S(2)}, u32[]{:S(2)}) collective-permute-start(f32[5,16,512]{2,1,0:T(8,128)S(1)} %get-tuple-element.58), channel_id=1, source_target_pairs={{0,2},{1,3},{2,0},{3,1},{4,6},{5,7},{6,4},{7,5},{8,10},{9,11},{10,... | collective-permute-start | bytes 491528 | tf_op jit(solution)/shard_map/ppermute | solution.py:481
  18.2 1.3 %collective-permute-start.3 = (f32[5,8,1,512]{3,2,1,0:T(1,128)S(1)}, f32[5,8,1,512]{3,2,1,0:T(1,128)S(1)}, u32[]{:S(2)}, u32[]{:S(2)}) collective-permute-start(f32[5,8,1,512]{3,2,1,0:T(1,128)S(1)} %get-tuple-element.52), channel_id=1, source_target_pairs={{0,1},{1,0},{2,3},{3,2},{4,5},{5,4},{6,7},{7,6},{8,9},{9,8},{10,11... | collective-permute-start | bytes 245768 | tf_op jit(solution)/shard_map/ppermute | solution.py:467
  18.2 4.9 %collective-permute-start.5 = (f32[5,2,1,512]{3,2,1,0:T(1,128)S(1)}, f32[5,2,1,512]{3,2,1,0:T(1,128)S(1)}, u32[]{:S(2)}, u32[]{:S(2)}) collective-permute-start(f32[5,2,1,512]{3,2,1,0:T(1,128)S(1)} %get-tuple-element.55), channel_id=1, source_target_pairs={{0,1},{1,0},{2,3},{3,2},{4,5},{5,4},{6,7},{7,6},{8,9},{9,8},{10,11... | collective-permute-start | bytes 61448 | tf_op jit(solution)/shard_map/ppermute | solution.py:467
